TPU v7x, 256 devices: a whole 4x4x8 slice. The times are simulated.
256 devices in a mesh: dp: 16 (over y, x), mem: 16 (over z, core).
Axes of the slice: x: 4, y: 4, z: 8, core: 2. Of those that a mesh axis runs over, the one named last changes fastest.
Arguments:
- grad_out: bfloat16 [2048, 4096], P('dp', 'mem'), may hold values from -16 to 16
- values: bfloat16 [4096, 4096], P('dp', 'mem'), may hold values from -0.0234375 to 0.0234375
- slot_rows: int32 [2048, 32], P('dp'), may hold values from 0 to 4095, all different within a row
- weights: float32 [2048, 32], P('dp'), may hold values from 0 to 1, as said below
- sub_picks: int32 [2, 2048, 32], P(None, 'dp'), may hold values from 0 to 1023
- queries: bfloat16 [2048, 1024], P('dp'), may hold values from -6 to 6
- sub_keys: bfloat16 [2, 1024, 512], replicated, may hold values from -0.25 to 0.25
- layer_input: bfloat16 [2048, 4096], P('dp', 'mem'), may hold values from -6 to 6
Outputs:
- value_grad: float32 [4096, 4096], P('dp', 'mem')
- key_grad: float32 [2, 1024, 512], P(None, 'dp')
- proj_grad: float32 [1024, 4096], P('dp', 'mem')
Inputs may be any that keep to these rules, and one draw needn't show every extreme that they name: `slot_rows`: the 32 value rows of one token are distinct, and every value row is read by some token. Each token's 32 weights are positive and sum to one.
All inputs are finite; a program needn't handle non-finite values.
Results may differ from a plain program's by a relative error of at most 0.004.
Values may be sent and summed in bfloat16 or wider, within the bound.
No kernel may reach another device: no remote copies, remote signals or barrier semaphores. Data moves between devices by JAX's collectives and lax.ppermute only.
A program may use at most 64 MiB of HBM per device.

v0:
```python
import functools

import jax
import jax.numpy as jnp
from jax import lax
from jax.experimental import pallas as pl
from jax.experimental.pallas import tpu as pltpu
from jax.sharding import PartitionSpec as P


f32 = jnp.float32
bf16 = jnp.bfloat16
SIDE = 4
VM = pl.BlockSpec(memory_space=pltpu.VMEM)
FAR = pl.BlockSpec(memory_space=pltpu.HBM)


def run(kernel, outs, args, scratch=(), flops=0, data=0, far=(), out_spec=VM, room=16):
    return pl.pallas_call(
        kernel,
        out_shape=outs,
        in_specs=[FAR if at in far else VM for at in range(len(args))],
        out_specs=jax.tree.map(lambda _: out_spec, outs),
        scratch_shapes=list(scratch),
        cost_estimate=pl.CostEstimate(flops=flops, bytes_accessed=data, transcendentals=0),
        compiler_params=pltpu.CompilerParams(vmem_limit_bytes=room * 2**20),
    )(*args)


def shape(dims, dtype):
    return jax.ShapeDtypeStruct(dims, dtype)


def row_codes(ids):
    power = ids >> 7
    scale = (1 << (power & 15)).astype(f32) * jnp.where(power >= 16, 65536.0, 1.0)
    return ((ids & 127) + 128).astype(f32) * scale


def pack_kernel(grad_ref, rows_ref, weights_ref, out_ref, one_ref, ids_ref, wide_ref, in_sem, out_sem):
    tokens = grad_ref.shape[0]
    copies = (
        pltpu.make_async_copy(rows_ref, ids_ref, in_sem.at[0]),
        pltpu.make_async_copy(weights_ref, wide_ref, in_sem.at[1]),
        pltpu.make_async_copy(grad_ref, one_ref.at[pl.ds(0, tokens), :], in_sem.at[2]),
    )
    for copy in copies:
        copy.start()
    copies[0].wait()
    copies[1].wait()
    both = jnp.concatenate([row_codes(ids_ref[...]), wide_ref[...]], axis=1)
    one_ref[tokens:, :] = both.astype(bf16)
    copies[2].wait()
    sends = [
        pltpu.make_async_copy(one_ref, out_ref.at[at], out_sem.at[at])
        for at in range(out_ref.shape[0])
    ]
    for send in sends:
        send.start()
    for send in sends:
        send.wait()


def power_of(base, exponent, bits):
    scale = jnp.float32(1.0)
    for bit in range(bits):
        scale = scale * jnp.where((exponent >> bit) & 1 == 1, base ** (2**bit), 1.0)
    return scale


def group_rows(codes):
    row = lax.axis_index("dp") // SIDE
    moved = codes.astype(f32) * power_of(2.0**-8, row, 2)
    inside = (moved >= 128.0) & (moved < 32768.0)
    local = jnp.full(codes.shape, -128, jnp.int32)
    for step in (4, 2, 1):
        above = moved >= 128.0 * 2.0**step
        moved = jnp.where(above, moved * 2.0**-step, moved)
        local = jnp.where(above, local + 128 * step, local)
    return jnp.where(inside, local + moved.astype(jnp.int32), -1)


def slot_kernel(recv_ref, own_ref, *refs):
    values_refs, (out_ref, own_here_ref, sem) = refs[:-3], refs[-3:]
    blocks, slots, tokens = out_ref.shape
    val_rows = own_ref.shape[0]
    column = lax.axis_index("dp") % SIDE
    fetch = pltpu.make_async_copy(own_ref, own_here_ref, sem)
    fetch.start()
    rows = [group_rows(recv_ref[at, tokens:, :tokens]) for at in range(blocks)]
    accs = [[jnp.zeros((8, tokens), f32) for _ in range(slots // 8)] for _ in range(blocks)]
    for shift in range(len(values_refs), -1, -1):
        if shift == 0:
            fetch.wait()
        values_ref = values_refs[shift - 1] if shift else own_here_ref
        first = ((column + SIDE - shift) % SIDE) * (val_rows // 8)
        for at in range(blocks):
            score = lax.dot_general(
                values_ref[...],
                recv_ref[at, :tokens, :],
                (((1,), (1,)), ((), ())),
                preferred_element_type=f32,
            )
            for part in range(slots // 8):
                row = rows[at][part * 8 : part * 8 + 8]
                low, high = row & 7, (row >> 3) - first
                for tile in range(val_rows // 8):
                    got = jnp.take_along_axis(score[tile * 8 : tile * 8 + 8], low, axis=0)
                    accs[at][part] = jnp.where(high == tile, got, accs[at][part])
    for at in range(blocks):
        for part in range(slots // 8):
            out_ref[at, part * 8 : part * 8 + 8, :] = accs[at][part]


def wide_row(ref, at):
    return jnp.broadcast_to(ref[at, :][None, :], (16, ref.shape[1])).astype(bf16)


def value_kernel(shifts, recv_ref, *refs):
    out_refs, (rows_ref, wide_ref, bag_ref, grads_ref) = refs[:-4], refs[-4:]
    blocks = recv_ref.shape[0]
    val_rows = out_refs[0].shape[0]
    slots, tokens = rows_ref.shape[1:]
    tiles = val_rows // 16
    owner = lax.axis_index("dp")
    row, column = owner // SIDE, owner % SIDE
    base = row_codes(lax.broadcasted_iota(jnp.int32, (val_rows, tokens), 0))
    for at in range(blocks):
        rows_ref[at] = recv_ref[at, tokens:, :tokens].astype(f32)
        wide_ref[at] = recv_ref[at, tokens:, tokens:].astype(f32)
        grads_ref[at * tokens : at * tokens + tokens, :] = recv_ref[at, :tokens, :]
    for shift, out_ref in zip(shifts, out_refs):
        holder = row * SIDE + (column + shift) % SIDE
        codes = (base * power_of(4.0, holder, 4)).astype(bf16)
        codes = [codes[tile * 16 : tile * 16 + 16] for tile in range(tiles)]

        def one(at, carry, codes=codes):
            span = pl.ds(pl.multiple_of(at * tokens, tokens), tokens)
            bags = [jnp.zeros((16, tokens), bf16)] * tiles
            for slot in range(slots):
                code_now = wide_row(rows_ref.at[at], slot)
                weight = wide_row(wide_ref.at[at], slot)
                bags = [jnp.where(code == code_now, weight, bag) for code, bag in zip(codes, bags)]
            for tile in range(tiles):
                bag_ref[tile * 16 : tile * 16 + 16, span] = bags[tile]
            return carry

        lax.fori_loop(0, blocks, one, 0)
        total = jnp.dot(bag_ref[...], grads_ref[...], preferred_element_type=f32)
        out_ref[...] = total.astype(out_ref.dtype)


def add_kernel(*refs):
    total = refs[0][...].astype(f32)
    for ref in refs[1:-1]:
        total = total + ref[...].astype(f32)
    refs[-1][...] = total


def part_kernel(
    slot_ref,
    weights_ref,
    picks_ref,
    queries_ref,
    keys_ref,
    layer_ref,
    out_ref,
    score_ref,
    pick_code_ref,
    pick_wide_ref,
    score_wide_ref,
    sub_ref,
    mine_ref,
    sem,
):
    slots, tokens = slot_ref.shape
    halves, subs, width = keys_ref.shape
    quarter = lax.axis_index("mem") & 3
    cut = mine_ref.shape[1]
    fetch = pltpu.make_async_copy(
        queries_ref.at[:, pl.ds(pl.multiple_of(quarter * cut, cut), cut)], mine_ref, sem
    )
    fetch.start()
    weights = weights_ref[...]
    slot_grad = slot_ref[...]
    centered = slot_grad - jnp.sum(weights * slot_grad, axis=0, keepdims=True)
    score_ref[0] = weights * centered
    block = 128
    tiles = block // 16
    base = lax.broadcasted_iota(jnp.int32, (block, tokens), 0).astype(f32) + 128.0
    for half in range(halves):
        picks = picks_ref[half]
        merged = jnp.zeros((slots, tokens), f32)
        for slot in range(slots):
            same = picks == picks_ref[half, slot : slot + 1, :]
            merged = merged + jnp.where(same, score_ref[0, slot : slot + 1, :], 0.0)
        score_ref[1] = merged
        pick_code_ref[...] = row_codes(picks)
        for slot in range(slots):
            pick_wide_ref[slot] = wide_row(pick_code_ref, slot)
            score_wide_ref[slot] = wide_row(score_ref.at[1], slot)

        def one(at, carry, half=half):
            codes = (base * (1 << at).astype(f32)).astype(bf16)
            codes = [codes[tile * 16 : tile * 16 + 16] for tile in range(tiles)]
            accs = [jnp.zeros((16, tokens), bf16)] * tiles
            for slot in range(slots):
                pick, score = pick_wide_ref[slot], score_wide_ref[slot]
                accs = [jnp.where(code == pick, score, acc) for code, acc in zip(codes, accs)]
            for tile in range(tiles):
                start = pl.multiple_of(at * block + tile * 16, 16)
                sub_ref[half, pl.ds(start, 16), :] = accs[tile]
            return carry

        lax.fori_loop(0, subs // block, one, 0)
    dests = out_ref.shape[0]
    own = subs // dests
    layer = layer_ref[...]
    for half in range(halves):
        dquery = lax.dot_general(
            sub_ref[half], keys_ref[half], (((0,), (0,)), ((), ())), preferred_element_type=f32
        ).astype(bf16)
        proj = lax.dot_general(
            dquery, layer, (((0,), (0,)), ((), ())), preferred_element_type=f32
        ).astype(bf16)
        per = width // own
        for at in range(per):
            out_ref[half * per + at, :own, :] = proj[at * own : at * own + own]
    fetch.wait()
    key = jnp.dot(sub_ref[quarter >> 1], mine_ref[...], preferred_element_type=f32).astype(bf16)
    for at in range(dests):
        out_ref[at, own:, :] = key[at * own : at * own + own]


def sum_kernel(first, parts_ref, out_ref):
    rows = slice(first, first + out_ref.shape[0])
    total = parts_ref[0, rows, :].astype(f32)
    for at in range(1, parts_ref.shape[0]):
        total = total + parts_ref[at, rows, :].astype(f32)
    out_ref[...] = total.astype(out_ref.dtype)


def join_kernel(own_ref, one_ref, two_ref, three_ref, out_ref):
    quarter = lax.axis_index("mem") & 3
    cut = own_ref.shape[1]
    for at, ref in enumerate((own_ref, one_ref, two_ref, three_ref)):
        there = quarter ^ at
        out_ref[there >> 1, :, pl.ds(pl.multiple_of((there & 1) * cut, cut), cut)] = ref[...].astype(f32)


def swap(x, mask, count):
    return lax.ppermute(x, "mem", [(at, at ^ mask) for at in range(count)])


def step_body(grad_out, values, slot_rows, weights, sub_picks, queries, sub_keys, layer_input):
    groups = lax.axis_size("dp")
    mem_count = lax.axis_size("mem")
    tokens, width = grad_out.shape
    slots = slot_rows.shape[1]
    val_rows = values.shape[0]
    halves, subs, key_width = sub_keys.shape
    weights_t = weights.T
    rows_t = slot_rows.T
    picks_t = jnp.swapaxes(sub_picks, 1, 2)

    def along_x(x, shift):
        return lax.ppermute(
            x, "dp", [(at, at // SIDE * SIDE + (at + shift) % SIDE) for at in range(groups)]
        )

    columns = [[row * SIDE + column for row in range(SIDE)] for column in range(SIDE)]

    near_values = [along_x(values, shift) for shift in (1, 2, 3)]
    sent = run(
        pack_kernel,
        shape((SIDE, tokens + slots, width), bf16),
        (grad_out, rows_t, weights_t),
        scratch=(
            pltpu.VMEM((tokens + slots, width), bf16),
            pltpu.VMEM((slots, tokens), jnp.int32),
            pltpu.VMEM((slots, tokens), f32),
            pltpu.SemaphoreType.DMA((3,)),
            pltpu.SemaphoreType.DMA((SIDE,)),
        ),
        far=(0, 1, 2),
        out_spec=FAR,
        room=60,
    )
    recv = lax.all_to_all(sent, "dp", 0, 0, tiled=True, axis_index_groups=columns)
    shifts = (2, 1, 3, 0)
    away = run(
        functools.partial(value_kernel, shifts),
        [shape((val_rows, width), bf16 if shift else f32) for shift in shifts],
        (recv,),
        scratch=(
            pltpu.VMEM((SIDE, slots, tokens), f32),
            pltpu.VMEM((SIDE, slots, tokens), f32),
            pltpu.VMEM((val_rows, SIDE * tokens), bf16),
            pltpu.VMEM((SIDE * tokens, width), bf16),
        ),
        flops=4 * 10**9,
        data=2**21,
    )
    near = lax.optimization_barrier((*near_values, *away))
    near_values, (two_away, one_away, three_away, mine) = near[:3], near[3:]
    slot_parts = run(
        slot_kernel,
        shape((SIDE, slots, tokens), f32),
        (recv, values, *near_values),
        scratch=(pltpu.VMEM((val_rows, width), bf16), pltpu.SemaphoreType.DMA(())),
        flops=10**9,
        data=2**20,
        far=(1,),
    )
    slot_parts = lax.all_to_all(slot_parts, "dp", 0, 0, tiled=True, axis_index_groups=columns)
    slot_grad = jnp.sum(slot_parts, axis=0)

    one, two, three = (swap(slot_grad, mask, mem_count) for mask in (1, 2, 3))
    slot_grad = (slot_grad + one) + (two + three)
    slot_grad, two_away, one_away, three_away = lax.optimization_barrier(
        (slot_grad, two_away, one_away, three_away)
    )
    sums = [along_x(two_away, 2), along_x(one_away, 1)]
    sums.append(along_x(three_away, 3))
    step = swap(slot_grad, 4, mem_count)
    slot_grad = slot_grad + step
    step = swap(slot_grad, 12, mem_count)
    slot_grad = slot_grad + step

    own = subs // groups
    parts = run(
        part_kernel,
        shape((groups, 2 * own, width), bf16),
        (slot_grad, weights_t, picks_t, queries, sub_keys, layer_input),
        scratch=(
            pltpu.VMEM((2, slots, tokens), f32),
            pltpu.VMEM((slots, tokens), f32),
            pltpu.VMEM((slots, 16, tokens), bf16),
            pltpu.VMEM((slots, 16, tokens), bf16),
            pltpu.VMEM((halves, subs, tokens), bf16),
            pltpu.VMEM((tokens, queries.shape[1] // 4), bf16),
            pltpu.SemaphoreType.DMA(()),
        ),
        far=(3,),
    )
    parts, mine, *sums = lax.optimization_barrier((parts, mine, *sums))
    parts = lax.all_to_all(parts, "dp", 0, 0, tiled=True)
    key = run(functools.partial(sum_kernel, own), shape((own, width), bf16), (parts,))
    key, mine, *sums = lax.optimization_barrier((key, mine, *sums))
    others = [swap(key, mask, mem_count) for mask in (1, 2, 3)]
    proj_grad = run(
        functools.partial(sum_kernel, 0),
        shape((own, width), f32),
        (parts,),
        flops=10**9,
        data=2**19,
    )
    value_grad = run(
        add_kernel, shape((val_rows, width), f32), (mine, *sums), flops=10**9, data=2**19
    )
    key_grad = run(join_kernel, shape((halves, own, key_width), f32), (key, *others))
    return (value_grad, key_grad, proj_grad)


def solution(mesh):
    return jax.shard_map(
        step_body,
        mesh=mesh,
        in_specs=(
            P("dp", "mem"),
            P("dp", "mem"),
            P("dp", None),
            P("dp", None),
            P(None, "dp", None),
            P("dp", None),
            P(),
            P("dp", "mem"),
        ),
        out_specs=(P("dp", "mem"), P(None, "dp", None), P("dp", "mem")),
        check_vma=False,
    )
```

profile of v0, /device:TPU:1, one launch (start us, length us, event | category | flops | bytes accessed | tf_op | source)
XLA Modules:
  0.0 79.6 jit_solution(15682970004986868340)
XLA Ops:
  0.6 1.7 %shard_map.103 = bf16[4,160,256]{2,1,0:T(8,128)(2,1)} custom-call(bf16[128,256]{1,0:T(8,128)(2,1)} %grad_ref.1, s32[32,128]{1,0:T(8,128)} %bitcast.6, f32[32,128]{1,0:T(8,128)} %bitcast.3), custom_call_target="tpu_custom_call" | custom-call | tf_op jit(solution)/shard_map/pallas_call | solution.py:19
  2.3 5.0 %all-to-all-start = ((bf16[4,160,256]{2,1,0:T(8,128)(2,1)}), bf16[4,160,256]{2,1,0:T(8,128)(2,1)S(1)}, u32[]{:S(2)}, u32[]{:S(2)}) async-start(bf16[4,160,256]{2,1,0:T(8,128)(2,1)} %shard_map.103), calls=%async_computation | async-start | bytes 655360 | tf_op jit(solution)/shard_map/all_to_all | solution.py:289
  7.3 0.0 copy-start.5
  7.3 2.7 %collective-permute-start.1 = (bf16[256,256]{1,0:T(8,128)(2,1)}, bf16[256,256]{1,0:T(8,128)(2,1)S(1)}, u32[]{:S(2)}, u32[]{:S(2)}) collective-permute-start(bf16[256,256]{1,0:T(8,128)(2,1)} %own_ref.1), channel_id=1, source_target_pairs={{0,32},{16,48},{32,0},{48,16},{64,96},{80,112},{96,64},{112,80},{1... | collective-permute-start | bytes 393224 | tf_op jit(solution)/shard_map/ppermute | solution.py:267
  10.1 0.3 collective-permute-start
  10.4 2.4 %collective-permute-start.2 = (bf16[256,256]{1,0:T(8,128)(2,1)}, bf16[256,256]{1,0:T(8,128)(2,1)}, u32[]{:S(2)}, u32[]{:S(2)}) collective-permute-start(bf16[256,256]{1,0:T(8,128)(2,1)} %own_ref.1), channel_id=1, source_target_pairs={{0,48},{16,0},{32,16},{48,32},{64,112},{80,64},{96,80},{112,96},{1... | collective-permute-start | bytes 393224 | tf_op jit(solution)/shard_map/ppermute | solution.py:267
  12.7 0.5 all-to-all-done.recv_ref
  13.2 3.7 %shard_map.104 = (bf16[256,256]{1,0:T(8,128)(2,1)S(1)}, bf16[256,256]{1,0:T(8,128)(2,1)S(1)}, bf16[256,256]{1,0:T(8,128)(2,1)S(1)}, f32[256,256]{1,0:T(8,128)S(1)}) custom-call(bf16[4,160,256]{2,1,0:T(8,128)(2,1)S(1)} %all-to-all-done.recv_ref), custom_call_target="tpu_custom_call" | custom-call | flops 4000000000 | bytes 2097152 | tf_op jit(solution)/shard_map/pallas_call | solution.py:19
  16.9 0.0 copy-start.6
  16.9 0.7 copy-done.6
  17.6 0.0 copy-start
  17.6 0.0 copy-start.1
  17.6 0.0 copy-start.2
  17.6 0.0 copy-start.3
  17.6 0.0 copy-start.4
  17.7 0.0 collective-permute-done.1.refs_1_
  17.7 0.0 collective-permute-done.refs_0_
  17.7 0.0 collective-permute-done.2.refs_2_
  17.7 0.0 copy-done.5
  17.7 2.4 %shard_map.105 = f32[4,32,128]{2,1,0:T(8,128)S(1)} custom-call(bf16[4,160,256]{2,1,0:T(8,128)(2,1)S(1)} %all-to-all-done.recv_ref, bf16[256,256]{1,0:T(8,128)(2,1)S(1)} %copy-done.5, bf16[256,256]{1,0:T(8,128)(2,1)} %collective-permute-done.refs_0_, bf16[256,256]{1,0:T(8,128)(2,1)S(1)} %collective-permute-done.1.refs_1_, ...), custom_call_target="tpu_custom_call" | custom-call | flops 1000000000 | bytes 1048576 | tf_op jit(solution)/shard_map/pallas_call | solution.py:19
  20.1 8.4 %all_to_all.15 = f32[4,32,128]{2,1,0:T(8,128)S(1)} all-to-all(f32[4,32,128]{2,1,0:T(8,128)S(1)} %shard_map.105), channel_id=1, replica_groups={{0,64,128,192},{16,80,144,208},{32,96,160,224},{48,112,176,240},{1,65,1..., dimensions={0} | all-to-all | bytes 131072 | tf_op jit(solution)/shard_map/all_to_all | solution.py:315
  28.5 4.8 %collective-permute-start.5 = (f32[32,128]{1,0:T(8,128)S(1)}, f32[32,128]{1,0:T(8,128)S(1)}, u32[]{:S(2)}, u32[]{:S(2)}) collective-permute-start(f32[32,128]{1,0:T(8,128)S(1)} %reduce_sum.9), channel_id=1, source_target_pairs={{0,3},{1,2},{2,1},{3,0},{4,7},{5,6},{6,5},{7,4},{8,11},{9,10},{10,... | collective-permute-start | bytes 49160 | tf_op jit(solution)/shard_map/ppermute | solution.py:252
  33.3 0.0 collective-permute-start.4
  33.3 0.5 collective-permute-start.3
  33.8 0.9 %collective-permute-done.5 = f32[32,128]{1,0:T(8,128)S(1)} collective-permute-done((f32[32,128]{1,0:T(8,128)S(1)}, f32[32,128]{1,0:T(8,128)S(1)}, u32[]{:S(2)}, u32[]{:S(2)}) %collective-permute-start.5) | collective-permute-done | bytes 16416 | tf_op jit(solution)/shard_map/ppermute | solution.py:252
  34.7 1.2 %collective-permute-done.4 = f32[32,128]{1,0:T(8,128)S(1)} collective-permute-done((f32[32,128]{1,0:T(8,128)S(1)}, f32[32,128]{1,0:T(8,128)S(1)}, u32[]{:S(2)}, u32[]{:S(2)}) %collective-permute-start.4) | collective-permute-done | bytes 16416 | tf_op jit(solution)/shard_map/ppermute | solution.py:252
  35.9 0.0 collective-permute-done.3
  35.9 1.7 %collective-permute-start.8 = (bf16[256,256]{1,0:T(8,128)(2,1)S(1)}, bf16[256,256]{1,0:T(8,128)(2,1)S(1)}, u32[]{:S(2)}, u32[]{:S(2)}) collective-permute-start(bf16[256,256]{1,0:T(8,128)(2,1)S(1)} %get-tuple-element.40), channel_id=1, source_target_pairs={{0,32},{16,48},{32,0},{48,16},{64,96},{80,112},{96,64},{112,80},{1... | collective-permute-start | bytes 393224 | tf_op jit(solution)/shard_map/ppermute | solution.py:267
  37.6 0.6 collective-permute-start.9
  38.2 2.1 %collective-permute-start.10 = (bf16[256,256]{1,0:T(8,128)(2,1)S(1)}, bf16[256,256]{1,0:T(8,128)(2,1)S(1)}, u32[]{:S(2)}, u32[]{:S(2)}) collective-permute-start(bf16[256,256]{1,0:T(8,128)(2,1)S(1)} %get-tuple-element.42), channel_id=1, source_target_pairs={{0,48},{16,0},{32,16},{48,32},{64,112},{80,64},{96,80},{112,96},{1... | collective-permute-start | bytes 393224 | tf_op jit(solution)/shard_map/ppermute | solution.py:267
  40.3 3.0 %collective-permute-start.6 = (f32[32,128]{1,0:T(8,128)S(1)}, f32[32,128]{1,0:T(8,128)S(1)}, u32[]{:S(2)}, u32[]{:S(2)}) collective-permute-start(f32[32,128]{1,0:T(8,128)S(1)} %add_add_fusion), channel_id=1, source_target_pairs={{0,4},{1,5},{2,6},{3,7},{4,0},{5,1},{6,2},{7,3},{8,12},{9,13},{10,... | collective-permute-start | bytes 49160 | tf_op jit(solution)/shard_map/ppermute | solution.py:252
  43.3 1.6 %collective-permute-done.6 = f32[32,128]{1,0:T(8,128)S(1)} collective-permute-done((f32[32,128]{1,0:T(8,128)S(1)}, f32[32,128]{1,0:T(8,128)S(1)}, u32[]{:S(2)}, u32[]{:S(2)}) %collective-permute-start.6) | collective-permute-done | bytes 16416 | tf_op jit(solution)/shard_map/ppermute | solution.py:252
  44.9 4.7 %collective-permute-start.7 = (f32[32,128]{1,0:T(8,128)S(1)}, f32[32,128]{1,0:T(8,128)S(1)}, u32[]{:S(2)}, u32[]{:S(2)}) collective-permute-start(f32[32,128]{1,0:T(8,128)S(1)} %add.18), channel_id=1, source_target_pairs={{0,12},{1,13},{2,14},{3,15},{4,8},{5,9},{6,10},{7,11},{8,4},{9,5},... | collective-permute-start | bytes 49160 | tf_op jit(solution)/shard_map/ppermute | solution.py:252
  49.6 1.1 %collective-permute-done.7 = f32[32,128]{1,0:T(8,128)S(1)} collective-permute-done((f32[32,128]{1,0:T(8,128)S(1)}, f32[32,128]{1,0:T(8,128)S(1)}, u32[]{:S(2)}, u32[]{:S(2)}) %collective-permute-start.7) | collective-permute-done | bytes 16416 | tf_op jit(solution)/shard_map/ppermute | solution.py:252
  50.7 0.0 copy-done
  50.7 0.0 copy-done.1
  50.7 0.0 copy-done.2
  50.7 0.0 copy-done.3
  50.7 0.0 copy-done.4
  50.7 3.0 %shard_map.106 = bf16[16,128,256]{2,1,0:T(8,128)(2,1)S(1)} custom-call(f32[32,128]{1,0:T(8,128)S(1)} %add.19.slot_ref, f32[32,128]{1,0:T(8,128)S(1)} %bitcast.4, s32[2,32,128]{2,1,0:T(8,128)S(1)} %bitcast.5, bf16[128,1024]{1,0:T(8,128)(2,1)S(1)} %copy-done.1, bf16[2,1024,512]{2,1,0:T(8,128)(2,1)S(1)} %copy-done, bf16[128,256]{1,0:T(8,128)(2,1)S(1)} %copy-done.2), custom_call_target="tpu_custom_call" | custom-call | tf_op jit(solution)/shard_map/pallas_call | solution.py:19
  53.8 0.0 copy-start.7
  53.8 0.0 collective-permute-done.8.refs_1_
  53.8 0.0 collective-permute-done.9.refs_2_
  53.8 0.0 collective-permute-done.10.refs_3_
  53.8 16.8 %all_to_all.16.parts_ref = bf16[16,128,256]{2,1,0:T(8,128)(2,1)S(1)} all-to-all(bf16[16,128,256]{2,1,0:T(8,128)(2,1)S(1)} %shard_map.106), channel_id=1, replica_groups=mesh['dp'=16,'mem'=16] {'dp'}, dimensions={0} | all-to-all | bytes 2097152 | tf_op jit(solution)/shard_map/all_to_all | solution.py:347
  70.6 0.1 shard_map.107.own_ref
  70.7 4.8 %collective-permute-start.13 = (bf16[64,256]{1,0:T(8,128)(2,1)S(1)}, bf16[64,256]{1,0:T(8,128)(2,1)S(1)}, u32[]{:S(2)}, u32[]{:S(2)}) collective-permute-start(bf16[64,256]{1,0:T(8,128)(2,1)S(1)} %shard_map.107.own_ref), channel_id=1, source_target_pairs={{0,3},{1,2},{2,1},{3,0},{4,7},{5,6},{6,5},{7,4},{8,11},{9,10},{10,... | collective-permute-start | bytes 98312 | tf_op jit(solution)/shard_map/ppermute | solution.py:252
  75.6 0.7 collective-permute-start.12
  76.3 0.0 collective-permute-start.11
  76.3 0.0 copy-done.7
  76.3 0.8 shard_map.108
  77.0 0.7 shard_map.110
  77.7 0.0 collective-permute-done.13.three_ref
  77.7 1.1 %collective-permute-done.12.two_ref = bf16[64,256]{1,0:T(8,128)(2,1)S(1)} collective-permute-done((bf16[64,256]{1,0:T(8,128)(2,1)S(1)}, bf16[64,256]{1,0:T(8,128)(2,1)S(1)}, u32[]{:S(2)}, u32[]{:S(2)}) %collective-permute-start.12) | collective-permute-done | bytes 32800 | tf_op jit(solution)/shard_map/ppermute | solution.py:252
  78.8 0.0 collective-permute-done.11.one_ref
  78.8 0.7 shard_map.109
  (4 shorter events, 0.0 us)
Async XLA Ops:
  2.3 10.9 %all-to-all-start = ((bf16[4,160,256]{2,1,0:T(8,128)(2,1)}), bf16[4,160,256]{2,1,0:T(8,128)(2,1)S(1)}, u32[]{:S(2)}, u32[]{:S(2)}) async-start(bf16[4,160,256]{2,1,0:T(8,128)(2,1)} %shard_map.103), calls=%async_computation | async-start | bytes 655360 | tf_op jit(solution)/shard_map/all_to_all | solution.py:289
  7.3 10.4 %copy-start.5 = (bf16[256,256]{1,0:T(8,128)(2,1)S(1)}, bf16[256,256]{1,0:T(8,128)(2,1)}, u32[]{:S(2)}) copy-start(bf16[256,256]{1,0:T(8,128)(2,1)} %own_ref.1) | copy-start | bytes 393220
  7.3 10.3 %collective-permute-start.1 = (bf16[256,256]{1,0:T(8,128)(2,1)}, bf16[256,256]{1,0:T(8,128)(2,1)S(1)}, u32[]{:S(2)}, u32[]{:S(2)}) collective-permute-start(bf16[256,256]{1,0:T(8,128)(2,1)} %own_ref.1), channel_id=1, source_target_pairs={{0,32},{16,48},{32,0},{48,16},{64,96},{80,112},{96,64},{112,80},{1... | collective-permute-start | bytes 393224 | tf_op jit(solution)/shard_map/ppermute | solution.py:267
  10.1 7.6 %collective-permute-start = (bf16[256,256]{1,0:T(8,128)(2,1)}, bf16[256,256]{1,0:T(8,128)(2,1)}, u32[]{:S(2)}, u32[]{:S(2)}) collective-permute-start(bf16[256,256]{1,0:T(8,128)(2,1)} %own_ref.1), channel_id=1, source_target_pairs={{0,16},{16,32},{32,48},{48,0},{64,80},{80,96},{96,112},{112,64},{1... | collective-permute-start | bytes 393224 | tf_op jit(solution)/shard_map/ppermute | solution.py:267
  10.4 7.3 %collective-permute-start.2 = (bf16[256,256]{1,0:T(8,128)(2,1)}, bf16[256,256]{1,0:T(8,128)(2,1)}, u32[]{:S(2)}, u32[]{:S(2)}) collective-permute-start(bf16[256,256]{1,0:T(8,128)(2,1)} %own_ref.1), channel_id=1, source_target_pairs={{0,48},{16,0},{32,16},{48,32},{64,112},{80,64},{96,80},{112,96},{1... | collective-permute-start | bytes 393224 | tf_op jit(solution)/shard_map/ppermute | solution.py:267
  16.9 0.7 copy-start.6
  17.6 33.1 %copy-start = (bf16[2,1024,512]{2,1,0:T(8,128)(2,1)S(1)}, bf16[2,1024,512]{2,1,0:T(8,128)(2,1)}, u32[]{:S(2)}) copy-start(bf16[2,1024,512]{2,1,0:T(8,128)(2,1)} %keys_ref.1) | copy-start | bytes 6291460
  17.6 33.1 %copy-start.1 = (bf16[128,1024]{1,0:T(8,128)(2,1)S(1)}, bf16[128,1024]{1,0:T(8,128)(2,1)}, u32[]{:S(2)}) copy-start(bf16[128,1024]{1,0:T(8,128)(2,1)} %queries_ref.1) | copy-start | bytes 786436
  17.6 33.1 %copy-start.2 = (bf16[128,256]{1,0:T(8,128)(2,1)S(1)}, bf16[128,256]{1,0:T(8,128)(2,1)}, u32[]{:S(2)}) copy-start(bf16[128,256]{1,0:T(8,128)(2,1)} %layer_ref.1) | copy-start | bytes 196612
  17.6 33.1 %copy-start.3 = (f32[128,32]{0,1:T(8,128)S(1)}, f32[128,32]{0,1:T(8,128)}, u32[]{:S(2)}) copy-start(f32[128,32]{0,1:T(8,128)} %param.11) | copy-start | bytes 49156
  17.6 33.1 %copy-start.4 = (s32[2,128,32]{1,2,0:T(8,128)S(1)}, s32[2,128,32]{1,2,0:T(8,128)}, u32[]{:S(2)}) copy-start(s32[2,128,32]{1,2,0:T(8,128)} %param.12) | copy-start | bytes 98308
  28.5 6.2 %collective-permute-start.5 = (f32[32,128]{1,0:T(8,128)S(1)}, f32[32,128]{1,0:T(8,128)S(1)}, u32[]{:S(2)}, u32[]{:S(2)}) collective-permute-start(f32[32,128]{1,0:T(8,128)S(1)} %reduce_sum.9), channel_id=1, source_target_pairs={{0,3},{1,2},{2,1},{3,0},{4,7},{5,6},{6,5},{7,4},{8,11},{9,10},{10,... | collective-permute-start | bytes 49160 | tf_op jit(solution)/shard_map/ppermute | solution.py:252
  33.3 2.6 %collective-permute-start.4 = (f32[32,128]{1,0:T(8,128)S(1)}, f32[32,128]{1,0:T(8,128)S(1)}, u32[]{:S(2)}, u32[]{:S(2)}) collective-permute-start(f32[32,128]{1,0:T(8,128)S(1)} %reduce_sum.9), channel_id=1, source_target_pairs={{0,2},{1,3},{2,0},{3,1},{4,6},{5,7},{6,4},{7,5},{8,10},{9,11},{10,... | collective-permute-start | bytes 49160 | tf_op jit(solution)/shard_map/ppermute | solution.py:252
  33.3 2.6 %collective-permute-start.3 = (f32[32,128]{1,0:T(8,128)S(1)}, f32[32,128]{1,0:T(8,128)S(1)}, u32[]{:S(2)}, u32[]{:S(2)}) collective-permute-start(f32[32,128]{1,0:T(8,128)S(1)} %reduce_sum.9), channel_id=1, source_target_pairs={{0,1},{1,0},{2,3},{3,2},{4,5},{5,4},{6,7},{7,6},{8,9},{9,8},{10,11... | collective-permute-start | bytes 49160 | tf_op jit(solution)/shard_map/ppermute | solution.py:252
  35.9 17.9 %collective-permute-start.8 = (bf16[256,256]{1,0:T(8,128)(2,1)S(1)}, bf16[256,256]{1,0:T(8,128)(2,1)S(1)}, u32[]{:S(2)}, u32[]{:S(2)}) collective-permute-start(bf16[256,256]{1,0:T(8,128)(2,1)S(1)} %get-tuple-element.40), channel_id=1, source_target_pairs={{0,32},{16,48},{32,0},{48,16},{64,96},{80,112},{96,64},{112,80},{1... | collective-permute-start | bytes 393224 | tf_op jit(solution)/shard_map/ppermute | solution.py:267
  37.6 16.2 %collective-permute-start.9 = (bf16[256,256]{1,0:T(8,128)(2,1)S(1)}, bf16[256,256]{1,0:T(8,128)(2,1)S(1)}, u32[]{:S(2)}, u32[]{:S(2)}) collective-permute-start(bf16[256,256]{1,0:T(8,128)(2,1)S(1)} %get-tuple-element.41), channel_id=1, source_target_pairs={{0,16},{16,32},{32,48},{48,0},{64,80},{80,96},{96,112},{112,64},{1... | collective-permute-start | bytes 393224 | tf_op jit(solution)/shard_map/ppermute | solution.py:267
  38.2 15.6 %collective-permute-start.10 = (bf16[256,256]{1,0:T(8,128)(2,1)S(1)}, bf16[256,256]{1,0:T(8,128)(2,1)S(1)}, u32[]{:S(2)}, u32[]{:S(2)}) collective-permute-start(bf16[256,256]{1,0:T(8,128)(2,1)S(1)} %get-tuple-element.42), channel_id=1, source_target_pairs={{0,48},{16,0},{32,16},{48,32},{64,112},{80,64},{96,80},{112,96},{1... | collective-permute-start | bytes 393224 | tf_op jit(solution)/shard_map/ppermute | solution.py:267
  40.3 4.6 %collective-permute-start.6 = (f32[32,128]{1,0:T(8,128)S(1)}, f32[32,128]{1,0:T(8,128)S(1)}, u32[]{:S(2)}, u32[]{:S(2)}) collective-permute-start(f32[32,128]{1,0:T(8,128)S(1)} %add_add_fusion), channel_id=1, source_target_pairs={{0,4},{1,5},{2,6},{3,7},{4,0},{5,1},{6,2},{7,3},{8,12},{9,13},{10,... | collective-permute-start | bytes 49160 | tf_op jit(solution)/shard_map/ppermute | solution.py:252
  44.9 5.8 %collective-permute-start.7 = (f32[32,128]{1,0:T(8,128)S(1)}, f32[32,128]{1,0:T(8,128)S(1)}, u32[]{:S(2)}, u32[]{:S(2)}) collective-permute-start(f32[32,128]{1,0:T(8,128)S(1)} %add.18), channel_id=1, source_target_pairs={{0,12},{1,13},{2,14},{3,15},{4,8},{5,9},{6,10},{7,11},{8,4},{9,5},... | collective-permute-start | bytes 49160 | tf_op jit(solution)/shard_map/ppermute | solution.py:252
  53.8 22.5 %copy-start.7 = (f32[256,256]{1,0:T(8,128)S(1)}, f32[256,256]{1,0:T(8,128)}, u32[]{:S(2)}) copy-start(f32[256,256]{1,0:T(8,128)} %copy-done.6) | copy-start | bytes 786436
  70.7 7.0 %collective-permute-start.13 = (bf16[64,256]{1,0:T(8,128)(2,1)S(1)}, bf16[64,256]{1,0:T(8,128)(2,1)S(1)}, u32[]{:S(2)}, u32[]{:S(2)}) collective-permute-start(bf16[64,256]{1,0:T(8,128)(2,1)S(1)} %shard_map.107.own_ref), channel_id=1, source_target_pairs={{0,3},{1,2},{2,1},{3,0},{4,7},{5,6},{6,5},{7,4},{8,11},{9,10},{10,... | collective-permute-start | bytes 98312 | tf_op jit(solution)/shard_map/ppermute | solution.py:252
  75.6 3.3 %collective-permute-start.12 = (bf16[64,256]{1,0:T(8,128)(2,1)S(1)}, bf16[64,256]{1,0:T(8,128)(2,1)S(1)}, u32[]{:S(2)}, u32[]{:S(2)}) collective-permute-start(bf16[64,256]{1,0:T(8,128)(2,1)S(1)} %shard_map.107.own_ref), channel_id=1, source_target_pairs={{0,2},{1,3},{2,0},{3,1},{4,6},{5,7},{6,4},{7,5},{8,10},{9,11},{10,... | collective-permute-start | bytes 98312 | tf_op jit(solution)/shard_map/ppermute | solution.py:252
  76.3 2.6 %collective-permute-start.11 = (bf16[64,256]{1,0:T(8,128)(2,1)S(1)}, bf16[64,256]{1,0:T(8,128)(2,1)S(1)}, u32[]{:S(2)}, u32[]{:S(2)}) collective-permute-start(bf16[64,256]{1,0:T(8,128)(2,1)S(1)} %shard_map.107.own_ref), channel_id=1, source_target_pairs={{0,1},{1,0},{2,3},{3,2},{4,5},{5,4},{6,7},{7,6},{8,9},{9,8},{10,11... | collective-permute-start | bytes 98312 | tf_op jit(solution)/shard_map/ppermute | solution.py:252
where the time goes:
time: 79.9 us; the launch traced here: 79.6 us
  starting transfers between devices  33.3 us (42%)
  blocking collectives  25.2 us (32%)
  Pallas kernels  13.1 us (16%)
  waiting for transfers between devices  6.37 us (8%)
  between operations  0.8 us (1%)
    ppermute x8, starting transfers between devices, swap(): return lax.ppermute(x, 'mem', [(at, at ^ mask) for at in range(count)])  18.5 us
    all_to_all x1, blocking collectives, step_body(): parts = lax.all_to_all(parts, 'dp', 0, 0, tiled=True)  16.8 us
    pallas_call x8, Pallas kernels, run(): pl.pallas_call(kernel, out_shape=outs, in_specs=[FAR if at in far else VM...  13.1 us
    ppermute x6, starting transfers between devices, along_x(): lax.ppermute(x, 'dp', [(at, at // SIDE * SIDE + (at + shift) % SIDE) for...  9.8 us
    all_to_all x1, blocking collectives, step_body(): lax.all_to_all(slot_parts, 'dp', 0, 0, tiled=True, axis_index_groups=colu...  8.4 us
    ppermute x8, waiting for transfers between devices, swap(): return lax.ppermute(x, 'mem', [(at, at ^ mask) for at in range(count)])  5.9 us
    all_to_all x1, starting transfers between devices, step_body(): lax.all_to_all(sent, 'dp', 0, 0, tiled=True, axis_index_groups=columns)  5.01 us
  transfers between devices with their start and end apart: 15, of which 6 were waited for; matrix products, arithmetic and copies ran while one was open for 0% of the time, Pallas kernels for 10%

commit v1 on v0

--- a/solution.py
+++ b/solution.py
@@ -15,15 +15,15 @@
 FAR = pl.BlockSpec(memory_space=pltpu.HBM)
 
 
-def run(kernel, outs, args, scratch=(), flops=0, data=0, far=(), out_spec=VM, room=16):
+def run(kernel, outs, args, scratch=(), flops=0, data=0, far=()):
     return pl.pallas_call(
         kernel,
         out_shape=outs,
         in_specs=[FAR if at in far else VM for at in range(len(args))],
-        out_specs=jax.tree.map(lambda _: out_spec, outs),
+        out_specs=jax.tree.map(lambda _: VM, outs),
         scratch_shapes=list(scratch),
         cost_estimate=pl.CostEstimate(flops=flops, bytes_accessed=data, transcendentals=0),
-        compiler_params=pltpu.CompilerParams(vmem_limit_bytes=room * 2**20),
+        compiler_params=pltpu.CompilerParams(vmem_limit_bytes=16 * 2**20),
     )(*args)
 
 
@@ -37,28 +37,24 @@
     return ((ids & 127) + 128).astype(f32) * scale
 
 
-def pack_kernel(grad_ref, rows_ref, weights_ref, out_ref, one_ref, ids_ref, wide_ref, in_sem, out_sem):
+def pack_kernel(grad_ref, rows_ref, weights_ref, out_ref, ids_ref, wide_ref, sems):
     tokens = grad_ref.shape[0]
-    copies = (
-        pltpu.make_async_copy(rows_ref, ids_ref, in_sem.at[0]),
-        pltpu.make_async_copy(weights_ref, wide_ref, in_sem.at[1]),
-        pltpu.make_async_copy(grad_ref, one_ref.at[pl.ds(0, tokens), :], in_sem.at[2]),
-    )
+    copies = [
+        pltpu.make_async_copy(rows_ref, ids_ref, sems.at[0]),
+        pltpu.make_async_copy(weights_ref, wide_ref, sems.at[1]),
+    ]
+    for at in range(out_ref.shape[0]):
+        here = out_ref.at[at, pl.ds(0, tokens), :]
+        copies.append(pltpu.make_async_copy(grad_ref, here, sems.at[2 + at]))
     for copy in copies:
         copy.start()
     copies[0].wait()
     copies[1].wait()
-    both = jnp.concatenate([row_codes(ids_ref[...]), wide_ref[...]], axis=1)
-    one_ref[tokens:, :] = both.astype(bf16)
-    copies[2].wait()
-    sends = [
-        pltpu.make_async_copy(one_ref, out_ref.at[at], out_sem.at[at])
-        for at in range(out_ref.shape[0])
-    ]
-    for send in sends:
-        send.start()
-    for send in sends:
-        send.wait()
+    both = jnp.concatenate([row_codes(ids_ref[...]), wide_ref[...]], axis=1).astype(bf16)
+    for at in range(out_ref.shape[0]):
+        out_ref[at, tokens:, :] = both
+    for copy in copies[2:]:
+        copy.wait()
 
 
 def power_of(base, exponent, bits):
@@ -248,6 +244,10 @@
         out_ref[there >> 1, :, pl.ds(pl.multiple_of((there & 1) * cut, cut), cut)] = ref[...].astype(f32)
 
 
+def stay(x):
+    return pltpu.with_memory_space_constraint(x, pltpu.HBM)
+
+
 def swap(x, mask, count):
     return lax.ppermute(x, "mem", [(at, at ^ mask) for at in range(count)])
 
@@ -270,43 +270,40 @@
 
     columns = [[row * SIDE + column for row in range(SIDE)] for column in range(SIDE)]
 
-    near_values = [along_x(values, shift) for shift in (1, 2, 3)]
+    far_values = along_x(values, 2)
+    near_values = [along_x(values, 1), far_values, along_x(values, 3)]
     sent = run(
         pack_kernel,
         shape((SIDE, tokens + slots, width), bf16),
-        (grad_out, rows_t, weights_t),
+        [stay(x) for x in (grad_out, rows_t, weights_t)],
         scratch=(
-            pltpu.VMEM((tokens + slots, width), bf16),
             pltpu.VMEM((slots, tokens), jnp.int32),
             pltpu.VMEM((slots, tokens), f32),
-            pltpu.SemaphoreType.DMA((3,)),
-            pltpu.SemaphoreType.DMA((SIDE,)),
+            pltpu.SemaphoreType.DMA((2 + SIDE,)),
         ),
         far=(0, 1, 2),
-        out_spec=FAR,
-        room=60,
     )
     recv = lax.all_to_all(sent, "dp", 0, 0, tiled=True, axis_index_groups=columns)
-    shifts = (2, 1, 3, 0)
-    away = run(
-        functools.partial(value_kernel, shifts),
-        [shape((val_rows, width), bf16 if shift else f32) for shift in shifts],
-        (recv,),
-        scratch=(
-            pltpu.VMEM((SIDE, slots, tokens), f32),
-            pltpu.VMEM((SIDE, slots, tokens), f32),
-            pltpu.VMEM((val_rows, SIDE * tokens), bf16),
-            pltpu.VMEM((SIDE * tokens, width), bf16),
-        ),
-        flops=4 * 10**9,
-        data=2**21,
-    )
-    near = lax.optimization_barrier((*near_values, *away))
-    near_values, (two_away, one_away, three_away, mine) = near[:3], near[3:]
+
+    def value_part(shifts, recv):
+        return run(
+            functools.partial(value_kernel, shifts),
+            [shape((val_rows, width), bf16 if shift else f32) for shift in shifts],
+            (recv,),
+            scratch=(
+                pltpu.VMEM((SIDE, slots, tokens), f32),
+                pltpu.VMEM((SIDE, slots, tokens), f32),
+                pltpu.VMEM((val_rows, SIDE * tokens), bf16),
+                pltpu.VMEM((SIDE * tokens, width), bf16),
+            ),
+            flops=2 * 10**9,
+            data=2**20,
+        )
+
     slot_parts = run(
         slot_kernel,
         shape((SIDE, slots, tokens), f32),
-        (recv, values, *near_values),
+        (recv, stay(values), *near_values),
         scratch=(pltpu.VMEM((val_rows, width), bf16), pltpu.SemaphoreType.DMA(())),
         flops=10**9,
         data=2**20,
@@ -315,17 +312,21 @@
     slot_parts = lax.all_to_all(slot_parts, "dp", 0, 0, tiled=True, axis_index_groups=columns)
     slot_grad = jnp.sum(slot_parts, axis=0)
 
+    slot_grad, recv = lax.optimization_barrier((slot_grad, recv))
     one, two, three = (swap(slot_grad, mask, mem_count) for mask in (1, 2, 3))
+    two_away, one_away = value_part((2, 1), recv)
     slot_grad = (slot_grad + one) + (two + three)
-    slot_grad, two_away, one_away, three_away = lax.optimization_barrier(
-        (slot_grad, two_away, one_away, three_away)
-    )
+    slot_grad, recv, two_away, one_away = lax.optimization_barrier(
+        (slot_grad, recv, two_away, one_away)
+    )
+    step = swap(slot_grad, 4, mem_count)
     sums = [along_x(two_away, 2), along_x(one_away, 1)]
+    slot_grad = slot_grad + step
+    slot_grad, recv = lax.optimization_barrier((slot_grad, recv))
+    step = swap(slot_grad, 12, mem_count)
+    three_away, mine = value_part((3, 0), recv)
+    slot_grad = slot_grad + step
     sums.append(along_x(three_away, 3))
-    step = swap(slot_grad, 4, mem_count)
-    slot_grad = slot_grad + step
-    step = swap(slot_grad, 12, mem_count)
-    slot_grad = slot_grad + step
 
     own = subs // groups
     parts = run(

time: 79.9 us -> 78 us (0.976)
  starting transfers between devices: 33.3 us -> 31.6 us
    ppermute x6, waiting for transfers between devices: 0.02 us -> 4.7 us  [along_x(): lax.ppermute(x, 'dp', [(at, at // SIDE * SIDE + (at + shift) % SIDE) for...]
    ppermute x8, waiting for transfers between devices: 5.9 us -> 2.39 us  [swap(): return lax.ppermute(x, 'mem', [(at, at ^ mask) for at in range(count)])]
    ppermute x8, starting transfers between devices: 18.5 us -> 16.9 us  [swap(): return lax.ppermute(x, 'mem', [(at, at ^ mask) for at in range(count)])]
    pallas_call x8 -> x9, Pallas kernels: 13.1 us -> 12.4 us  [run(): pl.pallas_call(kernel, out_shape=outs, in_specs=[FAR if at in far else VM...]
  transfers between devices with their start and end apart: 15 -> 15, of which waited for: 6 -> 5; matrix products, arithmetic and copies ran while one was open for 0% -> 0% of each run, Pallas kernels for 10% -> 11%
where the time goes in v1:
time: 78 us; the launch traced here: 77.7 us
  starting transfers between devices  31.6 us (41%)
  blocking collectives  25.8 us (33%)
  Pallas kernels  12.4 us (16%)
  waiting for transfers between devices  7.1 us (9%)
  between operations  0.79 us (1%)
    all_to_all x1, blocking collectives, step_body(): parts = lax.all_to_all(parts, 'dp', 0, 0, tiled=True)  17.3 us
    ppermute x8, starting transfers between devices, swap(): return lax.ppermute(x, 'mem', [(at, at ^ mask) for at in range(count)])  16.9 us
    pallas_call x9, Pallas kernels, run(): pl.pallas_call(kernel, out_shape=outs, in_specs=[FAR if at in far else VM...  12.4 us
    ppermute x6, starting transfers between devices, along_x(): lax.ppermute(x, 'dp', [(at, at // SIDE * SIDE + (at + shift) % SIDE) for...  9.67 us
    all_to_all x1, blocking collectives, step_body(): lax.all_to_all(slot_parts, 'dp', 0, 0, tiled=True, axis_index_groups=colu...  8.53 us
    all_to_all x1, starting transfers between devices, step_body(): lax.all_to_all(sent, 'dp', 0, 0, tiled=True, axis_index_groups=columns)  5.01 us
    ppermute x6, waiting for transfers between devices, along_x(): lax.ppermute(x, 'dp', [(at, at // SIDE * SIDE + (at + shift) % SIDE) for...  4.7 us
    ppermute x8, waiting for transfers between devices, swap(): return lax.ppermute(x, 'mem', [(at, at ^ mask) for at in range(count)])  2.39 us
  transfers between devices with their start and end apart: 15, of which 5 were waited for; matrix products, arithmetic and copies ran while one was open for 0% of the time, Pallas kernels for 11%

profile of v1, /device:TPU:1, one launch (start us, length us, event | category | flops | bytes accessed | tf_op | source)
XLA Modules:
  0.0 77.7 jit_solution(13636063647967685364)
XLA Ops:
  0.6 1.8 %shard_map.103 = bf16[4,160,256]{2,1,0:T(8,128)(2,1)} custom-call(bf16[128,256]{1,0:T(8,128)(2,1)} %grad_ref.1, s32[32,128]{1,0:T(8,128)} %bitcast.6, f32[32,128]{1,0:T(8,128)} %bitcast.3), custom_call_target="tpu_custom_call" | custom-call | tf_op jit(solution)/shard_map/pallas_call | solution.py:19
  2.4 5.0 %all-to-all-start = ((bf16[4,160,256]{2,1,0:T(8,128)(2,1)}), bf16[4,160,256]{2,1,0:T(8,128)(2,1)S(1)}, u32[]{:S(2)}, u32[]{:S(2)}) async-start(bf16[4,160,256]{2,1,0:T(8,128)(2,1)} %shard_map.103), calls=%async_computation | async-start | bytes 655360 | tf_op jit(solution)/shard_map/all_to_all | solution.py:286
  7.4 2.7 %collective-permute-start.1 = (bf16[256,256]{1,0:T(8,128)(2,1)}, bf16[256,256]{1,0:T(8,128)(2,1)S(1)}, u32[]{:S(2)}, u32[]{:S(2)}) collective-permute-start(bf16[256,256]{1,0:T(8,128)(2,1)} %own_ref.1), channel_id=1, source_target_pairs={{0,32},{16,48},{32,0},{48,16},{64,96},{80,112},{96,64},{112,80},{1... | collective-permute-start | bytes 393224 | tf_op jit(solution)/shard_map/ppermute | solution.py:267
  10.2 0.3 collective-permute-start
  10.5 2.4 %collective-permute-start.2 = (bf16[256,256]{1,0:T(8,128)(2,1)}, bf16[256,256]{1,0:T(8,128)(2,1)S(1)}, u32[]{:S(2)}, u32[]{:S(2)}) collective-permute-start(bf16[256,256]{1,0:T(8,128)(2,1)} %own_ref.1), channel_id=1, source_target_pairs={{0,48},{16,0},{32,16},{48,32},{64,112},{80,64},{96,80},{112,96},{1... | collective-permute-start | bytes 393224 | tf_op jit(solution)/shard_map/ppermute | solution.py:267
  12.9 0.1 collective-permute-done.1.refs_1_
  13.0 4.6 %collective-permute-done.refs_0_ = bf16[256,256]{1,0:T(8,128)(2,1)S(1)} collective-permute-done((bf16[256,256]{1,0:T(8,128)(2,1)}, bf16[256,256]{1,0:T(8,128)(2,1)S(1)}, u32[]{:S(2)}, u32[]{:S(2)}) %collective-permute-start) | collective-permute-done | bytes 131104 | tf_op jit(solution)/shard_map/ppermute | solution.py:267
  17.6 0.0 collective-permute-done.2.refs_2_
  17.6 0.0 all-to-all-done.recv_ref
  17.6 1.5 %shard_map.104 = f32[4,32,128]{2,1,0:T(8,128)S(1)} custom-call(bf16[4,160,256]{2,1,0:T(8,128)(2,1)S(1)} %all-to-all-done.recv_ref, bf16[256,256]{1,0:T(8,128)(2,1)} %own_ref.1, bf16[256,256]{1,0:T(8,128)(2,1)S(1)} %collective-permute-done.refs_0_, bf16[256,256]{1,0:T(8,128)(2,1)S(1)} %collective-permute-done.1.refs_1_, ...), custom_call_target="tpu_custom_call" | custom-call | flops 1000000000 | bytes 1048576 | tf_op jit(solution)/shard_map/pallas_call | solution.py:19
  19.0 8.5 %all_to_all.15 = f32[4,32,128]{2,1,0:T(8,128)S(1)} all-to-all(f32[4,32,128]{2,1,0:T(8,128)S(1)} %shard_map.104), channel_id=1, replica_groups={{0,64,128,192},{16,80,144,208},{32,96,160,224},{48,112,176,240},{1,65,1..., dimensions={0} | all-to-all | bytes 131072 | tf_op jit(solution)/shard_map/all_to_all | solution.py:312
  27.6 4.0 %collective-permute-start.5 = (f32[32,128]{1,0:T(8,128)S(1)}, f32[32,128]{1,0:T(8,128)S(1)}, u32[]{:S(2)}, u32[]{:S(2)}) collective-permute-start(f32[32,128]{1,0:T(8,128)S(1)} %reduce_sum.9), channel_id=1, source_target_pairs={{0,3},{1,2},{2,1},{3,0},{4,7},{5,6},{6,5},{7,4},{8,11},{9,10},{10,... | collective-permute-start | bytes 49160 | tf_op jit(solution)/shard_map/ppermute | solution.py:252
  31.5 0.2 collective-permute-start.4
  31.8 0.3 collective-permute-start.3
  32.0 1.9 %shard_map.105 = (bf16[256,256]{1,0:T(8,128)(2,1)S(1)}, bf16[256,256]{1,0:T(8,128)(2,1)S(1)}) custom-call(bf16[4,160,256]{2,1,0:T(8,128)(2,1)S(1)} %all-to-all-done.recv_ref), custom_call_target="tpu_custom_call" | custom-call | flops 2000000000 | bytes 1048576 | tf_op jit(solution)/shard_map/pallas_call | solution.py:19
  33.9 0.0 collective-permute-done.5
  34.0 0.2 collective-permute-done.4
  34.1 0.0 collective-permute-done.3
  34.1 3.1 %collective-permute-start.6 = (f32[32,128]{1,0:T(8,128)S(1)}, f32[32,128]{1,0:T(8,128)S(1)}, u32[]{:S(2)}, u32[]{:S(2)}) collective-permute-start(f32[32,128]{1,0:T(8,128)S(1)} %add_add_fusion), channel_id=1, source_target_pairs={{0,4},{1,5},{2,6},{3,7},{4,0},{5,1},{6,2},{7,3},{8,12},{9,13},{10,... | collective-permute-start | bytes 49160 | tf_op jit(solution)/shard_map/ppermute | solution.py:252
  37.2 1.5 %collective-permute-start.8 = (bf16[256,256]{1,0:T(8,128)(2,1)S(1)}, bf16[256,256]{1,0:T(8,128)(2,1)S(1)}, u32[]{:S(2)}, u32[]{:S(2)}) collective-permute-start(bf16[256,256]{1,0:T(8,128)(2,1)S(1)} %get-tuple-element.34), channel_id=1, source_target_pairs={{0,32},{16,48},{32,0},{48,16},{64,96},{80,112},{96,64},{112,80},{1... | collective-permute-start | bytes 393224 | tf_op jit(solution)/shard_map/ppermute | solution.py:267
  38.7 1.7 %collective-permute-start.9 = (bf16[256,256]{1,0:T(8,128)(2,1)S(1)}, bf16[256,256]{1,0:T(8,128)(2,1)S(1)}, u32[]{:S(2)}, u32[]{:S(2)}) collective-permute-start(bf16[256,256]{1,0:T(8,128)(2,1)S(1)} %get-tuple-element.35), channel_id=1, source_target_pairs={{0,16},{16,32},{32,48},{48,0},{64,80},{80,96},{96,112},{112,64},{1... | collective-permute-start | bytes 393224 | tf_op jit(solution)/shard_map/ppermute | solution.py:267
  40.4 0.0 collective-permute-done.6
  40.4 0.0 copy-start
  40.4 0.0 copy-start.1
  40.5 0.0 copy-start.2
  40.5 0.0 copy-start.3
  40.5 0.0 copy-start.4
  40.5 1.9 %shard_map.107 = (bf16[256,256]{1,0:T(8,128)(2,1)S(1)}, f32[256,256]{1,0:T(8,128)S(1)}) custom-call(bf16[4,160,256]{2,1,0:T(8,128)(2,1)S(1)} %all-to-all-done.recv_ref), custom_call_target="tpu_custom_call" | custom-call | flops 2000000000 | bytes 1048576 | tf_op jit(solution)/shard_map/pallas_call | solution.py:19
  42.4 1.0 %collective-permute-start.10 = (bf16[256,256]{1,0:T(8,128)(2,1)S(1)}, bf16[256,256]{1,0:T(8,128)(2,1)S(1)}, u32[]{:S(2)}, u32[]{:S(2)}) collective-permute-start(bf16[256,256]{1,0:T(8,128)(2,1)S(1)} %get-tuple-element.36), channel_id=1, source_target_pairs={{0,48},{16,0},{32,16},{48,32},{64,112},{80,64},{96,80},{112,96},{1... | collective-permute-start | bytes 393224 | tf_op jit(solution)/shard_map/ppermute | solution.py:267
  43.4 4.4 %collective-permute-start.7 = (f32[32,128]{1,0:T(8,128)S(1)}, f32[32,128]{1,0:T(8,128)S(1)}, u32[]{:S(2)}, u32[]{:S(2)}) collective-permute-start(f32[32,128]{1,0:T(8,128)S(1)} %add.18), channel_id=1, source_target_pairs={{0,12},{1,13},{2,14},{3,15},{4,8},{5,9},{6,10},{7,11},{8,4},{9,5},... | collective-permute-start | bytes 49160 | tf_op jit(solution)/shard_map/ppermute | solution.py:252
  47.8 1.1 %collective-permute-done.7 = f32[32,128]{1,0:T(8,128)S(1)} collective-permute-done((f32[32,128]{1,0:T(8,128)S(1)}, f32[32,128]{1,0:T(8,128)S(1)}, u32[]{:S(2)}, u32[]{:S(2)}) %collective-permute-start.7) | collective-permute-done | bytes 16416 | tf_op jit(solution)/shard_map/ppermute | solution.py:252
  49.0 0.0 copy-done
  49.0 0.0 copy-done.1
  49.0 0.0 copy-done.2
  49.0 0.0 copy-done.3
  49.0 0.0 copy-done.4
  49.0 3.0 %shard_map.106 = bf16[16,128,256]{2,1,0:T(8,128)(2,1)S(1)} custom-call(f32[32,128]{1,0:T(8,128)S(1)} %add.19.slot_ref, f32[32,128]{1,0:T(8,128)S(1)} %bitcast.4, s32[2,32,128]{2,1,0:T(8,128)S(1)} %bitcast.5, bf16[128,1024]{1,0:T(8,128)(2,1)S(1)} %copy-done.1, bf16[2,1024,512]{2,1,0:T(8,128)(2,1)S(1)} %copy-done, bf16[128,256]{1,0:T(8,128)(2,1)S(1)} %copy-done.2), custom_call_target="tpu_custom_call" | custom-call | tf_op jit(solution)/shard_map/pallas_call | solution.py:19
  52.1 0.0 collective-permute-done.8.refs_1_
  52.1 0.0 collective-permute-done.9.refs_2_
  52.1 0.0 collective-permute-done.10.refs_3_
  52.1 17.3 %all_to_all.16.parts_ref = bf16[16,128,256]{2,1,0:T(8,128)(2,1)S(1)} all-to-all(bf16[16,128,256]{2,1,0:T(8,128)(2,1)S(1)} %shard_map.106), channel_id=1, replica_groups=mesh['dp'=16,'mem'=16] {'dp'}, dimensions={0} | all-to-all | bytes 2097152 | tf_op jit(solution)/shard_map/all_to_all | solution.py:348
  69.4 0.1 shard_map.108.own_ref
  69.4 4.3 %collective-permute-start.13 = (bf16[64,256]{1,0:T(8,128)(2,1)S(1)}, bf16[64,256]{1,0:T(8,128)(2,1)S(1)}, u32[]{:S(2)}, u32[]{:S(2)}) collective-permute-start(bf16[64,256]{1,0:T(8,128)(2,1)S(1)} %shard_map.108.own_ref), channel_id=1, source_target_pairs={{0,3},{1,2},{2,1},{3,0},{4,7},{5,6},{6,5},{7,4},{8,11},{9,10},{10,... | collective-permute-start | bytes 98312 | tf_op jit(solution)/shard_map/ppermute | solution.py:252
  73.7 0.7 collective-permute-start.12
  74.4 0.0 collective-permute-start.11
  74.4 0.8 shard_map.109
  75.2 0.7 shard_map.111
  75.9 0.0 collective-permute-done.13.three_ref
  75.9 1.1 %collective-permute-done.12.two_ref = bf16[64,256]{1,0:T(8,128)(2,1)S(1)} collective-permute-done((bf16[64,256]{1,0:T(8,128)(2,1)S(1)}, bf16[64,256]{1,0:T(8,128)(2,1)S(1)}, u32[]{:S(2)}, u32[]{:S(2)}) %collective-permute-start.12) | collective-permute-done | bytes 32800 | tf_op jit(solution)/shard_map/ppermute | solution.py:252
  77.0 0.0 collective-permute-done.11.one_ref
  77.0 0.7 shard_map.110
  (4 shorter events, 0.0 us)
Async XLA Ops:
  2.4 15.1 %all-to-all-start = ((bf16[4,160,256]{2,1,0:T(8,128)(2,1)}), bf16[4,160,256]{2,1,0:T(8,128)(2,1)S(1)}, u32[]{:S(2)}, u32[]{:S(2)}) async-start(bf16[4,160,256]{2,1,0:T(8,128)(2,1)} %shard_map.103), calls=%async_computation | async-start | bytes 655360 | tf_op jit(solution)/shard_map/all_to_all | solution.py:286
  7.4 5.5 %collective-permute-start.1 = (bf16[256,256]{1,0:T(8,128)(2,1)}, bf16[256,256]{1,0:T(8,128)(2,1)S(1)}, u32[]{:S(2)}, u32[]{:S(2)}) collective-permute-start(bf16[256,256]{1,0:T(8,128)(2,1)} %own_ref.1), channel_id=1, source_target_pairs={{0,32},{16,48},{32,0},{48,16},{64,96},{80,112},{96,64},{112,80},{1... | collective-permute-start | bytes 393224 | tf_op jit(solution)/shard_map/ppermute | solution.py:267
  10.2 7.4 %collective-permute-start = (bf16[256,256]{1,0:T(8,128)(2,1)}, bf16[256,256]{1,0:T(8,128)(2,1)S(1)}, u32[]{:S(2)}, u32[]{:S(2)}) collective-permute-start(bf16[256,256]{1,0:T(8,128)(2,1)} %own_ref.1), channel_id=1, source_target_pairs={{0,16},{16,32},{32,48},{48,0},{64,80},{80,96},{96,112},{112,64},{1... | collective-permute-start | bytes 393224 | tf_op jit(solution)/shard_map/ppermute | solution.py:267
  10.5 7.1 %collective-permute-start.2 = (bf16[256,256]{1,0:T(8,128)(2,1)}, bf16[256,256]{1,0:T(8,128)(2,1)S(1)}, u32[]{:S(2)}, u32[]{:S(2)}) collective-permute-start(bf16[256,256]{1,0:T(8,128)(2,1)} %own_ref.1), channel_id=1, source_target_pairs={{0,48},{16,0},{32,16},{48,32},{64,112},{80,64},{96,80},{112,96},{1... | collective-permute-start | bytes 393224 | tf_op jit(solution)/shard_map/ppermute | solution.py:267
  27.6 6.4 %collective-permute-start.5 = (f32[32,128]{1,0:T(8,128)S(1)}, f32[32,128]{1,0:T(8,128)S(1)}, u32[]{:S(2)}, u32[]{:S(2)}) collective-permute-start(f32[32,128]{1,0:T(8,128)S(1)} %reduce_sum.9), channel_id=1, source_target_pairs={{0,3},{1,2},{2,1},{3,0},{4,7},{5,6},{6,5},{7,4},{8,11},{9,10},{10,... | collective-permute-start | bytes 49160 | tf_op jit(solution)/shard_map/ppermute | solution.py:252
  31.5 2.6 %collective-permute-start.4 = (f32[32,128]{1,0:T(8,128)S(1)}, f32[32,128]{1,0:T(8,128)S(1)}, u32[]{:S(2)}, u32[]{:S(2)}) collective-permute-start(f32[32,128]{1,0:T(8,128)S(1)} %reduce_sum.9), channel_id=1, source_target_pairs={{0,2},{1,3},{2,0},{3,1},{4,6},{5,7},{6,4},{7,5},{8,10},{9,11},{10,... | collective-permute-start | bytes 49160 | tf_op jit(solution)/shard_map/ppermute | solution.py:252
  31.8 2.4 %collective-permute-start.3 = (f32[32,128]{1,0:T(8,128)S(1)}, f32[32,128]{1,0:T(8,128)S(1)}, u32[]{:S(2)}, u32[]{:S(2)}) collective-permute-start(f32[32,128]{1,0:T(8,128)S(1)} %reduce_sum.9), channel_id=1, source_target_pairs={{0,1},{1,0},{2,3},{3,2},{4,5},{5,4},{6,7},{7,6},{8,9},{9,8},{10,11... | collective-permute-start | bytes 49160 | tf_op jit(solution)/shard_map/ppermute | solution.py:252
  34.1 6.3 %collective-permute-start.6 = (f32[32,128]{1,0:T(8,128)S(1)}, f32[32,128]{1,0:T(8,128)S(1)}, u32[]{:S(2)}, u32[]{:S(2)}) collective-permute-start(f32[32,128]{1,0:T(8,128)S(1)} %add_add_fusion), channel_id=1, source_target_pairs={{0,4},{1,5},{2,6},{3,7},{4,0},{5,1},{6,2},{7,3},{8,12},{9,13},{10,... | collective-permute-start | bytes 49160 | tf_op jit(solution)/shard_map/ppermute | solution.py:252
  37.2 14.9 %collective-permute-start.8 = (bf16[256,256]{1,0:T(8,128)(2,1)S(1)}, bf16[256,256]{1,0:T(8,128)(2,1)S(1)}, u32[]{:S(2)}, u32[]{:S(2)}) collective-permute-start(bf16[256,256]{1,0:T(8,128)(2,1)S(1)} %get-tuple-element.34), channel_id=1, source_target_pairs={{0,32},{16,48},{32,0},{48,16},{64,96},{80,112},{96,64},{112,80},{1... | collective-permute-start | bytes 393224 | tf_op jit(solution)/shard_map/ppermute | solution.py:267
  38.7 13.4 %collective-permute-start.9 = (bf16[256,256]{1,0:T(8,128)(2,1)S(1)}, bf16[256,256]{1,0:T(8,128)(2,1)S(1)}, u32[]{:S(2)}, u32[]{:S(2)}) collective-permute-start(bf16[256,256]{1,0:T(8,128)(2,1)S(1)} %get-tuple-element.35), channel_id=1, source_target_pairs={{0,16},{16,32},{32,48},{48,0},{64,80},{80,96},{96,112},{112,64},{1... | collective-permute-start | bytes 393224 | tf_op jit(solution)/shard_map/ppermute | solution.py:267
  40.4 8.5 %copy-start = (bf16[2,1024,512]{2,1,0:T(8,128)(2,1)S(1)}, bf16[2,1024,512]{2,1,0:T(8,128)(2,1)}, u32[]{:S(2)}) copy-start(bf16[2,1024,512]{2,1,0:T(8,128)(2,1)} %keys_ref.1) | copy-start | bytes 6291460
  40.4 8.5 %copy-start.1 = (bf16[128,1024]{1,0:T(8,128)(2,1)S(1)}, bf16[128,1024]{1,0:T(8,128)(2,1)}, u32[]{:S(2)}) copy-start(bf16[128,1024]{1,0:T(8,128)(2,1)} %queries_ref.1) | copy-start | bytes 786436
  40.5 8.5 %copy-start.2 = (bf16[128,256]{1,0:T(8,128)(2,1)S(1)}, bf16[128,256]{1,0:T(8,128)(2,1)}, u32[]{:S(2)}) copy-start(bf16[128,256]{1,0:T(8,128)(2,1)} %layer_ref.1) | copy-start | bytes 196612
  40.5 8.5 %copy-start.3 = (f32[128,32]{0,1:T(8,128)S(1)}, f32[128,32]{0,1:T(8,128)}, u32[]{:S(2)}) copy-start(f32[128,32]{0,1:T(8,128)} %param.11) | copy-start | bytes 49156
  40.5 8.5 %copy-start.4 = (s32[2,128,32]{1,2,0:T(8,128)S(1)}, s32[2,128,32]{1,2,0:T(8,128)}, u32[]{:S(2)}) copy-start(s32[2,128,32]{1,2,0:T(8,128)} %param.12) | copy-start | bytes 98308
  42.4 9.7 %collective-permute-start.10 = (bf16[256,256]{1,0:T(8,128)(2,1)S(1)}, bf16[256,256]{1,0:T(8,128)(2,1)S(1)}, u32[]{:S(2)}, u32[]{:S(2)}) collective-permute-start(bf16[256,256]{1,0:T(8,128)(2,1)S(1)} %get-tuple-element.36), channel_id=1, source_target_pairs={{0,48},{16,0},{32,16},{48,32},{64,112},{80,64},{96,80},{112,96},{1... | collective-permute-start | bytes 393224 | tf_op jit(solution)/shard_map/ppermute | solution.py:267
  43.4 5.5 %collective-permute-start.7 = (f32[32,128]{1,0:T(8,128)S(1)}, f32[32,128]{1,0:T(8,128)S(1)}, u32[]{:S(2)}, u32[]{:S(2)}) collective-permute-start(f32[32,128]{1,0:T(8,128)S(1)} %add.18), channel_id=1, source_target_pairs={{0,12},{1,13},{2,14},{3,15},{4,8},{5,9},{6,10},{7,11},{8,4},{9,5},... | collective-permute-start | bytes 49160 | tf_op jit(solution)/shard_map/ppermute | solution.py:252
  69.4 6.5 %collective-permute-start.13 = (bf16[64,256]{1,0:T(8,128)(2,1)S(1)}, bf16[64,256]{1,0:T(8,128)(2,1)S(1)}, u32[]{:S(2)}, u32[]{:S(2)}) collective-permute-start(bf16[64,256]{1,0:T(8,128)(2,1)S(1)} %shard_map.108.own_ref), channel_id=1, source_target_pairs={{0,3},{1,2},{2,1},{3,0},{4,7},{5,6},{6,5},{7,4},{8,11},{9,10},{10,... | collective-permute-start | bytes 98312 | tf_op jit(solution)/shard_map/ppermute | solution.py:252
  73.7 3.3 %collective-permute-start.12 = (bf16[64,256]{1,0:T(8,128)(2,1)S(1)}, bf16[64,256]{1,0:T(8,128)(2,1)S(1)}, u32[]{:S(2)}, u32[]{:S(2)}) collective-permute-start(bf16[64,256]{1,0:T(8,128)(2,1)S(1)} %shard_map.108.own_ref), channel_id=1, source_target_pairs={{0,2},{1,3},{2,0},{3,1},{4,6},{5,7},{6,4},{7,5},{8,10},{9,11},{10,... | collective-permute-start | bytes 98312 | tf_op jit(solution)/shard_map/ppermute | solution.py:252
  74.4 2.6 %collective-permute-start.11 = (bf16[64,256]{1,0:T(8,128)(2,1)S(1)}, bf16[64,256]{1,0:T(8,128)(2,1)S(1)}, u32[]{:S(2)}, u32[]{:S(2)}) collective-permute-start(bf16[64,256]{1,0:T(8,128)(2,1)S(1)} %shard_map.108.own_ref), channel_id=1, source_target_pairs={{0,1},{1,0},{2,3},{3,2},{4,5},{5,4},{6,7},{7,6},{8,9},{9,8},{10,11... | collective-permute-start | bytes 98312 | tf_op jit(solution)/shard_map/ppermute | solution.py:252

commit v2 on v1

--- a/solution.py
+++ b/solution.py
@@ -77,20 +77,22 @@
 
 
 def slot_kernel(recv_ref, own_ref, *refs):
-    values_refs, (out_ref, own_here_ref, sem) = refs[:-3], refs[-3:]
-    blocks, slots, tokens = out_ref.shape
+    values_refs, out_refs, (own_here_ref, sem) = refs[: SIDE - 1], refs[SIDE - 1 : -2], refs[-2:]
+    slots, tokens = out_refs[0].shape
     val_rows = own_ref.shape[0]
-    column = lax.axis_index("dp") % SIDE
+    owner = lax.axis_index("dp")
+    row, column = owner // SIDE, owner % SIDE
     fetch = pltpu.make_async_copy(own_ref, own_here_ref, sem)
     fetch.start()
-    rows = [group_rows(recv_ref[at, tokens:, :tokens]) for at in range(blocks)]
-    accs = [[jnp.zeros((8, tokens), f32) for _ in range(slots // 8)] for _ in range(blocks)]
-    for shift in range(len(values_refs), -1, -1):
+    blocks = [(row + away) % SIDE for away in range(SIDE)]
+    local = [group_rows(recv_ref[at, tokens:, :tokens]) for at in blocks]
+    accs = [[jnp.zeros((8, tokens), f32) for _ in range(slots // 8)] for _ in blocks]
+    for shift in range(SIDE - 1, -1, -1):
         if shift == 0:
             fetch.wait()
         values_ref = values_refs[shift - 1] if shift else own_here_ref
         first = ((column + SIDE - shift) % SIDE) * (val_rows // 8)
-        for at in range(blocks):
+        for away, at in enumerate(blocks):
             score = lax.dot_general(
                 values_ref[...],
                 recv_ref[at, :tokens, :],
@@ -98,14 +100,14 @@
                 preferred_element_type=f32,
             )
             for part in range(slots // 8):
-                row = rows[at][part * 8 : part * 8 + 8]
-                low, high = row & 7, (row >> 3) - first
+                rows = local[away][part * 8 : part * 8 + 8]
+                low, high = rows & 7, (rows >> 3) - first
                 for tile in range(val_rows // 8):
                     got = jnp.take_along_axis(score[tile * 8 : tile * 8 + 8], low, axis=0)
-                    accs[at][part] = jnp.where(high == tile, got, accs[at][part])
-    for at in range(blocks):
+                    accs[away][part] = jnp.where(high == tile, got, accs[away][part])
+    for away, out_ref in enumerate(out_refs):
         for part in range(slots // 8):
-            out_ref[at, part * 8 : part * 8 + 8, :] = accs[at][part]
+            out_ref[part * 8 : part * 8 + 8, :] = accs[away][part]
 
 
 def wide_row(ref, at):
@@ -268,6 +270,9 @@
             x, "dp", [(at, at // SIDE * SIDE + (at + shift) % SIDE) for at in range(groups)]
         )
 
+    def along_y(x, shift):
+        return lax.ppermute(x, "dp", [(at, (at + shift * SIDE) % groups) for at in range(groups)])
+
     columns = [[row * SIDE + column for row in range(SIDE)] for column in range(SIDE)]
 
     far_values = along_x(values, 2)
@@ -302,31 +307,31 @@
 
     slot_parts = run(
         slot_kernel,
-        shape((SIDE, slots, tokens), f32),
+        [shape((slots, tokens), f32)] * SIDE,
         (recv, stay(values), *near_values),
         scratch=(pltpu.VMEM((val_rows, width), bf16), pltpu.SemaphoreType.DMA(())),
         flops=10**9,
         data=2**20,
         far=(1,),
     )
-    slot_parts = lax.all_to_all(slot_parts, "dp", 0, 0, tiled=True, axis_index_groups=columns)
-    slot_grad = jnp.sum(slot_parts, axis=0)
-
-    slot_grad, recv = lax.optimization_barrier((slot_grad, recv))
+    *slot_parts, recv = lax.optimization_barrier((*slot_parts, recv))
+    back = [along_y(slot_parts[shift], shift) for shift in (1, 2, 3)]
+    aways = value_part((2, 1, 3), recv)
+    slot_grad = (slot_parts[0] + back[0]) + (back[1] + back[2])
+    slot_grad, recv, *aways = lax.optimization_barrier((slot_grad, recv, *aways))
+    two_away, one_away, three_away = aways
+
     one, two, three = (swap(slot_grad, mask, mem_count) for mask in (1, 2, 3))
-    two_away, one_away = value_part((2, 1), recv)
     slot_grad = (slot_grad + one) + (two + three)
-    slot_grad, recv, two_away, one_away = lax.optimization_barrier(
-        (slot_grad, recv, two_away, one_away)
-    )
+    slot_grad, two_away, one_away = lax.optimization_barrier((slot_grad, two_away, one_away))
     step = swap(slot_grad, 4, mem_count)
     sums = [along_x(two_away, 2), along_x(one_away, 1)]
     slot_grad = slot_grad + step
-    slot_grad, recv = lax.optimization_barrier((slot_grad, recv))
+    slot_grad, recv, three_away = lax.optimization_barrier((slot_grad, recv, three_away))
     step = swap(slot_grad, 12, mem_count)
-    three_away, mine = value_part((3, 0), recv)
+    sums.append(along_x(three_away, 3))
+    (mine,) = value_part((0,), recv)
     slot_grad = slot_grad + step
-    sums.append(along_x(three_away, 3))
 
     own = subs // groups
     parts = run(

time: 78 us -> 76.1 us (0.976)
  blocking collectives: 25.8 us -> 17.5 us
  starting transfers between devices: 31.6 us -> 37 us
  waiting for transfers between devices: 7.1 us -> 7.89 us
    all_to_all x1 -> x0, blocking collectives: 8.53 us -> none  [step_body(): lax.all_to_all(slot_parts, 'dp', 0, 0, tiled=True, axis_index_groups=colu...]
    ppermute x0 -> x3, starting transfers between devices: none -> 5.13 us  [along_y(): lax.ppermute(x, 'dp', [(at, (at + shift * SIDE) % groups) for at in range...]
    ppermute x8, waiting for transfers between devices: 2.39 us -> 3.18 us  [swap(): return lax.ppermute(x, 'mem', [(at, at ^ mask) for at in range(count)])]
  transfers between devices with their start and end apart: 15 -> 18, of which waited for: 5 -> 5; matrix products, arithmetic and copies ran while one was open for 0% -> 0% of each run, Pallas kernels for 11% -> 11%
where the time goes in v2:
time: 76.1 us; the launch traced here: 75.8 us
  starting transfers between devices  37 us (49%)
  blocking collectives  17.5 us (23%)
  Pallas kernels  12.6 us (17%)
  waiting for transfers between devices  7.89 us (10%)
  between operations  0.84 us (1%)
    all_to_all x1, blocking collectives, step_body(): parts = lax.all_to_all(parts, 'dp', 0, 0, tiled=True)  17.5 us
    ppermute x8, starting transfers between devices, swap(): return lax.ppermute(x, 'mem', [(at, at ^ mask) for at in range(count)])  16.5 us
    pallas_call x9, Pallas kernels, run(): pl.pallas_call(kernel, out_shape=outs, in_specs=[FAR if at in far else VM...  12.6 us
    ppermute x6, starting transfers between devices, along_x(): lax.ppermute(x, 'dp', [(at, at // SIDE * SIDE + (at + shift) % SIDE) for...  10.3 us
    ppermute x3, starting transfers between devices, along_y(): lax.ppermute(x, 'dp', [(at, (at + shift * SIDE) % groups) for at in range...  5.13 us
    all_to_all x1, starting transfers between devices, step_body(): lax.all_to_all(sent, 'dp', 0, 0, tiled=True, axis_index_groups=columns)  5.01 us
    ppermute x6, waiting for transfers between devices, along_x(): lax.ppermute(x, 'dp', [(at, at // SIDE * SIDE + (at + shift) % SIDE) for...  4.7 us
    ppermute x8, waiting for transfers between devices, swap(): return lax.ppermute(x, 'mem', [(at, at ^ mask) for at in range(count)])  3.18 us
  transfers between devices with their start and end apart: 18, of which 5 were waited for; matrix products, arithmetic and copies ran while one was open for 0% of the time, Pallas kernels for 11%

profile of v2, /device:TPU:1, one launch (start us, length us, event | category | flops | bytes accessed | tf_op | source)
XLA Modules:
  0.0 75.8 jit_solution(17958413564127441105)
XLA Ops:
  0.6 1.8 %shard_map.103 = bf16[4,160,256]{2,1,0:T(8,128)(2,1)} custom-call(bf16[128,256]{1,0:T(8,128)(2,1)} %grad_ref.1, s32[32,128]{1,0:T(8,128)} %bitcast.6, f32[32,128]{1,0:T(8,128)} %bitcast.3), custom_call_target="tpu_custom_call" | custom-call | tf_op jit(solution)/shard_map/pallas_call | solution.py:19
  2.4 5.0 %all-to-all-start = ((bf16[4,160,256]{2,1,0:T(8,128)(2,1)}), bf16[4,160,256]{2,1,0:T(8,128)(2,1)S(1)}, u32[]{:S(2)}, u32[]{:S(2)}) async-start(bf16[4,160,256]{2,1,0:T(8,128)(2,1)} %shard_map.103), calls=%async_computation | async-start | bytes 655360 | tf_op jit(solution)/shard_map/all_to_all | solution.py:291
  7.4 2.7 %collective-permute-start.1 = (bf16[256,256]{1,0:T(8,128)(2,1)}, bf16[256,256]{1,0:T(8,128)(2,1)S(1)}, u32[]{:S(2)}, u32[]{:S(2)}) collective-permute-start(bf16[256,256]{1,0:T(8,128)(2,1)} %own_ref.1), channel_id=1, source_target_pairs={{0,32},{16,48},{32,0},{48,16},{64,96},{80,112},{96,64},{112,80},{1... | collective-permute-start | bytes 393224 | tf_op jit(solution)/shard_map/ppermute | solution.py:269
  10.2 0.3 collective-permute-start
  10.5 2.4 %collective-permute-start.2 = (bf16[256,256]{1,0:T(8,128)(2,1)}, bf16[256,256]{1,0:T(8,128)(2,1)S(1)}, u32[]{:S(2)}, u32[]{:S(2)}) collective-permute-start(bf16[256,256]{1,0:T(8,128)(2,1)} %own_ref.1), channel_id=1, source_target_pairs={{0,48},{16,0},{32,16},{48,32},{64,112},{80,64},{96,80},{112,96},{1... | collective-permute-start | bytes 393224 | tf_op jit(solution)/shard_map/ppermute | solution.py:269
  12.8 0.1 collective-permute-done.1.refs_1_
  13.0 4.6 %collective-permute-done.refs_0_ = bf16[256,256]{1,0:T(8,128)(2,1)S(1)} collective-permute-done((bf16[256,256]{1,0:T(8,128)(2,1)}, bf16[256,256]{1,0:T(8,128)(2,1)S(1)}, u32[]{:S(2)}, u32[]{:S(2)}) %collective-permute-start) | collective-permute-done | bytes 131104 | tf_op jit(solution)/shard_map/ppermute | solution.py:269
  17.5 0.0 collective-permute-done.2.refs_2_
  17.5 0.0 all-to-all-done.recv_ref
  17.5 1.8 %shard_map.104 = (f32[32,128]{1,0:T(8,128)S(1)}, f32[32,128]{1,0:T(8,128)S(1)}, f32[32,128]{1,0:T(8,128)S(1)}, f32[32,128]{1,0:T(8,128)S(1)}) custom-call(bf16[4,160,256]{2,1,0:T(8,128)(2,1)S(1)} %all-to-all-done.recv_ref, bf16[256,256]{1,0:T(8,128)(2,1)} %own_ref.1, bf16[256,256]{1,0:T(8,128)(2,1)S(1)} %collective-permute-done.refs_0_, ...), custom_call_target="tpu_custom_call" | custom-call | flops 1000000000 | bytes 1048576 | tf_op jit(solution)/shard_map/pallas_call | solution.py:19
  19.4 1.6 %collective-permute-start.3 = (f32[32,128]{1,0:T(8,128)S(1)}, f32[32,128]{1,0:T(8,128)S(1)}, u32[]{:S(2)}, u32[]{:S(2)}) collective-permute-start(f32[32,128]{1,0:T(8,128)S(1)} %get-tuple-element.41), channel_id=1, source_target_pairs={{0,64},{16,80},{32,96},{48,112},{64,128},{80,144},{96,160},{112,17... | collective-permute-start | bytes 49160 | tf_op jit(solution)/shard_map/ppermute | solution.py:274
  20.9 2.4 %collective-permute-start.4 = (f32[32,128]{1,0:T(8,128)S(1)}, f32[32,128]{1,0:T(8,128)S(1)}, u32[]{:S(2)}, u32[]{:S(2)}) collective-permute-start(f32[32,128]{1,0:T(8,128)S(1)} %get-tuple-element.42), channel_id=1, source_target_pairs={{0,128},{16,144},{32,160},{48,176},{64,192},{80,208},{96,224},{112... | collective-permute-start | bytes 49160 | tf_op jit(solution)/shard_map/ppermute | solution.py:274
  23.3 1.2 %collective-permute-start.5 = (f32[32,128]{1,0:T(8,128)S(1)}, f32[32,128]{1,0:T(8,128)S(1)}, u32[]{:S(2)}, u32[]{:S(2)}) collective-permute-start(f32[32,128]{1,0:T(8,128)S(1)} %get-tuple-element.43), channel_id=1, source_target_pairs={{0,192},{16,208},{32,224},{48,240},{64,0},{80,16},{96,32},{112,48}... | collective-permute-start | bytes 49160 | tf_op jit(solution)/shard_map/ppermute | solution.py:274
  24.5 2.8 %shard_map.105 = (bf16[256,256]{1,0:T(8,128)(2,1)S(1)}, bf16[256,256]{1,0:T(8,128)(2,1)S(1)}, bf16[256,256]{1,0:T(8,128)(2,1)S(1)}) custom-call(bf16[4,160,256]{2,1,0:T(8,128)(2,1)S(1)} %all-to-all-done.recv_ref), custom_call_target="tpu_custom_call" | custom-call | flops 2000000000 | bytes 1048576 | tf_op jit(solution)/shard_map/pallas_call | solution.py:19
  27.3 0.0 collective-permute-done.3
  27.3 0.0 collective-permute-done.4
  27.3 0.0 collective-permute-done.5
  27.3 3.4 %collective-permute-start.8 = (f32[32,128]{1,0:T(8,128)S(1)}, f32[32,128]{1,0:T(8,128)S(1)}, u32[]{:S(2)}, u32[]{:S(2)}) collective-permute-start(f32[32,128]{1,0:T(8,128)S(1)} %add_add_fusion.1), channel_id=1, source_target_pairs={{0,3},{1,2},{2,1},{3,0},{4,7},{5,6},{6,5},{7,4},{8,11},{9,10},{10,... | collective-permute-start | bytes 49160 | tf_op jit(solution)/shard_map/ppermute | solution.py:254
  30.7 0.2 collective-permute-start.7
  30.9 0.3 collective-permute-start.6
  31.2 1.2 %collective-permute-done.8 = f32[32,128]{1,0:T(8,128)S(1)} collective-permute-done((f32[32,128]{1,0:T(8,128)S(1)}, f32[32,128]{1,0:T(8,128)S(1)}, u32[]{:S(2)}, u32[]{:S(2)}) %collective-permute-start.8) | collective-permute-done | bytes 16416 | tf_op jit(solution)/shard_map/ppermute | solution.py:254
  32.4 0.8 %collective-permute-done.7 = f32[32,128]{1,0:T(8,128)S(1)} collective-permute-done((f32[32,128]{1,0:T(8,128)S(1)}, f32[32,128]{1,0:T(8,128)S(1)}, u32[]{:S(2)}, u32[]{:S(2)}) %collective-permute-start.7) | collective-permute-done | bytes 16416 | tf_op jit(solution)/shard_map/ppermute | solution.py:254
  33.3 0.0 collective-permute-done.6
  33.3 3.1 %collective-permute-start.9 = (f32[32,128]{1,0:T(8,128)S(1)}, f32[32,128]{1,0:T(8,128)S(1)}, u32[]{:S(2)}, u32[]{:S(2)}) collective-permute-start(f32[32,128]{1,0:T(8,128)S(1)} %add_add_fusion), channel_id=1, source_target_pairs={{0,4},{1,5},{2,6},{3,7},{4,0},{5,1},{6,2},{7,3},{8,12},{9,13},{10,... | collective-permute-start | bytes 49160 | tf_op jit(solution)/shard_map/ppermute | solution.py:254
  36.4 1.5 %collective-permute-start.11 = (bf16[256,256]{1,0:T(8,128)(2,1)S(1)}, bf16[256,256]{1,0:T(8,128)(2,1)S(1)}, u32[]{:S(2)}, u32[]{:S(2)}) collective-permute-start(bf16[256,256]{1,0:T(8,128)(2,1)S(1)} %get-tuple-element.56), channel_id=1, source_target_pairs={{0,32},{16,48},{32,0},{48,16},{64,96},{80,112},{96,64},{112,80},{1... | collective-permute-start | bytes 393224 | tf_op jit(solution)/shard_map/ppermute | solution.py:269
  37.8 1.7 %collective-permute-start.12 = (bf16[256,256]{1,0:T(8,128)(2,1)S(1)}, bf16[256,256]{1,0:T(8,128)(2,1)S(1)}, u32[]{:S(2)}, u32[]{:S(2)}) collective-permute-start(bf16[256,256]{1,0:T(8,128)(2,1)S(1)} %get-tuple-element.57), channel_id=1, source_target_pairs={{0,16},{16,32},{32,48},{48,0},{64,80},{80,96},{96,112},{112,64},{1... | collective-permute-start | bytes 393224 | tf_op jit(solution)/shard_map/ppermute | solution.py:269
  39.6 0.0 collective-permute-done.9
  39.6 0.0 copy-start
  39.6 0.0 copy-start.1
  39.6 0.0 copy-start.2
  39.6 0.0 copy-start.3
  39.6 0.0 copy-start.4
  39.6 3.7 %collective-permute-start.10 = (f32[32,128]{1,0:T(8,128)S(1)}, f32[32,128]{1,0:T(8,128)S(1)}, u32[]{:S(2)}, u32[]{:S(2)}) collective-permute-start(f32[32,128]{1,0:T(8,128)S(1)} %add.30), channel_id=1, source_target_pairs={{0,12},{1,13},{2,14},{3,15},{4,8},{5,9},{6,10},{7,11},{8,4},{9,5},... | collective-permute-start | bytes 49160 | tf_op jit(solution)/shard_map/ppermute | solution.py:254
  43.4 1.7 %collective-permute-start.13 = (bf16[256,256]{1,0:T(8,128)(2,1)S(1)}, bf16[256,256]{1,0:T(8,128)(2,1)S(1)}, u32[]{:S(2)}, u32[]{:S(2)}) collective-permute-start(bf16[256,256]{1,0:T(8,128)(2,1)S(1)} %get-tuple-element.58), channel_id=1, source_target_pairs={{0,48},{16,0},{32,16},{48,32},{64,112},{80,64},{96,80},{112,96},{1... | collective-permute-start | bytes 393224 | tf_op jit(solution)/shard_map/ppermute | solution.py:269
  45.1 0.9 %shard_map.107.refs_0_ = f32[256,256]{1,0:T(8,128)S(1)} custom-call(bf16[4,160,256]{2,1,0:T(8,128)(2,1)S(1)} %all-to-all-done.recv_ref), custom_call_target="tpu_custom_call" | custom-call | flops 2000000000 | bytes 1048576 | tf_op jit(solution)/shard_map/pallas_call | solution.py:19
  46.0 0.0 collective-permute-done.10
  46.0 0.0 copy-done
  46.1 0.0 copy-done.1
  46.1 0.0 copy-done.2
  46.1 0.0 copy-done.3
  46.1 0.0 copy-done.4
  46.1 3.0 %shard_map.106 = bf16[16,128,256]{2,1,0:T(8,128)(2,1)S(1)} custom-call(f32[32,128]{1,0:T(8,128)S(1)} %add.31.slot_ref, f32[32,128]{1,0:T(8,128)S(1)} %bitcast.4, s32[2,32,128]{2,1,0:T(8,128)S(1)} %bitcast.5, bf16[128,1024]{1,0:T(8,128)(2,1)S(1)} %copy-done.1, bf16[2,1024,512]{2,1,0:T(8,128)(2,1)S(1)} %copy-done, bf16[128,256]{1,0:T(8,128)(2,1)S(1)} %copy-done.2), custom_call_target="tpu_custom_call" | custom-call | tf_op jit(solution)/shard_map/pallas_call | solution.py:19
  49.1 0.0 collective-permute-done.11.refs_1_
  49.2 0.0 collective-permute-done.12.refs_2_
  49.2 0.0 collective-permute-done.13.refs_3_
  49.2 17.5 %all_to_all.10.parts_ref = bf16[16,128,256]{2,1,0:T(8,128)(2,1)S(1)} all-to-all(bf16[16,128,256]{2,1,0:T(8,128)(2,1)S(1)} %shard_map.106), channel_id=1, replica_groups=mesh['dp'=16,'mem'=16] {'dp'}, dimensions={0} | all-to-all | bytes 2097152 | tf_op jit(solution)/shard_map/all_to_all | solution.py:353
  66.7 0.1 shard_map.108.own_ref
  66.8 5.1 %collective-permute-start.16 = (bf16[64,256]{1,0:T(8,128)(2,1)S(1)}, bf16[64,256]{1,0:T(8,128)(2,1)S(1)}, u32[]{:S(2)}, u32[]{:S(2)}) collective-permute-start(bf16[64,256]{1,0:T(8,128)(2,1)S(1)} %shard_map.108.own_ref), channel_id=1, source_target_pairs={{0,3},{1,2},{2,1},{3,0},{4,7},{5,6},{6,5},{7,4},{8,11},{9,10},{10,... | collective-permute-start | bytes 98312 | tf_op jit(solution)/shard_map/ppermute | solution.py:254
  71.8 0.7 collective-permute-start.15
  72.6 0.0 collective-permute-start.14
  72.6 0.8 shard_map.109
  73.3 0.7 shard_map.111
  74.0 0.0 collective-permute-done.16.three_ref
  74.0 1.1 %collective-permute-done.15.two_ref = bf16[64,256]{1,0:T(8,128)(2,1)S(1)} collective-permute-done((bf16[64,256]{1,0:T(8,128)(2,1)S(1)}, bf16[64,256]{1,0:T(8,128)(2,1)S(1)}, u32[]{:S(2)}, u32[]{:S(2)}) %collective-permute-start.15) | collective-permute-done | bytes 32800 | tf_op jit(solution)/shard_map/ppermute | solution.py:254
  75.1 0.0 collective-permute-done.14.one_ref
  75.1 0.7 shard_map.110
  (4 shorter events, 0.0 us)
Async XLA Ops:
  2.4 15.1 %all-to-all-start = ((bf16[4,160,256]{2,1,0:T(8,128)(2,1)}), bf16[4,160,256]{2,1,0:T(8,128)(2,1)S(1)}, u32[]{:S(2)}, u32[]{:S(2)}) async-start(bf16[4,160,256]{2,1,0:T(8,128)(2,1)} %shard_map.103), calls=%async_computation | async-start | bytes 655360 | tf_op jit(solution)/shard_map/all_to_all | solution.py:291
  7.4 5.5 %collective-permute-start.1 = (bf16[256,256]{1,0:T(8,128)(2,1)}, bf16[256,256]{1,0:T(8,128)(2,1)S(1)}, u32[]{:S(2)}, u32[]{:S(2)}) collective-permute-start(bf16[256,256]{1,0:T(8,128)(2,1)} %own_ref.1), channel_id=1, source_target_pairs={{0,32},{16,48},{32,0},{48,16},{64,96},{80,112},{96,64},{112,80},{1... | collective-permute-start | bytes 393224 | tf_op jit(solution)/shard_map/ppermute | solution.py:269
  10.2 7.4 %collective-permute-start = (bf16[256,256]{1,0:T(8,128)(2,1)}, bf16[256,256]{1,0:T(8,128)(2,1)S(1)}, u32[]{:S(2)}, u32[]{:S(2)}) collective-permute-start(bf16[256,256]{1,0:T(8,128)(2,1)} %own_ref.1), channel_id=1, source_target_pairs={{0,16},{16,32},{32,48},{48,0},{64,80},{80,96},{96,112},{112,64},{1... | collective-permute-start | bytes 393224 | tf_op jit(solution)/shard_map/ppermute | solution.py:269
  10.5 7.1 %collective-permute-start.2 = (bf16[256,256]{1,0:T(8,128)(2,1)}, bf16[256,256]{1,0:T(8,128)(2,1)S(1)}, u32[]{:S(2)}, u32[]{:S(2)}) collective-permute-start(bf16[256,256]{1,0:T(8,128)(2,1)} %own_ref.1), channel_id=1, source_target_pairs={{0,48},{16,0},{32,16},{48,32},{64,112},{80,64},{96,80},{112,96},{1... | collective-permute-start | bytes 393224 | tf_op jit(solution)/shard_map/ppermute | solution.py:269
  19.4 7.9 %collective-permute-start.3 = (f32[32,128]{1,0:T(8,128)S(1)}, f32[32,128]{1,0:T(8,128)S(1)}, u32[]{:S(2)}, u32[]{:S(2)}) collective-permute-start(f32[32,128]{1,0:T(8,128)S(1)} %get-tuple-element.41), channel_id=1, source_target_pairs={{0,64},{16,80},{32,96},{48,112},{64,128},{80,144},{96,160},{112,17... | collective-permute-start | bytes 49160 | tf_op jit(solution)/shard_map/ppermute | solution.py:274
  20.9 6.4 %collective-permute-start.4 = (f32[32,128]{1,0:T(8,128)S(1)}, f32[32,128]{1,0:T(8,128)S(1)}, u32[]{:S(2)}, u32[]{:S(2)}) collective-permute-start(f32[32,128]{1,0:T(8,128)S(1)} %get-tuple-element.42), channel_id=1, source_target_pairs={{0,128},{16,144},{32,160},{48,176},{64,192},{80,208},{96,224},{112... | collective-permute-start | bytes 49160 | tf_op jit(solution)/shard_map/ppermute | solution.py:274
  23.3 4.0 %collective-permute-start.5 = (f32[32,128]{1,0:T(8,128)S(1)}, f32[32,128]{1,0:T(8,128)S(1)}, u32[]{:S(2)}, u32[]{:S(2)}) collective-permute-start(f32[32,128]{1,0:T(8,128)S(1)} %get-tuple-element.43), channel_id=1, source_target_pairs={{0,192},{16,208},{32,224},{48,240},{64,0},{80,16},{96,32},{112,48}... | collective-permute-start | bytes 49160 | tf_op jit(solution)/shard_map/ppermute | solution.py:274
  27.3 5.1 %collective-permute-start.8 = (f32[32,128]{1,0:T(8,128)S(1)}, f32[32,128]{1,0:T(8,128)S(1)}, u32[]{:S(2)}, u32[]{:S(2)}) collective-permute-start(f32[32,128]{1,0:T(8,128)S(1)} %add_add_fusion.1), channel_id=1, source_target_pairs={{0,3},{1,2},{2,1},{3,0},{4,7},{5,6},{6,5},{7,4},{8,11},{9,10},{10,... | collective-permute-start | bytes 49160 | tf_op jit(solution)/shard_map/ppermute | solution.py:254
  30.7 2.6 %collective-permute-start.7 = (f32[32,128]{1,0:T(8,128)S(1)}, f32[32,128]{1,0:T(8,128)S(1)}, u32[]{:S(2)}, u32[]{:S(2)}) collective-permute-start(f32[32,128]{1,0:T(8,128)S(1)} %add_add_fusion.1), channel_id=1, source_target_pairs={{0,2},{1,3},{2,0},{3,1},{4,6},{5,7},{6,4},{7,5},{8,10},{9,11},{10,... | collective-permute-start | bytes 49160 | tf_op jit(solution)/shard_map/ppermute | solution.py:254
  30.9 2.4 %collective-permute-start.6 = (f32[32,128]{1,0:T(8,128)S(1)}, f32[32,128]{1,0:T(8,128)S(1)}, u32[]{:S(2)}, u32[]{:S(2)}) collective-permute-start(f32[32,128]{1,0:T(8,128)S(1)} %add_add_fusion.1), channel_id=1, source_target_pairs={{0,1},{1,0},{2,3},{3,2},{4,5},{5,4},{6,7},{7,6},{8,9},{9,8},{10,11... | collective-permute-start | bytes 49160 | tf_op jit(solution)/shard_map/ppermute | solution.py:254
  33.3 6.3 %collective-permute-start.9 = (f32[32,128]{1,0:T(8,128)S(1)}, f32[32,128]{1,0:T(8,128)S(1)}, u32[]{:S(2)}, u32[]{:S(2)}) collective-permute-start(f32[32,128]{1,0:T(8,128)S(1)} %add_add_fusion), channel_id=1, source_target_pairs={{0,4},{1,5},{2,6},{3,7},{4,0},{5,1},{6,2},{7,3},{8,12},{9,13},{10,... | collective-permute-start | bytes 49160 | tf_op jit(solution)/shard_map/ppermute | solution.py:254
  36.4 12.8 %collective-permute-start.11 = (bf16[256,256]{1,0:T(8,128)(2,1)S(1)}, bf16[256,256]{1,0:T(8,128)(2,1)S(1)}, u32[]{:S(2)}, u32[]{:S(2)}) collective-permute-start(bf16[256,256]{1,0:T(8,128)(2,1)S(1)} %get-tuple-element.56), channel_id=1, source_target_pairs={{0,32},{16,48},{32,0},{48,16},{64,96},{80,112},{96,64},{112,80},{1... | collective-permute-start | bytes 393224 | tf_op jit(solution)/shard_map/ppermute | solution.py:269
  37.8 11.3 %collective-permute-start.12 = (bf16[256,256]{1,0:T(8,128)(2,1)S(1)}, bf16[256,256]{1,0:T(8,128)(2,1)S(1)}, u32[]{:S(2)}, u32[]{:S(2)}) collective-permute-start(bf16[256,256]{1,0:T(8,128)(2,1)S(1)} %get-tuple-element.57), channel_id=1, source_target_pairs={{0,16},{16,32},{32,48},{48,0},{64,80},{80,96},{96,112},{112,64},{1... | collective-permute-start | bytes 393224 | tf_op jit(solution)/shard_map/ppermute | solution.py:269
  39.6 6.5 %copy-start = (bf16[2,1024,512]{2,1,0:T(8,128)(2,1)S(1)}, bf16[2,1024,512]{2,1,0:T(8,128)(2,1)}, u32[]{:S(2)}) copy-start(bf16[2,1024,512]{2,1,0:T(8,128)(2,1)} %keys_ref.1) | copy-start | bytes 6291460
  39.6 6.5 %copy-start.1 = (bf16[128,1024]{1,0:T(8,128)(2,1)S(1)}, bf16[128,1024]{1,0:T(8,128)(2,1)}, u32[]{:S(2)}) copy-start(bf16[128,1024]{1,0:T(8,128)(2,1)} %queries_ref.1) | copy-start | bytes 786436
  39.6 6.5 %copy-start.2 = (bf16[128,256]{1,0:T(8,128)(2,1)S(1)}, bf16[128,256]{1,0:T(8,128)(2,1)}, u32[]{:S(2)}) copy-start(bf16[128,256]{1,0:T(8,128)(2,1)} %layer_ref.1) | copy-start | bytes 196612
  39.6 6.5 %copy-start.3 = (f32[128,32]{0,1:T(8,128)S(1)}, f32[128,32]{0,1:T(8,128)}, u32[]{:S(2)}) copy-start(f32[128,32]{0,1:T(8,128)} %param.11) | copy-start | bytes 49156
  39.6 6.5 %copy-start.4 = (s32[2,128,32]{1,2,0:T(8,128)S(1)}, s32[2,128,32]{1,2,0:T(8,128)}, u32[]{:S(2)}) copy-start(s32[2,128,32]{1,2,0:T(8,128)} %param.12) | copy-start | bytes 98308
  39.6 6.4 %collective-permute-start.10 = (f32[32,128]{1,0:T(8,128)S(1)}, f32[32,128]{1,0:T(8,128)S(1)}, u32[]{:S(2)}, u32[]{:S(2)}) collective-permute-start(f32[32,128]{1,0:T(8,128)S(1)} %add.30), channel_id=1, source_target_pairs={{0,12},{1,13},{2,14},{3,15},{4,8},{5,9},{6,10},{7,11},{8,4},{9,5},... | collective-permute-start | bytes 49160 | tf_op jit(solution)/shard_map/ppermute | solution.py:254
  43.4 5.8 %collective-permute-start.13 = (bf16[256,256]{1,0:T(8,128)(2,1)S(1)}, bf16[256,256]{1,0:T(8,128)(2,1)S(1)}, u32[]{:S(2)}, u32[]{:S(2)}) collective-permute-start(bf16[256,256]{1,0:T(8,128)(2,1)S(1)} %get-tuple-element.58), channel_id=1, source_target_pairs={{0,48},{16,0},{32,16},{48,32},{64,112},{80,64},{96,80},{112,96},{1... | collective-permute-start | bytes 393224 | tf_op jit(solution)/shard_map/ppermute | solution.py:269
  66.8 7.3 %collective-permute-start.16 = (bf16[64,256]{1,0:T(8,128)(2,1)S(1)}, bf16[64,256]{1,0:T(8,128)(2,1)S(1)}, u32[]{:S(2)}, u32[]{:S(2)}) collective-permute-start(bf16[64,256]{1,0:T(8,128)(2,1)S(1)} %shard_map.108.own_ref), channel_id=1, source_target_pairs={{0,3},{1,2},{2,1},{3,0},{4,7},{5,6},{6,5},{7,4},{8,11},{9,10},{10,... | collective-permute-start | bytes 98312 | tf_op jit(solution)/shard_map/ppermute | solution.py:254
  71.8 3.3 %collective-permute-start.15 = (bf16[64,256]{1,0:T(8,128)(2,1)S(1)}, bf16[64,256]{1,0:T(8,128)(2,1)S(1)}, u32[]{:S(2)}, u32[]{:S(2)}) collective-permute-start(bf16[64,256]{1,0:T(8,128)(2,1)S(1)} %shard_map.108.own_ref), channel_id=1, source_target_pairs={{0,2},{1,3},{2,0},{3,1},{4,6},{5,7},{6,4},{7,5},{8,10},{9,11},{10,... | collective-permute-start | bytes 98312 | tf_op jit(solution)/shard_map/ppermute | solution.py:254
  72.6 2.5 %collective-permute-start.14 = (bf16[64,256]{1,0:T(8,128)(2,1)S(1)}, bf16[64,256]{1,0:T(8,128)(2,1)S(1)}, u32[]{:S(2)}, u32[]{:S(2)}) collective-permute-start(bf16[64,256]{1,0:T(8,128)(2,1)S(1)} %shard_map.108.own_ref), channel_id=1, source_target_pairs={{0,1},{1,0},{2,3},{3,2},{4,5},{5,4},{6,7},{7,6},{8,9},{9,8},{10,11... | collective-permute-start | bytes 98312 | tf_op jit(solution)/shard_map/ppermute | solution.py:254

commit v3 on v2

--- a/solution.py
+++ b/solution.py
@@ -37,24 +37,24 @@
     return ((ids & 127) + 128).astype(f32) * scale
 
 
-def pack_kernel(grad_ref, rows_ref, weights_ref, out_ref, ids_ref, wide_ref, sems):
+def pack_kernel(
+    grad_ref, rows_ref, weights_ref, values_ref, out_ref, values_out_ref, ids_ref, wide_ref, sems
+):
     tokens = grad_ref.shape[0]
     copies = [
         pltpu.make_async_copy(rows_ref, ids_ref, sems.at[0]),
         pltpu.make_async_copy(weights_ref, wide_ref, sems.at[1]),
+        pltpu.make_async_copy(grad_ref, out_ref.at[pl.ds(0, tokens), :], sems.at[2]),
+        pltpu.make_async_copy(values_ref, values_out_ref, sems.at[3]),
     ]
-    for at in range(out_ref.shape[0]):
-        here = out_ref.at[at, pl.ds(0, tokens), :]
-        copies.append(pltpu.make_async_copy(grad_ref, here, sems.at[2 + at]))
     for copy in copies:
         copy.start()
     copies[0].wait()
     copies[1].wait()
-    both = jnp.concatenate([row_codes(ids_ref[...]), wide_ref[...]], axis=1).astype(bf16)
-    for at in range(out_ref.shape[0]):
-        out_ref[at, tokens:, :] = both
-    for copy in copies[2:]:
-        copy.wait()
+    both = jnp.concatenate([row_codes(ids_ref[...]), wide_ref[...]], axis=1)
+    out_ref[tokens:, :] = both.astype(bf16)
+    copies[2].wait()
+    copies[3].wait()
 
 
 def power_of(base, exponent, bits):
@@ -76,57 +76,49 @@
     return jnp.where(inside, local + moved.astype(jnp.int32), -1)
 
 
-def slot_kernel(recv_ref, own_ref, *refs):
-    values_refs, out_refs, (own_here_ref, sem) = refs[: SIDE - 1], refs[SIDE - 1 : -2], refs[-2:]
+def slot_kernel(*refs):
+    block_refs, values_refs, out_refs = refs[:SIDE], refs[SIDE : 2 * SIDE], refs[2 * SIDE :]
     slots, tokens = out_refs[0].shape
-    val_rows = own_ref.shape[0]
-    owner = lax.axis_index("dp")
-    row, column = owner // SIDE, owner % SIDE
-    fetch = pltpu.make_async_copy(own_ref, own_here_ref, sem)
-    fetch.start()
-    blocks = [(row + away) % SIDE for away in range(SIDE)]
-    local = [group_rows(recv_ref[at, tokens:, :tokens]) for at in blocks]
-    accs = [[jnp.zeros((8, tokens), f32) for _ in range(slots // 8)] for _ in blocks]
-    for shift in range(SIDE - 1, -1, -1):
-        if shift == 0:
-            fetch.wait()
-        values_ref = values_refs[shift - 1] if shift else own_here_ref
-        first = ((column + SIDE - shift) % SIDE) * (val_rows // 8)
-        for away, at in enumerate(blocks):
+    val_rows = values_refs[0].shape[0]
+    column = lax.axis_index("dp") % SIDE
+    for back, block_ref in enumerate(block_refs):
+        local = group_rows(block_ref[tokens:, :tokens])
+        accs = [jnp.zeros((8, tokens), f32) for _ in range(slots // 8)]
+        for shift, values_ref in enumerate(values_refs):
             score = lax.dot_general(
                 values_ref[...],
-                recv_ref[at, :tokens, :],
+                block_ref[:tokens, :],
                 (((1,), (1,)), ((), ())),
                 preferred_element_type=f32,
             )
+            first = ((column + SIDE - shift) % SIDE) * (val_rows // 8)
             for part in range(slots // 8):
-                rows = local[away][part * 8 : part * 8 + 8]
+                rows = local[part * 8 : part * 8 + 8]
                 low, high = rows & 7, (rows >> 3) - first
                 for tile in range(val_rows // 8):
                     got = jnp.take_along_axis(score[tile * 8 : tile * 8 + 8], low, axis=0)
-                    accs[away][part] = jnp.where(high == tile, got, accs[away][part])
-    for away, out_ref in enumerate(out_refs):
+                    accs[part] = jnp.where(high == tile, got, accs[part])
         for part in range(slots // 8):
-            out_ref[part * 8 : part * 8 + 8, :] = accs[away][part]
+            out_refs[(SIDE - back) % SIDE][part * 8 : part * 8 + 8, :] = accs[part]
 
 
 def wide_row(ref, at):
     return jnp.broadcast_to(ref[at, :][None, :], (16, ref.shape[1])).astype(bf16)
 
 
-def value_kernel(shifts, recv_ref, *refs):
-    out_refs, (rows_ref, wide_ref, bag_ref, grads_ref) = refs[:-4], refs[-4:]
-    blocks = recv_ref.shape[0]
+def value_kernel(shifts, *refs):
+    block_refs, out_refs = refs[:SIDE], refs[SIDE:-4]
+    rows_ref, wide_ref, bag_ref, grads_ref = refs[-4:]
     val_rows = out_refs[0].shape[0]
     slots, tokens = rows_ref.shape[1:]
     tiles = val_rows // 16
     owner = lax.axis_index("dp")
     row, column = owner // SIDE, owner % SIDE
     base = row_codes(lax.broadcasted_iota(jnp.int32, (val_rows, tokens), 0))
-    for at in range(blocks):
-        rows_ref[at] = recv_ref[at, tokens:, :tokens].astype(f32)
-        wide_ref[at] = recv_ref[at, tokens:, tokens:].astype(f32)
-        grads_ref[at * tokens : at * tokens + tokens, :] = recv_ref[at, :tokens, :]
+    for at, block_ref in enumerate(block_refs):
+        rows_ref[at] = block_ref[tokens:, :tokens].astype(f32)
+        wide_ref[at] = block_ref[tokens:, tokens:].astype(f32)
+        grads_ref[at * tokens : at * tokens + tokens, :] = block_ref[:tokens, :]
     for shift, out_ref in zip(shifts, out_refs):
         holder = row * SIDE + (column + shift) % SIDE
         codes = (base * power_of(4.0, holder, 4)).astype(bf16)
@@ -143,7 +135,7 @@
                 bag_ref[tile * 16 : tile * 16 + 16, span] = bags[tile]
             return carry
 
-        lax.fori_loop(0, blocks, one, 0)
+        lax.fori_loop(0, SIDE, one, 0)
         total = jnp.dot(bag_ref[...], grads_ref[...], preferred_element_type=f32)
         out_ref[...] = total.astype(out_ref.dtype)
 
@@ -273,28 +265,26 @@
     def along_y(x, shift):
         return lax.ppermute(x, "dp", [(at, (at + shift * SIDE) % groups) for at in range(groups)])
 
-    columns = [[row * SIDE + column for row in range(SIDE)] for column in range(SIDE)]
-
     far_values = along_x(values, 2)
-    near_values = [along_x(values, 1), far_values, along_x(values, 3)]
-    sent = run(
+    sent, own_values = run(
         pack_kernel,
-        shape((SIDE, tokens + slots, width), bf16),
-        [stay(x) for x in (grad_out, rows_t, weights_t)],
+        [shape((tokens + slots, width), bf16), shape(values.shape, bf16)],
+        [stay(x) for x in (grad_out, rows_t, weights_t, values)],
         scratch=(
             pltpu.VMEM((slots, tokens), jnp.int32),
             pltpu.VMEM((slots, tokens), f32),
-            pltpu.SemaphoreType.DMA((2 + SIDE,)),
+            pltpu.SemaphoreType.DMA((4,)),
         ),
-        far=(0, 1, 2),
-    )
-    recv = lax.all_to_all(sent, "dp", 0, 0, tiled=True, axis_index_groups=columns)
+        far=(0, 1, 2, 3),
+    )
+    recv = [sent] + [along_y(sent, shift) for shift in (1, 2, 3)]
+    all_values = [own_values, along_x(values, 1), far_values, along_x(values, 3)]
 
     def value_part(shifts, recv):
         return run(
             functools.partial(value_kernel, shifts),
             [shape((val_rows, width), bf16 if shift else f32) for shift in shifts],
-            (recv,),
+            recv,
             scratch=(
                 pltpu.VMEM((SIDE, slots, tokens), f32),
                 pltpu.VMEM((SIDE, slots, tokens), f32),
@@ -308,17 +298,15 @@
     slot_parts = run(
         slot_kernel,
         [shape((slots, tokens), f32)] * SIDE,
-        (recv, stay(values), *near_values),
-        scratch=(pltpu.VMEM((val_rows, width), bf16), pltpu.SemaphoreType.DMA(())),
+        (*recv, *all_values),
         flops=10**9,
         data=2**20,
-        far=(1,),
-    )
-    *slot_parts, recv = lax.optimization_barrier((*slot_parts, recv))
+    )
+    slot_parts, recv = lax.optimization_barrier((slot_parts, recv))
     back = [along_y(slot_parts[shift], shift) for shift in (1, 2, 3)]
     aways = value_part((2, 1, 3), recv)
     slot_grad = (slot_parts[0] + back[0]) + (back[1] + back[2])
-    slot_grad, recv, *aways = lax.optimization_barrier((slot_grad, recv, *aways))
+    slot_grad, recv, aways = lax.optimization_barrier((slot_grad, recv, aways))
     two_away, one_away, three_away = aways
 
     one, two, three = (swap(slot_grad, mask, mem_count) for mask in (1, 2, 3))

time: 76.1 us -> 72.5 us (0.953)
  starting transfers between devices: 37 us -> 34 us
  Pallas kernels: 12.6 us -> 11.1 us
    all_to_all x1 -> x0, starting transfers between devices: 5.01 us -> none  [step_body(): lax.all_to_all(sent, 'dp', 0, 0, tiled=True, axis_index_groups=columns)]
    ppermute x3 -> x6, waiting for transfers between devices: 0.01 us -> 4.93 us  [along_y(): lax.ppermute(x, 'dp', [(at, (at + shift * SIDE) % groups) for at in range...]
    ppermute x6, waiting for transfers between devices: 4.7 us -> 0.02 us  [along_x(): lax.ppermute(x, 'dp', [(at, at // SIDE * SIDE + (at + shift) % SIDE) for...]
    ppermute x6, starting transfers between devices: 10.3 us -> 7.46 us  [along_x(): lax.ppermute(x, 'dp', [(at, at // SIDE * SIDE + (at + shift) % SIDE) for...]
    ppermute x8, starting transfers between devices: 16.5 us -> 19.1 us  [swap(): return lax.ppermute(x, 'mem', [(at, at ^ mask) for at in range(count)])]
    ppermute x3 -> x6, starting transfers between devices: 5.13 us -> 7.42 us  [along_y(): lax.ppermute(x, 'dp', [(at, (at + shift * SIDE) % groups) for at in range...]
    pallas_call x9, Pallas kernels: 12.6 us -> 11.1 us  [run(): pl.pallas_call(kernel, out_shape=outs, in_specs=[FAR if at in far else VM...]
  transfers between devices with their start and end apart: 18 -> 20, of which waited for: 5 -> 6; matrix products, arithmetic and copies ran while one was open for 0% -> 0% of each run, Pallas kernels for 11% -> 11%
where the time goes in v3:
time: 72.5 us; the launch traced here: 72.3 us
  starting transfers between devices  34 us (47%)
  blocking collectives  18 us (25%)
  Pallas kernels  11.1 us (15%)
  waiting for transfers between devices  8.29 us (11%)
  between operations  0.84 us (1%)
    ppermute x8, starting transfers between devices, swap(): return lax.ppermute(x, 'mem', [(at, at ^ mask) for at in range(count)])  19.1 us
    all_to_all x1, blocking collectives, step_body(): parts = lax.all_to_all(parts, 'dp', 0, 0, tiled=True)  18 us
    pallas_call x9, Pallas kernels, run(): pl.pallas_call(kernel, out_shape=outs, in_specs=[FAR if at in far else VM...  11.1 us
    ppermute x6, starting transfers between devices, along_x(): lax.ppermute(x, 'dp', [(at, at // SIDE * SIDE + (at + shift) % SIDE) for...  7.46 us
    ppermute x6, starting transfers between devices, along_y(): lax.ppermute(x, 'dp', [(at, (at + shift * SIDE) % groups) for at in range...  7.42 us
    ppermute x6, waiting for transfers between devices, along_y(): lax.ppermute(x, 'dp', [(at, (at + shift * SIDE) % groups) for at in range...  4.93 us
    ppermute x8, waiting for transfers between devices, swap(): return lax.ppermute(x, 'mem', [(at, at ^ mask) for at in range(count)])  3.35 us
  transfers between devices with their start and end apart: 20, of which 6 were waited for; matrix products, arithmetic and copies ran while one was open for 0% of the time, Pallas kernels for 11%

profile of v3, /device:TPU:1, one launch (start us, length us, event | category | flops | bytes accessed | tf_op | source)
XLA Modules:
  0.0 72.3 jit_solution(9951600427770714872)
XLA Ops:
  0.6 1.0 %shard_map.103 = (bf16[160,256]{1,0:T(8,128)(2,1)S(1)}, bf16[256,256]{1,0:T(8,128)(2,1)S(1)}) custom-call(bf16[128,256]{1,0:T(8,128)(2,1)} %grad_ref.1, s32[32,128]{1,0:T(8,128)} %bitcast.6, f32[32,128]{1,0:T(8,128)} %bitcast.3, bf16[256,256]{1,0:T(8,128)(2,1)} %values_ref.1), custom_call_target="tpu_custom_call" | custom-call | tf_op jit(solution)/shard_map/pallas_call | solution.py:19
  1.6 3.6 %collective-permute-start.2 = (bf16[160,256]{1,0:T(8,128)(2,1)S(1)}, bf16[160,256]{1,0:T(8,128)(2,1)S(1)}, u32[]{:S(2)}, u32[]{:S(2)}) collective-permute-start(bf16[160,256]{1,0:T(8,128)(2,1)S(1)} %get-tuple-element.74.refs_0_), channel_id=1, source_target_pairs={{0,192},{16,208},{32,224},{48,240},{64,0},{80,16},{96,32},{112,48}... | collective-permute-start | bytes 245768 | tf_op jit(solution)/shard_map/ppermute | solution.py:266
  5.3 1.2 %collective-permute-start.3 = (bf16[256,256]{1,0:T(8,128)(2,1)}, bf16[256,256]{1,0:T(8,128)(2,1)S(1)}, u32[]{:S(2)}, u32[]{:S(2)}) collective-permute-start(bf16[256,256]{1,0:T(8,128)(2,1)} %values_ref.1), channel_id=1, source_target_pairs={{0,16},{16,32},{32,48},{48,0},{64,80},{80,96},{96,112},{112,64},{1... | collective-permute-start | bytes 393224 | tf_op jit(solution)/shard_map/ppermute | solution.py:261
  6.5 1.5 %collective-permute-start.5 = (bf16[256,256]{1,0:T(8,128)(2,1)}, bf16[256,256]{1,0:T(8,128)(2,1)S(1)}, u32[]{:S(2)}, u32[]{:S(2)}) collective-permute-start(bf16[256,256]{1,0:T(8,128)(2,1)} %values_ref.1), channel_id=1, source_target_pairs={{0,48},{16,0},{32,16},{48,32},{64,112},{80,64},{96,80},{112,96},{1... | collective-permute-start | bytes 393224 | tf_op jit(solution)/shard_map/ppermute | solution.py:261
  8.0 1.5 %collective-permute-start.4 = (bf16[256,256]{1,0:T(8,128)(2,1)}, bf16[256,256]{1,0:T(8,128)(2,1)S(1)}, u32[]{:S(2)}, u32[]{:S(2)}) collective-permute-start(bf16[256,256]{1,0:T(8,128)(2,1)} %values_ref.1), channel_id=1, source_target_pairs={{0,32},{16,48},{32,0},{48,16},{64,96},{80,112},{96,64},{112,80},{1... | collective-permute-start | bytes 393224 | tf_op jit(solution)/shard_map/ppermute | solution.py:261
  9.5 0.3 collective-permute-start.1
  9.8 0.0 collective-permute-done.2.refs_3_
  9.8 0.7 collective-permute-start
  10.5 4.0 %collective-permute-done.1.refs_2_ = bf16[160,256]{1,0:T(8,128)(2,1)S(1)} collective-permute-done((bf16[160,256]{1,0:T(8,128)(2,1)S(1)}, bf16[160,256]{1,0:T(8,128)(2,1)S(1)}, u32[]{:S(2)}, u32[]{:S(2)}) %collective-permute-start.1) | collective-permute-done | bytes 81952 | tf_op jit(solution)/shard_map/ppermute | solution.py:266
  14.6 0.9 %collective-permute-done.refs_1_ = bf16[160,256]{1,0:T(8,128)(2,1)S(1)} collective-permute-done((bf16[160,256]{1,0:T(8,128)(2,1)S(1)}, bf16[160,256]{1,0:T(8,128)(2,1)S(1)}, u32[]{:S(2)}, u32[]{:S(2)}) %collective-permute-start) | collective-permute-done | bytes 81952 | tf_op jit(solution)/shard_map/ppermute | solution.py:266
  15.5 0.0 collective-permute-done.3.refs_5_
  15.5 0.0 collective-permute-done.5.refs_7_
  15.5 0.0 collective-permute-done.4.refs_6_
  15.5 1.1 %shard_map.104 = (f32[32,128]{1,0:T(8,128)S(1)}, f32[32,128]{1,0:T(8,128)S(1)}, f32[32,128]{1,0:T(8,128)S(1)}, f32[32,128]{1,0:T(8,128)S(1)}) custom-call(bf16[160,256]{1,0:T(8,128)(2,1)S(1)} %get-tuple-element.74.refs_0_, bf16[160,256]{1,0:T(8,128)(2,1)S(1)} %collective-permute-done.refs_1_, bf16[160,256]{1,0:T(8,128)(2,1)S(1)} %collective-permute-done.1.refs_2_, ...), custom_call_target="tpu_custom_call" | custom-call | flops 1000000000 | bytes 1048576 | tf_op jit(solution)/shard_map/pallas_call | solution.py:19
  16.6 0.1 collective-permute-start.6
  16.7 1.5 %collective-permute-start.7 = (f32[32,128]{1,0:T(8,128)S(1)}, f32[32,128]{1,0:T(8,128)S(1)}, u32[]{:S(2)}, u32[]{:S(2)}) collective-permute-start(f32[32,128]{1,0:T(8,128)S(1)} %get-tuple-element.55), channel_id=1, source_target_pairs={{0,128},{16,144},{32,160},{48,176},{64,192},{80,208},{96,224},{112... | collective-permute-start | bytes 49160 | tf_op jit(solution)/shard_map/ppermute | solution.py:266
  18.1 1.2 %collective-permute-start.8 = (f32[32,128]{1,0:T(8,128)S(1)}, f32[32,128]{1,0:T(8,128)S(1)}, u32[]{:S(2)}, u32[]{:S(2)}) collective-permute-start(f32[32,128]{1,0:T(8,128)S(1)} %get-tuple-element.56), channel_id=1, source_target_pairs={{0,192},{16,208},{32,224},{48,240},{64,0},{80,16},{96,32},{112,48}... | collective-permute-start | bytes 49160 | tf_op jit(solution)/shard_map/ppermute | solution.py:266
  19.4 2.8 %shard_map.105 = (bf16[256,256]{1,0:T(8,128)(2,1)S(1)}, bf16[256,256]{1,0:T(8,128)(2,1)S(1)}, bf16[256,256]{1,0:T(8,128)(2,1)S(1)}) custom-call(bf16[160,256]{1,0:T(8,128)(2,1)S(1)} %get-tuple-element.74.refs_0_, bf16[160,256]{1,0:T(8,128)(2,1)S(1)} %collective-permute-done.refs_1_, bf16[160,256]{1,0:T(8,128)(2,1)S(1)} %collective-permute-done.1.refs_2_, ...), custom_call_target="tpu_custom_call" | custom-call | flops 2000000000 | bytes 1048576 | tf_op jit(solution)/shard_map/pallas_call | solution.py:19
  22.1 0.0 collective-permute-done.6
  22.1 0.0 collective-permute-done.7
  22.1 0.0 collective-permute-done.8
  22.2 5.4 %collective-permute-start.11 = (f32[32,128]{1,0:T(8,128)S(1)}, f32[32,128]{1,0:T(8,128)S(1)}, u32[]{:S(2)}, u32[]{:S(2)}) collective-permute-start(f32[32,128]{1,0:T(8,128)S(1)} %add_add_fusion.1), channel_id=1, source_target_pairs={{0,3},{1,2},{2,1},{3,0},{4,7},{5,6},{6,5},{7,4},{8,11},{9,10},{10,... | collective-permute-start | bytes 49160 | tf_op jit(solution)/shard_map/ppermute | solution.py:246
  27.5 0.0 collective-permute-start.10
  27.5 0.5 collective-permute-start.9
  28.0 0.9 %collective-permute-done.11 = f32[32,128]{1,0:T(8,128)S(1)} collective-permute-done((f32[32,128]{1,0:T(8,128)S(1)}, f32[32,128]{1,0:T(8,128)S(1)}, u32[]{:S(2)}, u32[]{:S(2)}) %collective-permute-start.11) | collective-permute-done | bytes 16416 | tf_op jit(solution)/shard_map/ppermute | solution.py:246
  29.0 1.2 %collective-permute-done.10 = f32[32,128]{1,0:T(8,128)S(1)} collective-permute-done((f32[32,128]{1,0:T(8,128)S(1)}, f32[32,128]{1,0:T(8,128)S(1)}, u32[]{:S(2)}, u32[]{:S(2)}) %collective-permute-start.10) | collective-permute-done | bytes 16416 | tf_op jit(solution)/shard_map/ppermute | solution.py:246
  30.1 0.0 collective-permute-done.9
  30.1 3.1 %collective-permute-start.12 = (f32[32,128]{1,0:T(8,128)S(1)}, f32[32,128]{1,0:T(8,128)S(1)}, u32[]{:S(2)}, u32[]{:S(2)}) collective-permute-start(f32[32,128]{1,0:T(8,128)S(1)} %add_add_fusion), channel_id=1, source_target_pairs={{0,4},{1,5},{2,6},{3,7},{4,0},{5,1},{6,2},{7,3},{8,12},{9,13},{10,... | collective-permute-start | bytes 49160 | tf_op jit(solution)/shard_map/ppermute | solution.py:246
  33.2 1.4 %collective-permute-start.14 = (bf16[256,256]{1,0:T(8,128)(2,1)S(1)}, bf16[256,256]{1,0:T(8,128)(2,1)S(1)}, u32[]{:S(2)}, u32[]{:S(2)}) collective-permute-start(bf16[256,256]{1,0:T(8,128)(2,1)S(1)} %get-tuple-element.78), channel_id=1, source_target_pairs={{0,32},{16,48},{32,0},{48,16},{64,96},{80,112},{96,64},{112,80},{1... | collective-permute-start | bytes 393224 | tf_op jit(solution)/shard_map/ppermute | solution.py:261
  34.7 0.0 collective-permute-start.15
  34.7 0.2 collective-permute-done.12
  34.8 0.0 copy-start
  34.8 0.0 copy-start.1
  34.8 0.0 copy-start.2
  34.8 0.0 copy-start.3
  34.8 0.0 copy-start.4
  34.9 4.6 %collective-permute-start.13 = (f32[32,128]{1,0:T(8,128)S(1)}, f32[32,128]{1,0:T(8,128)S(1)}, u32[]{:S(2)}, u32[]{:S(2)}) collective-permute-start(f32[32,128]{1,0:T(8,128)S(1)} %add.30), channel_id=1, source_target_pairs={{0,12},{1,13},{2,14},{3,15},{4,8},{5,9},{6,10},{7,11},{8,4},{9,5},... | collective-permute-start | bytes 49160 | tf_op jit(solution)/shard_map/ppermute | solution.py:246
  39.5 1.8 %collective-permute-start.16 = (bf16[256,256]{1,0:T(8,128)(2,1)S(1)}, bf16[256,256]{1,0:T(8,128)(2,1)S(1)}, u32[]{:S(2)}, u32[]{:S(2)}) collective-permute-start(bf16[256,256]{1,0:T(8,128)(2,1)S(1)} %get-tuple-element.80), channel_id=1, source_target_pairs={{0,48},{16,0},{32,16},{48,32},{64,112},{80,64},{96,80},{112,96},{1... | collective-permute-start | bytes 393224 | tf_op jit(solution)/shard_map/ppermute | solution.py:261
  41.3 0.9 %shard_map.107.refs_0_ = f32[256,256]{1,0:T(8,128)S(1)} custom-call(bf16[160,256]{1,0:T(8,128)(2,1)S(1)} %get-tuple-element.74.refs_0_, bf16[160,256]{1,0:T(8,128)(2,1)S(1)} %collective-permute-done.refs_1_, bf16[160,256]{1,0:T(8,128)(2,1)S(1)} %collective-permute-done.1.refs_2_, bf16[160,256]{1,0:T(8,128)(2,1)S(1)} %collective-permute-done.2.refs_3_), custom_call_target="tpu_custom_call" | custom-call | flops 2000000000 | bytes 1048576 | tf_op jit(solution)/shard_map/pallas_call | solution.py:19
  42.3 0.0 collective-permute-done.13
  42.3 0.0 copy-done
  42.3 0.0 copy-done.1
  42.3 0.0 copy-done.2
  42.3 0.0 copy-done.3
  42.3 0.0 copy-done.4
  42.3 3.0 %shard_map.106 = bf16[16,128,256]{2,1,0:T(8,128)(2,1)S(1)} custom-call(f32[32,128]{1,0:T(8,128)S(1)} %add.31.slot_ref, f32[32,128]{1,0:T(8,128)S(1)} %bitcast.4, s32[2,32,128]{2,1,0:T(8,128)S(1)} %bitcast.5, bf16[128,1024]{1,0:T(8,128)(2,1)S(1)} %copy-done.1, bf16[2,1024,512]{2,1,0:T(8,128)(2,1)S(1)} %copy-done, bf16[128,256]{1,0:T(8,128)(2,1)S(1)} %copy-done.2), custom_call_target="tpu_custom_call" | custom-call | tf_op jit(solution)/shard_map/pallas_call | solution.py:19
  45.4 0.0 collective-permute-done.14.refs_1_
  45.4 0.0 collective-permute-done.15.refs_2_
  45.4 0.0 collective-permute-done.16.refs_3_
  45.4 18.0 %all_to_all.5.parts_ref = bf16[16,128,256]{2,1,0:T(8,128)(2,1)S(1)} all-to-all(bf16[16,128,256]{2,1,0:T(8,128)(2,1)S(1)} %shard_map.106), channel_id=1, replica_groups=mesh['dp'=16,'mem'=16] {'dp'}, dimensions={0} | all-to-all | bytes 2097152 | tf_op jit(solution)/shard_map/all_to_all | solution.py:341
  63.4 0.1 shard_map.108.own_ref
  63.5 4.8 %collective-permute-start.19 = (bf16[64,256]{1,0:T(8,128)(2,1)S(1)}, bf16[64,256]{1,0:T(8,128)(2,1)S(1)}, u32[]{:S(2)}, u32[]{:S(2)}) collective-permute-start(bf16[64,256]{1,0:T(8,128)(2,1)S(1)} %shard_map.108.own_ref), channel_id=1, source_target_pairs={{0,3},{1,2},{2,1},{3,0},{4,7},{5,6},{6,5},{7,4},{8,11},{9,10},{10,... | collective-permute-start | bytes 98312 | tf_op jit(solution)/shard_map/ppermute | solution.py:246
  68.3 0.7 %collective-permute-start.18 = (bf16[64,256]{1,0:T(8,128)(2,1)S(1)}, bf16[64,256]{1,0:T(8,128)(2,1)S(1)}, u32[]{:S(2)}, u32[]{:S(2)}) collective-permute-start(bf16[64,256]{1,0:T(8,128)(2,1)S(1)} %shard_map.108.own_ref), channel_id=1, source_target_pairs={{0,2},{1,3},{2,0},{3,1},{4,6},{5,7},{6,4},{7,5},{8,10},{9,11},{10,... | collective-permute-start | bytes 98312 | tf_op jit(solution)/shard_map/ppermute | solution.py:246
  69.0 0.0 collective-permute-start.17
  69.0 0.8 %shard_map.109 = f32[256,256]{1,0:T(8,128)} custom-call(f32[256,256]{1,0:T(8,128)S(1)} %shard_map.107.refs_0_, bf16[256,256]{1,0:T(8,128)(2,1)S(1)} %collective-permute-done.14.refs_1_, bf16[256,256]{1,0:T(8,128)(2,1)S(1)} %collective-permute-done.15.refs_2_, bf16[256,256]{1,0:T(8,128)(2,1)S(1)} %collective-permute-done.16.refs_3_), custom_call_target="tpu_custom_call" | custom-call | flops 1000000000 | bytes 524288 | tf_op jit(solution)/shard_map/pallas_call | solution.py:19
  69.8 0.7 shard_map.111
  70.5 0.0 collective-permute-done.19.three_ref
  70.5 1.1 %collective-permute-done.18.two_ref = bf16[64,256]{1,0:T(8,128)(2,1)S(1)} collective-permute-done((bf16[64,256]{1,0:T(8,128)(2,1)S(1)}, bf16[64,256]{1,0:T(8,128)(2,1)S(1)}, u32[]{:S(2)}, u32[]{:S(2)}) %collective-permute-start.18) | collective-permute-done | bytes 32800 | tf_op jit(solution)/shard_map/ppermute | solution.py:246
  71.6 0.0 collective-permute-done.17.one_ref
  71.6 0.7 %shard_map.110 = f32[2,64,512]{2,1,0:T(8,128)} custom-call(bf16[64,256]{1,0:T(8,128)(2,1)S(1)} %shard_map.108.own_ref, bf16[64,256]{1,0:T(8,128)(2,1)S(1)} %collective-permute-done.17.one_ref, bf16[64,256]{1,0:T(8,128)(2,1)S(1)} %collective-permute-done.18.two_ref, bf16[64,256]{1,0:T(8,128)(2,1)S(1)} %collective-permute-done.19.three_ref), custom_call_target="tpu_custom_call" | custom-call | tf_op jit(solution)/shard_map/pallas_call | solution.py:19
  (4 shorter events, 0.0 us)
Async XLA Ops:
  1.6 8.2 %collective-permute-start.2 = (bf16[160,256]{1,0:T(8,128)(2,1)S(1)}, bf16[160,256]{1,0:T(8,128)(2,1)S(1)}, u32[]{:S(2)}, u32[]{:S(2)}) collective-permute-start(bf16[160,256]{1,0:T(8,128)(2,1)S(1)} %get-tuple-element.74.refs_0_), channel_id=1, source_target_pairs={{0,192},{16,208},{32,224},{48,240},{64,0},{80,16},{96,32},{112,48}... | collective-permute-start | bytes 245768 | tf_op jit(solution)/shard_map/ppermute | solution.py:266
  5.3 10.2 %collective-permute-start.3 = (bf16[256,256]{1,0:T(8,128)(2,1)}, bf16[256,256]{1,0:T(8,128)(2,1)S(1)}, u32[]{:S(2)}, u32[]{:S(2)}) collective-permute-start(bf16[256,256]{1,0:T(8,128)(2,1)} %values_ref.1), channel_id=1, source_target_pairs={{0,16},{16,32},{32,48},{48,0},{64,80},{80,96},{96,112},{112,64},{1... | collective-permute-start | bytes 393224 | tf_op jit(solution)/shard_map/ppermute | solution.py:261
  6.5 9.0 %collective-permute-start.5 = (bf16[256,256]{1,0:T(8,128)(2,1)}, bf16[256,256]{1,0:T(8,128)(2,1)S(1)}, u32[]{:S(2)}, u32[]{:S(2)}) collective-permute-start(bf16[256,256]{1,0:T(8,128)(2,1)} %values_ref.1), channel_id=1, source_target_pairs={{0,48},{16,0},{32,16},{48,32},{64,112},{80,64},{96,80},{112,96},{1... | collective-permute-start | bytes 393224 | tf_op jit(solution)/shard_map/ppermute | solution.py:261
  8.0 7.5 %collective-permute-start.4 = (bf16[256,256]{1,0:T(8,128)(2,1)}, bf16[256,256]{1,0:T(8,128)(2,1)S(1)}, u32[]{:S(2)}, u32[]{:S(2)}) collective-permute-start(bf16[256,256]{1,0:T(8,128)(2,1)} %values_ref.1), channel_id=1, source_target_pairs={{0,32},{16,48},{32,0},{48,16},{64,96},{80,112},{96,64},{112,80},{1... | collective-permute-start | bytes 393224 | tf_op jit(solution)/shard_map/ppermute | solution.py:261
  9.5 5.1 %collective-permute-start.1 = (bf16[160,256]{1,0:T(8,128)(2,1)S(1)}, bf16[160,256]{1,0:T(8,128)(2,1)S(1)}, u32[]{:S(2)}, u32[]{:S(2)}) collective-permute-start(bf16[160,256]{1,0:T(8,128)(2,1)S(1)} %get-tuple-element.74.refs_0_), channel_id=1, source_target_pairs={{0,128},{16,144},{32,160},{48,176},{64,192},{80,208},{96,224},{112... | collective-permute-start | bytes 245768 | tf_op jit(solution)/shard_map/ppermute | solution.py:266
  9.8 5.6 %collective-permute-start = (bf16[160,256]{1,0:T(8,128)(2,1)S(1)}, bf16[160,256]{1,0:T(8,128)(2,1)S(1)}, u32[]{:S(2)}, u32[]{:S(2)}) collective-permute-start(bf16[160,256]{1,0:T(8,128)(2,1)S(1)} %get-tuple-element.74.refs_0_), channel_id=1, source_target_pairs={{0,64},{16,80},{32,96},{48,112},{64,128},{80,144},{96,160},{112,17... | collective-permute-start | bytes 245768 | tf_op jit(solution)/shard_map/ppermute | solution.py:266
  16.6 5.5 %collective-permute-start.6 = (f32[32,128]{1,0:T(8,128)S(1)}, f32[32,128]{1,0:T(8,128)S(1)}, u32[]{:S(2)}, u32[]{:S(2)}) collective-permute-start(f32[32,128]{1,0:T(8,128)S(1)} %get-tuple-element.54), channel_id=1, source_target_pairs={{0,64},{16,80},{32,96},{48,112},{64,128},{80,144},{96,160},{112,17... | collective-permute-start | bytes 49160 | tf_op jit(solution)/shard_map/ppermute | solution.py:266
  16.7 5.5 %collective-permute-start.7 = (f32[32,128]{1,0:T(8,128)S(1)}, f32[32,128]{1,0:T(8,128)S(1)}, u32[]{:S(2)}, u32[]{:S(2)}) collective-permute-start(f32[32,128]{1,0:T(8,128)S(1)} %get-tuple-element.55), channel_id=1, source_target_pairs={{0,128},{16,144},{32,160},{48,176},{64,192},{80,208},{96,224},{112... | collective-permute-start | bytes 49160 | tf_op jit(solution)/shard_map/ppermute | solution.py:266
  18.1 4.0 %collective-permute-start.8 = (f32[32,128]{1,0:T(8,128)S(1)}, f32[32,128]{1,0:T(8,128)S(1)}, u32[]{:S(2)}, u32[]{:S(2)}) collective-permute-start(f32[32,128]{1,0:T(8,128)S(1)} %get-tuple-element.56), channel_id=1, source_target_pairs={{0,192},{16,208},{32,224},{48,240},{64,0},{80,16},{96,32},{112,48}... | collective-permute-start | bytes 49160 | tf_op jit(solution)/shard_map/ppermute | solution.py:266
  22.2 6.8 %collective-permute-start.11 = (f32[32,128]{1,0:T(8,128)S(1)}, f32[32,128]{1,0:T(8,128)S(1)}, u32[]{:S(2)}, u32[]{:S(2)}) collective-permute-start(f32[32,128]{1,0:T(8,128)S(1)} %add_add_fusion.1), channel_id=1, source_target_pairs={{0,3},{1,2},{2,1},{3,0},{4,7},{5,6},{6,5},{7,4},{8,11},{9,10},{10,... | collective-permute-start | bytes 49160 | tf_op jit(solution)/shard_map/ppermute | solution.py:246
  27.5 2.6 %collective-permute-start.10 = (f32[32,128]{1,0:T(8,128)S(1)}, f32[32,128]{1,0:T(8,128)S(1)}, u32[]{:S(2)}, u32[]{:S(2)}) collective-permute-start(f32[32,128]{1,0:T(8,128)S(1)} %add_add_fusion.1), channel_id=1, source_target_pairs={{0,2},{1,3},{2,0},{3,1},{4,6},{5,7},{6,4},{7,5},{8,10},{9,11},{10,... | collective-permute-start | bytes 49160 | tf_op jit(solution)/shard_map/ppermute | solution.py:246
  27.5 2.6 %collective-permute-start.9 = (f32[32,128]{1,0:T(8,128)S(1)}, f32[32,128]{1,0:T(8,128)S(1)}, u32[]{:S(2)}, u32[]{:S(2)}) collective-permute-start(f32[32,128]{1,0:T(8,128)S(1)} %add_add_fusion.1), channel_id=1, source_target_pairs={{0,1},{1,0},{2,3},{3,2},{4,5},{5,4},{6,7},{7,6},{8,9},{9,8},{10,11... | collective-permute-start | bytes 49160 | tf_op jit(solution)/shard_map/ppermute | solution.py:246
  30.1 4.7 %collective-permute-start.12 = (f32[32,128]{1,0:T(8,128)S(1)}, f32[32,128]{1,0:T(8,128)S(1)}, u32[]{:S(2)}, u32[]{:S(2)}) collective-permute-start(f32[32,128]{1,0:T(8,128)S(1)} %add_add_fusion), channel_id=1, source_target_pairs={{0,4},{1,5},{2,6},{3,7},{4,0},{5,1},{6,2},{7,3},{8,12},{9,13},{10,... | collective-permute-start | bytes 49160 | tf_op jit(solution)/shard_map/ppermute | solution.py:246
  33.2 12.2 %collective-permute-start.14 = (bf16[256,256]{1,0:T(8,128)(2,1)S(1)}, bf16[256,256]{1,0:T(8,128)(2,1)S(1)}, u32[]{:S(2)}, u32[]{:S(2)}) collective-permute-start(bf16[256,256]{1,0:T(8,128)(2,1)S(1)} %get-tuple-element.78), channel_id=1, source_target_pairs={{0,32},{16,48},{32,0},{48,16},{64,96},{80,112},{96,64},{112,80},{1... | collective-permute-start | bytes 393224 | tf_op jit(solution)/shard_map/ppermute | solution.py:261
  34.7 10.7 %collective-permute-start.15 = (bf16[256,256]{1,0:T(8,128)(2,1)S(1)}, bf16[256,256]{1,0:T(8,128)(2,1)S(1)}, u32[]{:S(2)}, u32[]{:S(2)}) collective-permute-start(bf16[256,256]{1,0:T(8,128)(2,1)S(1)} %get-tuple-element.79), channel_id=1, source_target_pairs={{0,16},{16,32},{32,48},{48,0},{64,80},{80,96},{96,112},{112,64},{1... | collective-permute-start | bytes 393224 | tf_op jit(solution)/shard_map/ppermute | solution.py:261
  34.8 7.5 %copy-start = (bf16[2,1024,512]{2,1,0:T(8,128)(2,1)S(1)}, bf16[2,1024,512]{2,1,0:T(8,128)(2,1)}, u32[]{:S(2)}) copy-start(bf16[2,1024,512]{2,1,0:T(8,128)(2,1)} %keys_ref.1) | copy-start | bytes 6291460
  34.8 7.5 %copy-start.1 = (bf16[128,1024]{1,0:T(8,128)(2,1)S(1)}, bf16[128,1024]{1,0:T(8,128)(2,1)}, u32[]{:S(2)}) copy-start(bf16[128,1024]{1,0:T(8,128)(2,1)} %queries_ref.1) | copy-start | bytes 786436
  34.8 7.5 %copy-start.2 = (bf16[128,256]{1,0:T(8,128)(2,1)S(1)}, bf16[128,256]{1,0:T(8,128)(2,1)}, u32[]{:S(2)}) copy-start(bf16[128,256]{1,0:T(8,128)(2,1)} %layer_ref.1) | copy-start | bytes 196612
  34.8 7.5 %copy-start.3 = (f32[128,32]{0,1:T(8,128)S(1)}, f32[128,32]{0,1:T(8,128)}, u32[]{:S(2)}) copy-start(f32[128,32]{0,1:T(8,128)} %param.11) | copy-start | bytes 49156
  34.8 7.5 %copy-start.4 = (s32[2,128,32]{1,2,0:T(8,128)S(1)}, s32[2,128,32]{1,2,0:T(8,128)}, u32[]{:S(2)}) copy-start(s32[2,128,32]{1,2,0:T(8,128)} %param.12) | copy-start | bytes 98308
  34.9 7.4 %collective-permute-start.13 = (f32[32,128]{1,0:T(8,128)S(1)}, f32[32,128]{1,0:T(8,128)S(1)}, u32[]{:S(2)}, u32[]{:S(2)}) collective-permute-start(f32[32,128]{1,0:T(8,128)S(1)} %add.30), channel_id=1, source_target_pairs={{0,12},{1,13},{2,14},{3,15},{4,8},{5,9},{6,10},{7,11},{8,4},{9,5},... | collective-permute-start | bytes 49160 | tf_op jit(solution)/shard_map/ppermute | solution.py:246
  39.5 5.9 %collective-permute-start.16 = (bf16[256,256]{1,0:T(8,128)(2,1)S(1)}, bf16[256,256]{1,0:T(8,128)(2,1)S(1)}, u32[]{:S(2)}, u32[]{:S(2)}) collective-permute-start(bf16[256,256]{1,0:T(8,128)(2,1)S(1)} %get-tuple-element.80), channel_id=1, source_target_pairs={{0,48},{16,0},{32,16},{48,32},{64,112},{80,64},{96,80},{112,96},{1... | collective-permute-start | bytes 393224 | tf_op jit(solution)/shard_map/ppermute | solution.py:261
  63.5 7.0 %collective-permute-start.19 = (bf16[64,256]{1,0:T(8,128)(2,1)S(1)}, bf16[64,256]{1,0:T(8,128)(2,1)S(1)}, u32[]{:S(2)}, u32[]{:S(2)}) collective-permute-start(bf16[64,256]{1,0:T(8,128)(2,1)S(1)} %shard_map.108.own_ref), channel_id=1, source_target_pairs={{0,3},{1,2},{2,1},{3,0},{4,7},{5,6},{6,5},{7,4},{8,11},{9,10},{10,... | collective-permute-start | bytes 98312 | tf_op jit(solution)/shard_map/ppermute | solution.py:246
  68.3 3.3 %collective-permute-start.18 = (bf16[64,256]{1,0:T(8,128)(2,1)S(1)}, bf16[64,256]{1,0:T(8,128)(2,1)S(1)}, u32[]{:S(2)}, u32[]{:S(2)}) collective-permute-start(bf16[64,256]{1,0:T(8,128)(2,1)S(1)} %shard_map.108.own_ref), channel_id=1, source_target_pairs={{0,2},{1,3},{2,0},{3,1},{4,6},{5,7},{6,4},{7,5},{8,10},{9,11},{10,... | collective-permute-start | bytes 98312 | tf_op jit(solution)/shard_map/ppermute | solution.py:246
  69.0 2.6 %collective-permute-start.17 = (bf16[64,256]{1,0:T(8,128)(2,1)S(1)}, bf16[64,256]{1,0:T(8,128)(2,1)S(1)}, u32[]{:S(2)}, u32[]{:S(2)}) collective-permute-start(bf16[64,256]{1,0:T(8,128)(2,1)S(1)} %shard_map.108.own_ref), channel_id=1, source_target_pairs={{0,1},{1,0},{2,3},{3,2},{4,5},{5,4},{6,7},{7,6},{8,9},{9,8},{10,11... | collective-permute-start | bytes 98312 | tf_op jit(solution)/shard_map/ppermute | solution.py:246

commit v4 on v3

--- a/solution.py
+++ b/solution.py
@@ -164,7 +164,7 @@
     sem,
 ):
     slots, tokens = slot_ref.shape
-    halves, subs, width = keys_ref.shape
+    _, subs, width = keys_ref.shape
     quarter = lax.axis_index("mem") & 3
     cut = mine_ref.shape[1]
     fetch = pltpu.make_async_copy(
@@ -178,7 +178,12 @@
     block = 128
     tiles = block // 16
     base = lax.broadcasted_iota(jnp.int32, (block, tokens), 0).astype(f32) + 128.0
-    for half in range(halves):
+    dests = out_ref.shape[0]
+    own = subs // dests
+    per = width // own
+    layer = layer_ref[...]
+
+    def spread(half):
         picks = picks_ref[half]
         merged = jnp.zeros((slots, tokens), f32)
         for slot in range(slots):
@@ -187,35 +192,43 @@
         score_ref[1] = merged
         pick_code_ref[...] = row_codes(picks)
         for slot in range(slots):
-            pick_wide_ref[slot] = wide_row(pick_code_ref, slot)
-            score_wide_ref[slot] = wide_row(score_ref.at[1], slot)
-
-        def one(at, carry, half=half):
-            codes = (base * (1 << at).astype(f32)).astype(bf16)
-            codes = [codes[tile * 16 : tile * 16 + 16] for tile in range(tiles)]
-            accs = [jnp.zeros((16, tokens), bf16)] * tiles
-            for slot in range(slots):
-                pick, score = pick_wide_ref[slot], score_wide_ref[slot]
-                accs = [jnp.where(code == pick, score, acc) for code, acc in zip(codes, accs)]
-            for tile in range(tiles):
-                start = pl.multiple_of(at * block + tile * 16, 16)
-                sub_ref[half, pl.ds(start, 16), :] = accs[tile]
-            return carry
-
-        lax.fori_loop(0, subs // block, one, 0)
-    dests = out_ref.shape[0]
-    own = subs // dests
-    layer = layer_ref[...]
-    for half in range(halves):
+            pick_wide_ref[half, slot] = wide_row(pick_code_ref, slot)
+            score_wide_ref[half, slot] = wide_row(score_ref.at[1], slot)
+
+    def build(half, at, scale):
+        codes = (base * scale).astype(bf16)
+        codes = [codes[tile * 16 : tile * 16 + 16] for tile in range(tiles)]
+        accs = [jnp.zeros((16, tokens), bf16)] * tiles
+        for slot in range(slots):
+            pick, score = pick_wide_ref[half, slot], score_wide_ref[half, slot]
+            accs = [jnp.where(code == pick, score, acc) for code, acc in zip(codes, accs)]
+        for tile in range(tiles):
+            start = at * block + tile * 16
+            if not isinstance(at, int):
+                start = pl.multiple_of(start, 16)
+            sub_ref[half, pl.ds(start, 16), :] = accs[tile]
+
+    def multiply(half):
         dquery = lax.dot_general(
             sub_ref[half], keys_ref[half], (((0,), (0,)), ((), ())), preferred_element_type=f32
         ).astype(bf16)
         proj = lax.dot_general(
             dquery, layer, (((0,), (0,)), ((), ())), preferred_element_type=f32
         ).astype(bf16)
-        per = width // own
         for at in range(per):
             out_ref[half * per + at, :own, :] = proj[at * own : at * own + own]
+
+    def one(at, carry):
+        build(0, at, (1 << at).astype(f32))
+        return carry
+
+    spread(0)
+    lax.fori_loop(0, subs // block, one, 0)
+    spread(1)
+    multiply(0)
+    for at in range(subs // block):
+        build(1, at, 2.0**at)
+    multiply(1)
     fetch.wait()
     key = jnp.dot(sub_ref[quarter >> 1], mine_ref[...], preferred_element_type=f32).astype(bf16)
     for at in range(dests):
@@ -310,10 +323,11 @@
     two_away, one_away, three_away = aways
 
     one, two, three = (swap(slot_grad, mask, mem_count) for mask in (1, 2, 3))
+    sums = [along_x(two_away, 2)]
     slot_grad = (slot_grad + one) + (two + three)
-    slot_grad, two_away, one_away = lax.optimization_barrier((slot_grad, two_away, one_away))
+    slot_grad, one_away = lax.optimization_barrier((slot_grad, one_away))
     step = swap(slot_grad, 4, mem_count)
-    sums = [along_x(two_away, 2), along_x(one_away, 1)]
+    sums.append(along_x(one_away, 1))
     slot_grad = slot_grad + step
     slot_grad, recv, three_away = lax.optimization_barrier((slot_grad, recv, three_away))
     step = swap(slot_grad, 12, mem_count)
@@ -329,8 +343,8 @@
         scratch=(
             pltpu.VMEM((2, slots, tokens), f32),
             pltpu.VMEM((slots, tokens), f32),
-            pltpu.VMEM((slots, 16, tokens), bf16),
-            pltpu.VMEM((slots, 16, tokens), bf16),
+            pltpu.VMEM((halves, slots, 16, tokens), bf16),
+            pltpu.VMEM((halves, slots, 16, tokens), bf16),
             pltpu.VMEM((halves, subs, tokens), bf16),
             pltpu.VMEM((tokens, queries.shape[1] // 4), bf16),
             pltpu.SemaphoreType.DMA(()),

time: 72.5 us -> 72.5 us (level)
  no operation moved by 1% of the time
where the time goes in v4:
time: 72.5 us; the launch traced here: 72.3 us
  starting transfers between devices  34 us (47%)
  blocking collectives  18.2 us (25%)
  Pallas kernels  10.9 us (15%)
  waiting for transfers between devices  8.29 us (11%)
  between operations  0.84 us (1%)
    ppermute x8, starting transfers between devices, swap(): return lax.ppermute(x, 'mem', [(at, at ^ mask) for at in range(count)])  19.1 us
    all_to_all x1, blocking collectives, step_body(): parts = lax.all_to_all(parts, 'dp', 0, 0, tiled=True)  18.2 us
    pallas_call x9, Pallas kernels, run(): pl.pallas_call(kernel, out_shape=outs, in_specs=[FAR if at in far else VM...  10.9 us
    ppermute x6, starting transfers between devices, along_x(): lax.ppermute(x, 'dp', [(at, at // SIDE * SIDE + (at + shift) % SIDE) for...  7.46 us
    ppermute x6, starting transfers between devices, along_y(): lax.ppermute(x, 'dp', [(at, (at + shift * SIDE) % groups) for at in range...  7.42 us
    ppermute x6, waiting for transfers between devices, along_y(): lax.ppermute(x, 'dp', [(at, (at + shift * SIDE) % groups) for at in range...  4.93 us
    ppermute x8, waiting for transfers between devices, swap(): return lax.ppermute(x, 'mem', [(at, at ^ mask) for at in range(count)])  3.35 us
  transfers between devices with their start and end apart: 20, of which 6 were waited for; matrix products, arithmetic and copies ran while one was open for 0% of the time, Pallas kernels for 11%

profile of v4, /device:TPU:1, one launch (start us, length us, event | category | flops | bytes accessed | tf_op | source)
XLA Modules:
  0.0 72.3 jit_solution(3999655637146843846)
XLA Ops:
  0.6 1.0 %shard_map.103 = (bf16[160,256]{1,0:T(8,128)(2,1)S(1)}, bf16[256,256]{1,0:T(8,128)(2,1)S(1)}) custom-call(bf16[128,256]{1,0:T(8,128)(2,1)} %grad_ref.1, s32[32,128]{1,0:T(8,128)} %bitcast.6, f32[32,128]{1,0:T(8,128)} %bitcast.3, bf16[256,256]{1,0:T(8,128)(2,1)} %values_ref.1), custom_call_target="tpu_custom_call" | custom-call | tf_op jit(solution)/shard_map/pallas_call | solution.py:19
  1.6 3.6 %collective-permute-start.2 = (bf16[160,256]{1,0:T(8,128)(2,1)S(1)}, bf16[160,256]{1,0:T(8,128)(2,1)S(1)}, u32[]{:S(2)}, u32[]{:S(2)}) collective-permute-start(bf16[160,256]{1,0:T(8,128)(2,1)S(1)} %get-tuple-element.72.refs_0_), channel_id=1, source_target_pairs={{0,192},{16,208},{32,224},{48,240},{64,0},{80,16},{96,32},{112,48}... | collective-permute-start | bytes 245768 | tf_op jit(solution)/shard_map/ppermute | solution.py:279
  5.3 1.2 %collective-permute-start.3 = (bf16[256,256]{1,0:T(8,128)(2,1)}, bf16[256,256]{1,0:T(8,128)(2,1)S(1)}, u32[]{:S(2)}, u32[]{:S(2)}) collective-permute-start(bf16[256,256]{1,0:T(8,128)(2,1)} %values_ref.1), channel_id=1, source_target_pairs={{0,16},{16,32},{32,48},{48,0},{64,80},{80,96},{96,112},{112,64},{1... | collective-permute-start | bytes 393224 | tf_op jit(solution)/shard_map/ppermute | solution.py:274
  6.5 1.5 %collective-permute-start.5 = (bf16[256,256]{1,0:T(8,128)(2,1)}, bf16[256,256]{1,0:T(8,128)(2,1)S(1)}, u32[]{:S(2)}, u32[]{:S(2)}) collective-permute-start(bf16[256,256]{1,0:T(8,128)(2,1)} %values_ref.1), channel_id=1, source_target_pairs={{0,48},{16,0},{32,16},{48,32},{64,112},{80,64},{96,80},{112,96},{1... | collective-permute-start | bytes 393224 | tf_op jit(solution)/shard_map/ppermute | solution.py:274
  8.0 1.5 %collective-permute-start.4 = (bf16[256,256]{1,0:T(8,128)(2,1)}, bf16[256,256]{1,0:T(8,128)(2,1)S(1)}, u32[]{:S(2)}, u32[]{:S(2)}) collective-permute-start(bf16[256,256]{1,0:T(8,128)(2,1)} %values_ref.1), channel_id=1, source_target_pairs={{0,32},{16,48},{32,0},{48,16},{64,96},{80,112},{96,64},{112,80},{1... | collective-permute-start | bytes 393224 | tf_op jit(solution)/shard_map/ppermute | solution.py:274
  9.5 0.3 collective-permute-start.1
  9.8 0.0 collective-permute-done.2.refs_3_
  9.8 0.7 collective-permute-start
  10.5 4.0 %collective-permute-done.1.refs_2_ = bf16[160,256]{1,0:T(8,128)(2,1)S(1)} collective-permute-done((bf16[160,256]{1,0:T(8,128)(2,1)S(1)}, bf16[160,256]{1,0:T(8,128)(2,1)S(1)}, u32[]{:S(2)}, u32[]{:S(2)}) %collective-permute-start.1) | collective-permute-done | bytes 81952 | tf_op jit(solution)/shard_map/ppermute | solution.py:279
  14.6 0.9 %collective-permute-done.refs_1_ = bf16[160,256]{1,0:T(8,128)(2,1)S(1)} collective-permute-done((bf16[160,256]{1,0:T(8,128)(2,1)S(1)}, bf16[160,256]{1,0:T(8,128)(2,1)S(1)}, u32[]{:S(2)}, u32[]{:S(2)}) %collective-permute-start) | collective-permute-done | bytes 81952 | tf_op jit(solution)/shard_map/ppermute | solution.py:279
  15.5 0.0 collective-permute-done.3.refs_5_
  15.5 0.0 collective-permute-done.5.refs_7_
  15.5 0.0 collective-permute-done.4.refs_6_
  15.5 1.1 %shard_map.104 = (f32[32,128]{1,0:T(8,128)S(1)}, f32[32,128]{1,0:T(8,128)S(1)}, f32[32,128]{1,0:T(8,128)S(1)}, f32[32,128]{1,0:T(8,128)S(1)}) custom-call(bf16[160,256]{1,0:T(8,128)(2,1)S(1)} %get-tuple-element.72.refs_0_, bf16[160,256]{1,0:T(8,128)(2,1)S(1)} %collective-permute-done.refs_1_, bf16[160,256]{1,0:T(8,128)(2,1)S(1)} %collective-permute-done.1.refs_2_, ...), custom_call_target="tpu_custom_call" | custom-call | flops 1000000000 | bytes 1048576 | tf_op jit(solution)/shard_map/pallas_call | solution.py:19
  16.6 0.1 collective-permute-start.6
  16.7 1.5 %collective-permute-start.7 = (f32[32,128]{1,0:T(8,128)S(1)}, f32[32,128]{1,0:T(8,128)S(1)}, u32[]{:S(2)}, u32[]{:S(2)}) collective-permute-start(f32[32,128]{1,0:T(8,128)S(1)} %get-tuple-element.54), channel_id=1, source_target_pairs={{0,128},{16,144},{32,160},{48,176},{64,192},{80,208},{96,224},{112... | collective-permute-start | bytes 49160 | tf_op jit(solution)/shard_map/ppermute | solution.py:279
  18.1 1.2 %collective-permute-start.8 = (f32[32,128]{1,0:T(8,128)S(1)}, f32[32,128]{1,0:T(8,128)S(1)}, u32[]{:S(2)}, u32[]{:S(2)}) collective-permute-start(f32[32,128]{1,0:T(8,128)S(1)} %get-tuple-element.55), channel_id=1, source_target_pairs={{0,192},{16,208},{32,224},{48,240},{64,0},{80,16},{96,32},{112,48}... | collective-permute-start | bytes 49160 | tf_op jit(solution)/shard_map/ppermute | solution.py:279
  19.4 2.8 %shard_map.105 = (bf16[256,256]{1,0:T(8,128)(2,1)S(1)}, bf16[256,256]{1,0:T(8,128)(2,1)S(1)}, bf16[256,256]{1,0:T(8,128)(2,1)S(1)}) custom-call(bf16[160,256]{1,0:T(8,128)(2,1)S(1)} %get-tuple-element.72.refs_0_, bf16[160,256]{1,0:T(8,128)(2,1)S(1)} %collective-permute-done.refs_1_, bf16[160,256]{1,0:T(8,128)(2,1)S(1)} %collective-permute-done.1.refs_2_, ...), custom_call_target="tpu_custom_call" | custom-call | flops 2000000000 | bytes 1048576 | tf_op jit(solution)/shard_map/pallas_call | solution.py:19
  22.1 0.0 collective-permute-done.6
  22.1 0.0 collective-permute-done.7
  22.1 0.0 collective-permute-done.8
  22.2 5.4 %collective-permute-start.11 = (f32[32,128]{1,0:T(8,128)S(1)}, f32[32,128]{1,0:T(8,128)S(1)}, u32[]{:S(2)}, u32[]{:S(2)}) collective-permute-start(f32[32,128]{1,0:T(8,128)S(1)} %add_add_fusion.1), channel_id=1, source_target_pairs={{0,3},{1,2},{2,1},{3,0},{4,7},{5,6},{6,5},{7,4},{8,11},{9,10},{10,... | collective-permute-start | bytes 49160 | tf_op jit(solution)/shard_map/ppermute | solution.py:259
  27.5 0.0 collective-permute-start.10
  27.5 0.5 collective-permute-start.9
  28.0 0.9 %collective-permute-done.11 = f32[32,128]{1,0:T(8,128)S(1)} collective-permute-done((f32[32,128]{1,0:T(8,128)S(1)}, f32[32,128]{1,0:T(8,128)S(1)}, u32[]{:S(2)}, u32[]{:S(2)}) %collective-permute-start.11) | collective-permute-done | bytes 16416 | tf_op jit(solution)/shard_map/ppermute | solution.py:259
  29.0 1.2 %collective-permute-done.10 = f32[32,128]{1,0:T(8,128)S(1)} collective-permute-done((f32[32,128]{1,0:T(8,128)S(1)}, f32[32,128]{1,0:T(8,128)S(1)}, u32[]{:S(2)}, u32[]{:S(2)}) %collective-permute-start.10) | collective-permute-done | bytes 16416 | tf_op jit(solution)/shard_map/ppermute | solution.py:259
  30.1 0.0 collective-permute-done.9
  30.1 3.1 %collective-permute-start.12 = (f32[32,128]{1,0:T(8,128)S(1)}, f32[32,128]{1,0:T(8,128)S(1)}, u32[]{:S(2)}, u32[]{:S(2)}) collective-permute-start(f32[32,128]{1,0:T(8,128)S(1)} %add_add_fusion), channel_id=1, source_target_pairs={{0,4},{1,5},{2,6},{3,7},{4,0},{5,1},{6,2},{7,3},{8,12},{9,13},{10,... | collective-permute-start | bytes 49160 | tf_op jit(solution)/shard_map/ppermute | solution.py:259
  33.2 1.4 %collective-permute-start.14 = (bf16[256,256]{1,0:T(8,128)(2,1)S(1)}, bf16[256,256]{1,0:T(8,128)(2,1)S(1)}, u32[]{:S(2)}, u32[]{:S(2)}) collective-permute-start(bf16[256,256]{1,0:T(8,128)(2,1)S(1)} %get-tuple-element.76), channel_id=1, source_target_pairs={{0,32},{16,48},{32,0},{48,16},{64,96},{80,112},{96,64},{112,80},{1... | collective-permute-start | bytes 393224 | tf_op jit(solution)/shard_map/ppermute | solution.py:274
  34.7 0.0 collective-permute-start.15
  34.7 0.2 collective-permute-done.12
  34.8 0.0 copy-start
  34.8 0.0 copy-start.1
  34.8 0.0 copy-start.2
  34.8 0.0 copy-start.3
  34.8 0.0 copy-start.4
  34.9 4.6 %collective-permute-start.13 = (f32[32,128]{1,0:T(8,128)S(1)}, f32[32,128]{1,0:T(8,128)S(1)}, u32[]{:S(2)}, u32[]{:S(2)}) collective-permute-start(f32[32,128]{1,0:T(8,128)S(1)} %add.30), channel_id=1, source_target_pairs={{0,12},{1,13},{2,14},{3,15},{4,8},{5,9},{6,10},{7,11},{8,4},{9,5},... | collective-permute-start | bytes 49160 | tf_op jit(solution)/shard_map/ppermute | solution.py:259
  39.5 1.8 %collective-permute-start.16 = (bf16[256,256]{1,0:T(8,128)(2,1)S(1)}, bf16[256,256]{1,0:T(8,128)(2,1)S(1)}, u32[]{:S(2)}, u32[]{:S(2)}) collective-permute-start(bf16[256,256]{1,0:T(8,128)(2,1)S(1)} %get-tuple-element.78), channel_id=1, source_target_pairs={{0,48},{16,0},{32,16},{48,32},{64,112},{80,64},{96,80},{112,96},{1... | collective-permute-start | bytes 393224 | tf_op jit(solution)/shard_map/ppermute | solution.py:274
  41.3 0.9 %shard_map.107.refs_0_ = f32[256,256]{1,0:T(8,128)S(1)} custom-call(bf16[160,256]{1,0:T(8,128)(2,1)S(1)} %get-tuple-element.72.refs_0_, bf16[160,256]{1,0:T(8,128)(2,1)S(1)} %collective-permute-done.refs_1_, bf16[160,256]{1,0:T(8,128)(2,1)S(1)} %collective-permute-done.1.refs_2_, bf16[160,256]{1,0:T(8,128)(2,1)S(1)} %collective-permute-done.2.refs_3_), custom_call_target="tpu_custom_call" | custom-call | flops 2000000000 | bytes 1048576 | tf_op jit(solution)/shard_map/pallas_call | solution.py:19
  42.3 0.0 collective-permute-done.13
  42.3 0.0 copy-done
  42.3 0.0 copy-done.1
  42.3 0.0 copy-done.2
  42.3 0.0 copy-done.3
  42.3 0.0 copy-done.4
  42.3 2.8 %shard_map.106 = bf16[16,128,256]{2,1,0:T(8,128)(2,1)S(1)} custom-call(f32[32,128]{1,0:T(8,128)S(1)} %add.31.slot_ref, f32[32,128]{1,0:T(8,128)S(1)} %bitcast.4, s32[2,32,128]{2,1,0:T(8,128)S(1)} %bitcast.5, bf16[128,1024]{1,0:T(8,128)(2,1)S(1)} %copy-done.1, bf16[2,1024,512]{2,1,0:T(8,128)(2,1)S(1)} %copy-done, bf16[128,256]{1,0:T(8,128)(2,1)S(1)} %copy-done.2), custom_call_target="tpu_custom_call" | custom-call | tf_op jit(solution)/shard_map/pallas_call | solution.py:19
  45.2 0.0 collective-permute-done.14.refs_1_
  45.2 0.0 collective-permute-done.15.refs_2_
  45.2 0.0 collective-permute-done.16.refs_3_
  45.2 18.2 %all_to_all.5.parts_ref = bf16[16,128,256]{2,1,0:T(8,128)(2,1)S(1)} all-to-all(bf16[16,128,256]{2,1,0:T(8,128)(2,1)S(1)} %shard_map.106), channel_id=1, replica_groups=mesh['dp'=16,'mem'=16] {'dp'}, dimensions={0} | all-to-all | bytes 2097152 | tf_op jit(solution)/shard_map/all_to_all | solution.py:355
  63.4 0.1 shard_map.108.own_ref
  63.5 4.8 %collective-permute-start.19 = (bf16[64,256]{1,0:T(8,128)(2,1)S(1)}, bf16[64,256]{1,0:T(8,128)(2,1)S(1)}, u32[]{:S(2)}, u32[]{:S(2)}) collective-permute-start(bf16[64,256]{1,0:T(8,128)(2,1)S(1)} %shard_map.108.own_ref), channel_id=1, source_target_pairs={{0,3},{1,2},{2,1},{3,0},{4,7},{5,6},{6,5},{7,4},{8,11},{9,10},{10,... | collective-permute-start | bytes 98312 | tf_op jit(solution)/shard_map/ppermute | solution.py:259
  68.3 0.7 %collective-permute-start.18 = (bf16[64,256]{1,0:T(8,128)(2,1)S(1)}, bf16[64,256]{1,0:T(8,128)(2,1)S(1)}, u32[]{:S(2)}, u32[]{:S(2)}) collective-permute-start(bf16[64,256]{1,0:T(8,128)(2,1)S(1)} %shard_map.108.own_ref), channel_id=1, source_target_pairs={{0,2},{1,3},{2,0},{3,1},{4,6},{5,7},{6,4},{7,5},{8,10},{9,11},{10,... | collective-permute-start | bytes 98312 | tf_op jit(solution)/shard_map/ppermute | solution.py:259
  69.0 0.0 collective-permute-start.17
  69.0 0.8 %shard_map.109 = f32[256,256]{1,0:T(8,128)} custom-call(f32[256,256]{1,0:T(8,128)S(1)} %shard_map.107.refs_0_, bf16[256,256]{1,0:T(8,128)(2,1)S(1)} %collective-permute-done.14.refs_1_, bf16[256,256]{1,0:T(8,128)(2,1)S(1)} %collective-permute-done.15.refs_2_, bf16[256,256]{1,0:T(8,128)(2,1)S(1)} %collective-permute-done.16.refs_3_), custom_call_target="tpu_custom_call" | custom-call | flops 1000000000 | bytes 524288 | tf_op jit(solution)/shard_map/pallas_call | solution.py:19
  69.8 0.7 shard_map.111
  70.5 0.0 collective-permute-done.19.three_ref
  70.5 1.1 %collective-permute-done.18.two_ref = bf16[64,256]{1,0:T(8,128)(2,1)S(1)} collective-permute-done((bf16[64,256]{1,0:T(8,128)(2,1)S(1)}, bf16[64,256]{1,0:T(8,128)(2,1)S(1)}, u32[]{:S(2)}, u32[]{:S(2)}) %collective-permute-start.18) | collective-permute-done | bytes 32800 | tf_op jit(solution)/shard_map/ppermute | solution.py:259
  71.6 0.0 collective-permute-done.17.one_ref
  71.6 0.7 %shard_map.110 = f32[2,64,512]{2,1,0:T(8,128)} custom-call(bf16[64,256]{1,0:T(8,128)(2,1)S(1)} %shard_map.108.own_ref, bf16[64,256]{1,0:T(8,128)(2,1)S(1)} %collective-permute-done.17.one_ref, bf16[64,256]{1,0:T(8,128)(2,1)S(1)} %collective-permute-done.18.two_ref, bf16[64,256]{1,0:T(8,128)(2,1)S(1)} %collective-permute-done.19.three_ref), custom_call_target="tpu_custom_call" | custom-call | tf_op jit(solution)/shard_map/pallas_call | solution.py:19
  (4 shorter events, 0.0 us)
Async XLA Ops:
  1.6 8.2 %collective-permute-start.2 = (bf16[160,256]{1,0:T(8,128)(2,1)S(1)}, bf16[160,256]{1,0:T(8,128)(2,1)S(1)}, u32[]{:S(2)}, u32[]{:S(2)}) collective-permute-start(bf16[160,256]{1,0:T(8,128)(2,1)S(1)} %get-tuple-element.72.refs_0_), channel_id=1, source_target_pairs={{0,192},{16,208},{32,224},{48,240},{64,0},{80,16},{96,32},{112,48}... | collective-permute-start | bytes 245768 | tf_op jit(solution)/shard_map/ppermute | solution.py:279
  5.3 10.2 %collective-permute-start.3 = (bf16[256,256]{1,0:T(8,128)(2,1)}, bf16[256,256]{1,0:T(8,128)(2,1)S(1)}, u32[]{:S(2)}, u32[]{:S(2)}) collective-permute-start(bf16[256,256]{1,0:T(8,128)(2,1)} %values_ref.1), channel_id=1, source_target_pairs={{0,16},{16,32},{32,48},{48,0},{64,80},{80,96},{96,112},{112,64},{1... | collective-permute-start | bytes 393224 | tf_op jit(solution)/shard_map/ppermute | solution.py:274
  6.5 9.0 %collective-permute-start.5 = (bf16[256,256]{1,0:T(8,128)(2,1)}, bf16[256,256]{1,0:T(8,128)(2,1)S(1)}, u32[]{:S(2)}, u32[]{:S(2)}) collective-permute-start(bf16[256,256]{1,0:T(8,128)(2,1)} %values_ref.1), channel_id=1, source_target_pairs={{0,48},{16,0},{32,16},{48,32},{64,112},{80,64},{96,80},{112,96},{1... | collective-permute-start | bytes 393224 | tf_op jit(solution)/shard_map/ppermute | solution.py:274
  8.0 7.5 %collective-permute-start.4 = (bf16[256,256]{1,0:T(8,128)(2,1)}, bf16[256,256]{1,0:T(8,128)(2,1)S(1)}, u32[]{:S(2)}, u32[]{:S(2)}) collective-permute-start(bf16[256,256]{1,0:T(8,128)(2,1)} %values_ref.1), channel_id=1, source_target_pairs={{0,32},{16,48},{32,0},{48,16},{64,96},{80,112},{96,64},{112,80},{1... | collective-permute-start | bytes 393224 | tf_op jit(solution)/shard_map/ppermute | solution.py:274
  9.5 5.1 %collective-permute-start.1 = (bf16[160,256]{1,0:T(8,128)(2,1)S(1)}, bf16[160,256]{1,0:T(8,128)(2,1)S(1)}, u32[]{:S(2)}, u32[]{:S(2)}) collective-permute-start(bf16[160,256]{1,0:T(8,128)(2,1)S(1)} %get-tuple-element.72.refs_0_), channel_id=1, source_target_pairs={{0,128},{16,144},{32,160},{48,176},{64,192},{80,208},{96,224},{112... | collective-permute-start | bytes 245768 | tf_op jit(solution)/shard_map/ppermute | solution.py:279
  9.8 5.6 %collective-permute-start = (bf16[160,256]{1,0:T(8,128)(2,1)S(1)}, bf16[160,256]{1,0:T(8,128)(2,1)S(1)}, u32[]{:S(2)}, u32[]{:S(2)}) collective-permute-start(bf16[160,256]{1,0:T(8,128)(2,1)S(1)} %get-tuple-element.72.refs_0_), channel_id=1, source_target_pairs={{0,64},{16,80},{32,96},{48,112},{64,128},{80,144},{96,160},{112,17... | collective-permute-start | bytes 245768 | tf_op jit(solution)/shard_map/ppermute | solution.py:279
  16.6 5.5 %collective-permute-start.6 = (f32[32,128]{1,0:T(8,128)S(1)}, f32[32,128]{1,0:T(8,128)S(1)}, u32[]{:S(2)}, u32[]{:S(2)}) collective-permute-start(f32[32,128]{1,0:T(8,128)S(1)} %get-tuple-element.53), channel_id=1, source_target_pairs={{0,64},{16,80},{32,96},{48,112},{64,128},{80,144},{96,160},{112,17... | collective-permute-start | bytes 49160 | tf_op jit(solution)/shard_map/ppermute | solution.py:279
  16.7 5.5 %collective-permute-start.7 = (f32[32,128]{1,0:T(8,128)S(1)}, f32[32,128]{1,0:T(8,128)S(1)}, u32[]{:S(2)}, u32[]{:S(2)}) collective-permute-start(f32[32,128]{1,0:T(8,128)S(1)} %get-tuple-element.54), channel_id=1, source_target_pairs={{0,128},{16,144},{32,160},{48,176},{64,192},{80,208},{96,224},{112... | collective-permute-start | bytes 49160 | tf_op jit(solution)/shard_map/ppermute | solution.py:279
  18.1 4.0 %collective-permute-start.8 = (f32[32,128]{1,0:T(8,128)S(1)}, f32[32,128]{1,0:T(8,128)S(1)}, u32[]{:S(2)}, u32[]{:S(2)}) collective-permute-start(f32[32,128]{1,0:T(8,128)S(1)} %get-tuple-element.55), channel_id=1, source_target_pairs={{0,192},{16,208},{32,224},{48,240},{64,0},{80,16},{96,32},{112,48}... | collective-permute-start | bytes 49160 | tf_op jit(solution)/shard_map/ppermute | solution.py:279
  22.2 6.8 %collective-permute-start.11 = (f32[32,128]{1,0:T(8,128)S(1)}, f32[32,128]{1,0:T(8,128)S(1)}, u32[]{:S(2)}, u32[]{:S(2)}) collective-permute-start(f32[32,128]{1,0:T(8,128)S(1)} %add_add_fusion.1), channel_id=1, source_target_pairs={{0,3},{1,2},{2,1},{3,0},{4,7},{5,6},{6,5},{7,4},{8,11},{9,10},{10,... | collective-permute-start | bytes 49160 | tf_op jit(solution)/shard_map/ppermute | solution.py:259
  27.5 2.6 %collective-permute-start.10 = (f32[32,128]{1,0:T(8,128)S(1)}, f32[32,128]{1,0:T(8,128)S(1)}, u32[]{:S(2)}, u32[]{:S(2)}) collective-permute-start(f32[32,128]{1,0:T(8,128)S(1)} %add_add_fusion.1), channel_id=1, source_target_pairs={{0,2},{1,3},{2,0},{3,1},{4,6},{5,7},{6,4},{7,5},{8,10},{9,11},{10,... | collective-permute-start | bytes 49160 | tf_op jit(solution)/shard_map/ppermute | solution.py:259
  27.5 2.6 %collective-permute-start.9 = (f32[32,128]{1,0:T(8,128)S(1)}, f32[32,128]{1,0:T(8,128)S(1)}, u32[]{:S(2)}, u32[]{:S(2)}) collective-permute-start(f32[32,128]{1,0:T(8,128)S(1)} %add_add_fusion.1), channel_id=1, source_target_pairs={{0,1},{1,0},{2,3},{3,2},{4,5},{5,4},{6,7},{7,6},{8,9},{9,8},{10,11... | collective-permute-start | bytes 49160 | tf_op jit(solution)/shard_map/ppermute | solution.py:259
  30.1 4.7 %collective-permute-start.12 = (f32[32,128]{1,0:T(8,128)S(1)}, f32[32,128]{1,0:T(8,128)S(1)}, u32[]{:S(2)}, u32[]{:S(2)}) collective-permute-start(f32[32,128]{1,0:T(8,128)S(1)} %add_add_fusion), channel_id=1, source_target_pairs={{0,4},{1,5},{2,6},{3,7},{4,0},{5,1},{6,2},{7,3},{8,12},{9,13},{10,... | collective-permute-start | bytes 49160 | tf_op jit(solution)/shard_map/ppermute | solution.py:259
  33.2 12.0 %collective-permute-start.14 = (bf16[256,256]{1,0:T(8,128)(2,1)S(1)}, bf16[256,256]{1,0:T(8,128)(2,1)S(1)}, u32[]{:S(2)}, u32[]{:S(2)}) collective-permute-start(bf16[256,256]{1,0:T(8,128)(2,1)S(1)} %get-tuple-element.76), channel_id=1, source_target_pairs={{0,32},{16,48},{32,0},{48,16},{64,96},{80,112},{96,64},{112,80},{1... | collective-permute-start | bytes 393224 | tf_op jit(solution)/shard_map/ppermute | solution.py:274
  34.7 10.5 %collective-permute-start.15 = (bf16[256,256]{1,0:T(8,128)(2,1)S(1)}, bf16[256,256]{1,0:T(8,128)(2,1)S(1)}, u32[]{:S(2)}, u32[]{:S(2)}) collective-permute-start(bf16[256,256]{1,0:T(8,128)(2,1)S(1)} %get-tuple-element.77), channel_id=1, source_target_pairs={{0,16},{16,32},{32,48},{48,0},{64,80},{80,96},{96,112},{112,64},{1... | collective-permute-start | bytes 393224 | tf_op jit(solution)/shard_map/ppermute | solution.py:274
  34.8 7.5 %copy-start = (bf16[2,1024,512]{2,1,0:T(8,128)(2,1)S(1)}, bf16[2,1024,512]{2,1,0:T(8,128)(2,1)}, u32[]{:S(2)}) copy-start(bf16[2,1024,512]{2,1,0:T(8,128)(2,1)} %keys_ref.1) | copy-start | bytes 6291460
  34.8 7.5 %copy-start.1 = (bf16[128,1024]{1,0:T(8,128)(2,1)S(1)}, bf16[128,1024]{1,0:T(8,128)(2,1)}, u32[]{:S(2)}) copy-start(bf16[128,1024]{1,0:T(8,128)(2,1)} %queries_ref.1) | copy-start | bytes 786436
  34.8 7.5 %copy-start.2 = (bf16[128,256]{1,0:T(8,128)(2,1)S(1)}, bf16[128,256]{1,0:T(8,128)(2,1)}, u32[]{:S(2)}) copy-start(bf16[128,256]{1,0:T(8,128)(2,1)} %layer_ref.1) | copy-start | bytes 196612
  34.8 7.5 %copy-start.3 = (f32[128,32]{0,1:T(8,128)S(1)}, f32[128,32]{0,1:T(8,128)}, u32[]{:S(2)}) copy-start(f32[128,32]{0,1:T(8,128)} %param.11) | copy-start | bytes 49156
  34.8 7.5 %copy-start.4 = (s32[2,128,32]{1,2,0:T(8,128)S(1)}, s32[2,128,32]{1,2,0:T(8,128)}, u32[]{:S(2)}) copy-start(s32[2,128,32]{1,2,0:T(8,128)} %param.12) | copy-start | bytes 98308
  34.9 7.4 %collective-permute-start.13 = (f32[32,128]{1,0:T(8,128)S(1)}, f32[32,128]{1,0:T(8,128)S(1)}, u32[]{:S(2)}, u32[]{:S(2)}) collective-permute-start(f32[32,128]{1,0:T(8,128)S(1)} %add.30), channel_id=1, source_target_pairs={{0,12},{1,13},{2,14},{3,15},{4,8},{5,9},{6,10},{7,11},{8,4},{9,5},... | collective-permute-start | bytes 49160 | tf_op jit(solution)/shard_map/ppermute | solution.py:259
  39.5 5.7 %collective-permute-start.16 = (bf16[256,256]{1,0:T(8,128)(2,1)S(1)}, bf16[256,256]{1,0:T(8,128)(2,1)S(1)}, u32[]{:S(2)}, u32[]{:S(2)}) collective-permute-start(bf16[256,256]{1,0:T(8,128)(2,1)S(1)} %get-tuple-element.78), channel_id=1, source_target_pairs={{0,48},{16,0},{32,16},{48,32},{64,112},{80,64},{96,80},{112,96},{1... | collective-permute-start | bytes 393224 | tf_op jit(solution)/shard_map/ppermute | solution.py:274
  63.5 7.0 %collective-permute-start.19 = (bf16[64,256]{1,0:T(8,128)(2,1)S(1)}, bf16[64,256]{1,0:T(8,128)(2,1)S(1)}, u32[]{:S(2)}, u32[]{:S(2)}) collective-permute-start(bf16[64,256]{1,0:T(8,128)(2,1)S(1)} %shard_map.108.own_ref), channel_id=1, source_target_pairs={{0,3},{1,2},{2,1},{3,0},{4,7},{5,6},{6,5},{7,4},{8,11},{9,10},{10,... | collective-permute-start | bytes 98312 | tf_op jit(solution)/shard_map/ppermute | solution.py:259
  68.3 3.3 %collective-permute-start.18 = (bf16[64,256]{1,0:T(8,128)(2,1)S(1)}, bf16[64,256]{1,0:T(8,128)(2,1)S(1)}, u32[]{:S(2)}, u32[]{:S(2)}) collective-permute-start(bf16[64,256]{1,0:T(8,128)(2,1)S(1)} %shard_map.108.own_ref), channel_id=1, source_target_pairs={{0,2},{1,3},{2,0},{3,1},{4,6},{5,7},{6,4},{7,5},{8,10},{9,11},{10,... | collective-permute-start | bytes 98312 | tf_op jit(solution)/shard_map/ppermute | solution.py:259
  69.0 2.6 %collective-permute-start.17 = (bf16[64,256]{1,0:T(8,128)(2,1)S(1)}, bf16[64,256]{1,0:T(8,128)(2,1)S(1)}, u32[]{:S(2)}, u32[]{:S(2)}) collective-permute-start(bf16[64,256]{1,0:T(8,128)(2,1)S(1)} %shard_map.108.own_ref), channel_id=1, source_target_pairs={{0,1},{1,0},{2,3},{3,2},{4,5},{5,4},{6,7},{7,6},{8,9},{9,8},{10,11... | collective-permute-start | bytes 98312 | tf_op jit(solution)/shard_map/ppermute | solution.py:259

commit v5 on v4

--- a/solution.py
+++ b/solution.py
@@ -308,6 +308,7 @@
             data=2**20,
         )
 
+    two_away, one_away, three_away = value_part((2, 1, 3), recv)
     slot_parts = run(
         slot_kernel,
         [shape((slots, tokens), f32)] * SIDE,
@@ -317,22 +318,21 @@
     )
     slot_parts, recv = lax.optimization_barrier((slot_parts, recv))
     back = [along_y(slot_parts[shift], shift) for shift in (1, 2, 3)]
-    aways = value_part((2, 1, 3), recv)
+    (mine,) = value_part((0,), recv)
+    sums = [along_x(two_away, 2)]
     slot_grad = (slot_parts[0] + back[0]) + (back[1] + back[2])
-    slot_grad, recv, aways = lax.optimization_barrier((slot_grad, recv, aways))
-    two_away, one_away, three_away = aways
+    slot_grad, one_away, three_away, mine = lax.optimization_barrier(
+        (slot_grad, one_away, three_away, mine)
+    )
 
     one, two, three = (swap(slot_grad, mask, mem_count) for mask in (1, 2, 3))
-    sums = [along_x(two_away, 2)]
+    sums.append(along_x(one_away, 1))
     slot_grad = (slot_grad + one) + (two + three)
-    slot_grad, one_away = lax.optimization_barrier((slot_grad, one_away))
+    slot_grad, three_away = lax.optimization_barrier((slot_grad, three_away))
     step = swap(slot_grad, 4, mem_count)
-    sums.append(along_x(one_away, 1))
+    sums.append(along_x(three_away, 3))
     slot_grad = slot_grad + step
-    slot_grad, recv, three_away = lax.optimization_barrier((slot_grad, recv, three_away))
     step = swap(slot_grad, 12, mem_count)
-    sums.append(along_x(three_away, 3))
-    (mine,) = value_part((0,), recv)
     slot_grad = slot_grad + step
 
     own = subs // groups

time: 72.5 us -> 73.4 us (1.012)
  starting transfers between devices: 34 us -> 37.3 us
  blocking collectives: 18.2 us -> 16.6 us
  waiting for transfers between devices: 8.29 us -> 7.49 us
    ppermute x6, starting transfers between devices: 7.46 us -> 9.67 us  [along_x(): lax.ppermute(x, 'dp', [(at, at // SIDE * SIDE + (at + shift) % SIDE) for...]
    ppermute x6, waiting for transfers between devices: 4.93 us -> 2.76 us  [along_y(): lax.ppermute(x, 'dp', [(at, (at + shift * SIDE) % groups) for at in range...]
    all_to_all x1, blocking collectives: 18.2 us -> 16.6 us  [step_body(): parts = lax.all_to_all(parts, 'dp', 0, 0, tiled=True)]
    ppermute x6, starting transfers between devices: 7.42 us -> 8.85 us  [along_y(): lax.ppermute(x, 'dp', [(at, (at + shift * SIDE) % groups) for at in range...]
    ppermute x6, waiting for transfers between devices: 0.02 us -> 1.15 us  [along_x(): lax.ppermute(x, 'dp', [(at, at // SIDE * SIDE + (at + shift) % SIDE) for...]
  transfers between devices with their start and end apart: 20 -> 20, of which waited for: 6 -> 7; matrix products, arithmetic and copies ran while one was open for 0% -> 0% of each run, Pallas kernels for 11% -> 11%
where the time goes in v5:
time: 73.4 us; the launch traced here: 73.2 us
  starting transfers between devices  37.3 us (51%)
  blocking collectives  16.6 us (23%)
  Pallas kernels  10.9 us (15%)
  waiting for transfers between devices  7.49 us (10%)
  between operations  0.82 us (1%)
    ppermute x8, starting transfers between devices, swap(): return lax.ppermute(x, 'mem', [(at, at ^ mask) for at in range(count)])  18.8 us
    all_to_all x1, blocking collectives, step_body(): parts = lax.all_to_all(parts, 'dp', 0, 0, tiled=True)  16.6 us
    pallas_call x9, Pallas kernels, run(): pl.pallas_call(kernel, out_shape=outs, in_specs=[FAR if at in far else VM...  10.9 us
    ppermute x6, starting transfers between devices, along_x(): lax.ppermute(x, 'dp', [(at, at // SIDE * SIDE + (at + shift) % SIDE) for...  9.67 us
    ppermute x6, starting transfers between devices, along_y(): lax.ppermute(x, 'dp', [(at, (at + shift * SIDE) % groups) for at in range...  8.85 us
    ppermute x8, waiting for transfers between devices, swap(): return lax.ppermute(x, 'mem', [(at, at ^ mask) for at in range(count)])  3.57 us
    ppermute x6, waiting for transfers between devices, along_y(): lax.ppermute(x, 'dp', [(at, (at + shift * SIDE) % groups) for at in range...  2.76 us
  transfers between devices with their start and end apart: 20, of which 7 were waited for; matrix products, arithmetic and copies ran while one was open for 0% of the time, Pallas kernels for 11%

profile of v5, /device:TPU:1, one launch (start us, length us, event | category | flops | bytes accessed | tf_op | source)
XLA Modules:
  0.0 73.2 jit_solution(6385959219017047733)
XLA Ops:
  0.6 1.0 %shard_map.103 = (bf16[160,256]{1,0:T(8,128)(2,1)S(1)}, bf16[256,256]{1,0:T(8,128)(2,1)S(1)}) custom-call(bf16[128,256]{1,0:T(8,128)(2,1)} %grad_ref.1, s32[32,128]{1,0:T(8,128)} %bitcast.6, f32[32,128]{1,0:T(8,128)} %bitcast.3, bf16[256,256]{1,0:T(8,128)(2,1)} %values_ref.1), custom_call_target="tpu_custom_call" | custom-call | tf_op jit(solution)/shard_map/pallas_call | solution.py:19
  1.6 3.6 %collective-permute-start.2 = (bf16[160,256]{1,0:T(8,128)(2,1)S(1)}, bf16[160,256]{1,0:T(8,128)(2,1)S(1)}, u32[]{:S(2)}, u32[]{:S(2)}) collective-permute-start(bf16[160,256]{1,0:T(8,128)(2,1)S(1)} %get-tuple-element.48.refs_0_), channel_id=1, source_target_pairs={{0,192},{16,208},{32,224},{48,240},{64,0},{80,16},{96,32},{112,48}... | collective-permute-start | bytes 245768 | tf_op jit(solution)/shard_map/ppermute | solution.py:279
  5.3 0.3 collective-permute-start.1
  5.6 0.7 collective-permute-start
  6.3 1.2 %collective-permute-start.3 = (bf16[256,256]{1,0:T(8,128)(2,1)}, bf16[256,256]{1,0:T(8,128)(2,1)S(1)}, u32[]{:S(2)}, u32[]{:S(2)}) collective-permute-start(bf16[256,256]{1,0:T(8,128)(2,1)} %values_ref.1), channel_id=1, source_target_pairs={{0,16},{16,32},{32,48},{48,0},{64,80},{80,96},{96,112},{112,64},{1... | collective-permute-start | bytes 393224 | tf_op jit(solution)/shard_map/ppermute | solution.py:274
  7.5 1.5 %collective-permute-start.5 = (bf16[256,256]{1,0:T(8,128)(2,1)}, bf16[256,256]{1,0:T(8,128)(2,1)S(1)}, u32[]{:S(2)}, u32[]{:S(2)}) collective-permute-start(bf16[256,256]{1,0:T(8,128)(2,1)} %values_ref.1), channel_id=1, source_target_pairs={{0,48},{16,0},{32,16},{48,32},{64,112},{80,64},{96,80},{112,96},{1... | collective-permute-start | bytes 393224 | tf_op jit(solution)/shard_map/ppermute | solution.py:274
  9.0 0.0 collective-permute-done.2.refs_3_
  9.0 1.5 %collective-permute-start.4 = (bf16[256,256]{1,0:T(8,128)(2,1)}, bf16[256,256]{1,0:T(8,128)(2,1)S(1)}, u32[]{:S(2)}, u32[]{:S(2)}) collective-permute-start(bf16[256,256]{1,0:T(8,128)(2,1)} %values_ref.1), channel_id=1, source_target_pairs={{0,32},{16,48},{32,0},{48,16},{64,96},{80,112},{96,64},{112,80},{1... | collective-permute-start | bytes 393224 | tf_op jit(solution)/shard_map/ppermute | solution.py:274
  10.5 0.0 collective-permute-done.1.refs_2_
  10.5 1.8 %collective-permute-done.refs_1_ = bf16[160,256]{1,0:T(8,128)(2,1)S(1)} collective-permute-done((bf16[160,256]{1,0:T(8,128)(2,1)S(1)}, bf16[160,256]{1,0:T(8,128)(2,1)S(1)}, u32[]{:S(2)}, u32[]{:S(2)}) %collective-permute-start) | collective-permute-done | bytes 81952 | tf_op jit(solution)/shard_map/ppermute | solution.py:279
  12.3 2.8 %shard_map.105 = (bf16[256,256]{1,0:T(8,128)(2,1)S(1)}, bf16[256,256]{1,0:T(8,128)(2,1)S(1)}, bf16[256,256]{1,0:T(8,128)(2,1)S(1)}) custom-call(bf16[160,256]{1,0:T(8,128)(2,1)S(1)} %get-tuple-element.48.refs_0_, bf16[160,256]{1,0:T(8,128)(2,1)S(1)} %collective-permute-done.refs_1_, bf16[160,256]{1,0:T(8,128)(2,1)S(1)} %collective-permute-done.1.refs_2_, ...), custom_call_target="tpu_custom_call" | custom-call | flops 2000000000 | bytes 1048576 | tf_op jit(solution)/shard_map/pallas_call | solution.py:19
  15.1 0.0 collective-permute-done.3.refs_5_
  15.1 0.0 collective-permute-done.5.refs_7_
  15.1 1.1 %collective-permute-done.4.refs_6_ = bf16[256,256]{1,0:T(8,128)(2,1)S(1)} collective-permute-done((bf16[256,256]{1,0:T(8,128)(2,1)}, bf16[256,256]{1,0:T(8,128)(2,1)S(1)}, u32[]{:S(2)}, u32[]{:S(2)}) %collective-permute-start.4) | collective-permute-done | bytes 131104 | tf_op jit(solution)/shard_map/ppermute | solution.py:274
  16.2 1.1 %shard_map.104 = (f32[32,128]{1,0:T(8,128)S(1)}, f32[32,128]{1,0:T(8,128)S(1)}, f32[32,128]{1,0:T(8,128)S(1)}, f32[32,128]{1,0:T(8,128)S(1)}) custom-call(bf16[160,256]{1,0:T(8,128)(2,1)S(1)} %get-tuple-element.48.refs_0_, bf16[160,256]{1,0:T(8,128)(2,1)S(1)} %collective-permute-done.refs_1_, bf16[160,256]{1,0:T(8,128)(2,1)S(1)} %collective-permute-done.1.refs_2_, ...), custom_call_target="tpu_custom_call" | custom-call | flops 1000000000 | bytes 1048576 | tf_op jit(solution)/shard_map/pallas_call | solution.py:19
  17.4 0.0 copy-start
  17.4 0.0 copy-start.1
  17.4 0.0 copy-start.2
  17.4 0.0 copy-start.3
  17.4 0.0 copy-start.4
  17.4 1.7 %collective-permute-start.6 = (f32[32,128]{1,0:T(8,128)S(1)}, f32[32,128]{1,0:T(8,128)S(1)}, u32[]{:S(2)}, u32[]{:S(2)}) collective-permute-start(f32[32,128]{1,0:T(8,128)S(1)} %get-tuple-element.43), channel_id=1, source_target_pairs={{0,64},{16,80},{32,96},{48,112},{64,128},{80,144},{96,160},{112,17... | collective-permute-start | bytes 49160 | tf_op jit(solution)/shard_map/ppermute | solution.py:279
  19.1 1.6 %collective-permute-start.7 = (f32[32,128]{1,0:T(8,128)S(1)}, f32[32,128]{1,0:T(8,128)S(1)}, u32[]{:S(2)}, u32[]{:S(2)}) collective-permute-start(f32[32,128]{1,0:T(8,128)S(1)} %get-tuple-element.44), channel_id=1, source_target_pairs={{0,128},{16,144},{32,160},{48,176},{64,192},{80,208},{96,224},{112... | collective-permute-start | bytes 49160 | tf_op jit(solution)/shard_map/ppermute | solution.py:279
  20.7 0.9 %collective-permute-start.8 = (f32[32,128]{1,0:T(8,128)S(1)}, f32[32,128]{1,0:T(8,128)S(1)}, u32[]{:S(2)}, u32[]{:S(2)}) collective-permute-start(f32[32,128]{1,0:T(8,128)S(1)} %get-tuple-element.45), channel_id=1, source_target_pairs={{0,192},{16,208},{32,224},{48,240},{64,0},{80,16},{96,32},{112,48}... | collective-permute-start | bytes 49160 | tf_op jit(solution)/shard_map/ppermute | solution.py:279
  21.6 0.9 %shard_map.106.refs_0_ = f32[256,256]{1,0:T(8,128)S(1)} custom-call(bf16[160,256]{1,0:T(8,128)(2,1)S(1)} %get-tuple-element.48.refs_0_, bf16[160,256]{1,0:T(8,128)(2,1)S(1)} %collective-permute-done.refs_1_, bf16[160,256]{1,0:T(8,128)(2,1)S(1)} %collective-permute-done.1.refs_2_, bf16[160,256]{1,0:T(8,128)(2,1)S(1)} %collective-permute-done.2.refs_3_), custom_call_target="tpu_custom_call" | custom-call | flops 2000000000 | bytes 1048576 | tf_op jit(solution)/shard_map/pallas_call | solution.py:19
  22.5 0.0 collective-permute-done.6
  22.5 0.6 collective-permute-done.7
  23.2 0.3 collective-permute-done.8
  23.6 4.8 %collective-permute-start.11 = (f32[32,128]{1,0:T(8,128)S(1)}, f32[32,128]{1,0:T(8,128)S(1)}, u32[]{:S(2)}, u32[]{:S(2)}) collective-permute-start(f32[32,128]{1,0:T(8,128)S(1)} %add_add_fusion.1), channel_id=1, source_target_pairs={{0,3},{1,2},{2,1},{3,0},{4,7},{5,6},{6,5},{7,4},{8,11},{9,10},{10,... | collective-permute-start | bytes 49160 | tf_op jit(solution)/shard_map/ppermute | solution.py:259
  28.4 0.0 collective-permute-start.10
  28.4 0.5 collective-permute-start.9
  28.9 2.5 %collective-permute-start.14 = (bf16[256,256]{1,0:T(8,128)(2,1)S(1)}, bf16[256,256]{1,0:T(8,128)(2,1)S(1)}, u32[]{:S(2)}, u32[]{:S(2)}) collective-permute-start(bf16[256,256]{1,0:T(8,128)(2,1)S(1)} %get-tuple-element.56), channel_id=1, source_target_pairs={{0,32},{16,48},{32,0},{48,16},{64,96},{80,112},{96,64},{112,80},{1... | collective-permute-start | bytes 393224 | tf_op jit(solution)/shard_map/ppermute | solution.py:274
  31.4 0.3 collective-permute-start.15
  31.7 0.0 collective-permute-done.11
  31.7 0.0 collective-permute-done.10
  31.7 0.0 collective-permute-done.9
  31.7 2.6 %collective-permute-start.16 = (bf16[256,256]{1,0:T(8,128)(2,1)S(1)}, bf16[256,256]{1,0:T(8,128)(2,1)S(1)}, u32[]{:S(2)}, u32[]{:S(2)}) collective-permute-start(bf16[256,256]{1,0:T(8,128)(2,1)S(1)} %get-tuple-element.58), channel_id=1, source_target_pairs={{0,48},{16,0},{32,16},{48,32},{64,112},{80,64},{96,80},{112,96},{1... | collective-permute-start | bytes 393224 | tf_op jit(solution)/shard_map/ppermute | solution.py:274
  34.3 3.0 %collective-permute-start.12 = (f32[32,128]{1,0:T(8,128)S(1)}, f32[32,128]{1,0:T(8,128)S(1)}, u32[]{:S(2)}, u32[]{:S(2)}) collective-permute-start(f32[32,128]{1,0:T(8,128)S(1)} %add_add_fusion), channel_id=1, source_target_pairs={{0,4},{1,5},{2,6},{3,7},{4,0},{5,1},{6,2},{7,3},{8,12},{9,13},{10,... | collective-permute-start | bytes 49160 | tf_op jit(solution)/shard_map/ppermute | solution.py:259
  37.3 1.3 %collective-permute-done.12 = f32[32,128]{1,0:T(8,128)S(1)} collective-permute-done((f32[32,128]{1,0:T(8,128)S(1)}, f32[32,128]{1,0:T(8,128)S(1)}, u32[]{:S(2)}, u32[]{:S(2)}) %collective-permute-start.12) | collective-permute-done | bytes 16416 | tf_op jit(solution)/shard_map/ppermute | solution.py:259
  38.7 4.8 %collective-permute-start.13 = (f32[32,128]{1,0:T(8,128)S(1)}, f32[32,128]{1,0:T(8,128)S(1)}, u32[]{:S(2)}, u32[]{:S(2)}) collective-permute-start(f32[32,128]{1,0:T(8,128)S(1)} %add.30), channel_id=1, source_target_pairs={{0,12},{1,13},{2,14},{3,15},{4,8},{5,9},{6,10},{7,11},{8,4},{9,5},... | collective-permute-start | bytes 49160 | tf_op jit(solution)/shard_map/ppermute | solution.py:259
  43.5 1.1 %collective-permute-done.13 = f32[32,128]{1,0:T(8,128)S(1)} collective-permute-done((f32[32,128]{1,0:T(8,128)S(1)}, f32[32,128]{1,0:T(8,128)S(1)}, u32[]{:S(2)}, u32[]{:S(2)}) %collective-permute-start.13) | collective-permute-done | bytes 16416 | tf_op jit(solution)/shard_map/ppermute | solution.py:259
  44.6 0.0 copy-done
  44.6 0.0 copy-done.1
  44.6 0.0 copy-done.2
  44.6 0.0 copy-done.3
  44.7 0.0 copy-done.4
  44.7 2.8 %shard_map.107 = bf16[16,128,256]{2,1,0:T(8,128)(2,1)S(1)} custom-call(f32[32,128]{1,0:T(8,128)S(1)} %add.31.slot_ref, f32[32,128]{1,0:T(8,128)S(1)} %bitcast.4, s32[2,32,128]{2,1,0:T(8,128)S(1)} %bitcast.5, bf16[128,1024]{1,0:T(8,128)(2,1)S(1)} %copy-done.1, bf16[2,1024,512]{2,1,0:T(8,128)(2,1)S(1)} %copy-done, bf16[128,256]{1,0:T(8,128)(2,1)S(1)} %copy-done.2), custom_call_target="tpu_custom_call" | custom-call | tf_op jit(solution)/shard_map/pallas_call | solution.py:19
  47.5 0.0 collective-permute-done.14.refs_1_
  47.5 0.0 collective-permute-done.15.refs_2_
  47.5 0.0 collective-permute-done.16.refs_3_
  47.5 16.6 %all_to_all.5.parts_ref = bf16[16,128,256]{2,1,0:T(8,128)(2,1)S(1)} all-to-all(bf16[16,128,256]{2,1,0:T(8,128)(2,1)S(1)} %shard_map.107), channel_id=1, replica_groups=mesh['dp'=16,'mem'=16] {'dp'}, dimensions={0} | all-to-all | bytes 2097152 | tf_op jit(solution)/shard_map/all_to_all | solution.py:355
  64.1 0.1 shard_map.108.own_ref
  64.2 5.0 %collective-permute-start.19 = (bf16[64,256]{1,0:T(8,128)(2,1)S(1)}, bf16[64,256]{1,0:T(8,128)(2,1)S(1)}, u32[]{:S(2)}, u32[]{:S(2)}) collective-permute-start(bf16[64,256]{1,0:T(8,128)(2,1)S(1)} %shard_map.108.own_ref), channel_id=1, source_target_pairs={{0,3},{1,2},{2,1},{3,0},{4,7},{5,6},{6,5},{7,4},{8,11},{9,10},{10,... | collective-permute-start | bytes 98312 | tf_op jit(solution)/shard_map/ppermute | solution.py:259
  69.1 0.7 collective-permute-start.18
  69.9 0.0 collective-permute-start.17
  69.9 0.8 %shard_map.109 = f32[256,256]{1,0:T(8,128)} custom-call(f32[256,256]{1,0:T(8,128)S(1)} %shard_map.106.refs_0_, bf16[256,256]{1,0:T(8,128)(2,1)S(1)} %collective-permute-done.14.refs_1_, bf16[256,256]{1,0:T(8,128)(2,1)S(1)} %collective-permute-done.15.refs_2_, bf16[256,256]{1,0:T(8,128)(2,1)S(1)} %collective-permute-done.16.refs_3_), custom_call_target="tpu_custom_call" | custom-call | flops 1000000000 | bytes 524288 | tf_op jit(solution)/shard_map/pallas_call | solution.py:19
  70.6 0.7 shard_map.111
  71.3 0.0 collective-permute-done.19.three_ref
  71.3 1.1 %collective-permute-done.18.two_ref = bf16[64,256]{1,0:T(8,128)(2,1)S(1)} collective-permute-done((bf16[64,256]{1,0:T(8,128)(2,1)S(1)}, bf16[64,256]{1,0:T(8,128)(2,1)S(1)}, u32[]{:S(2)}, u32[]{:S(2)}) %collective-permute-start.18) | collective-permute-done | bytes 32800 | tf_op jit(solution)/shard_map/ppermute | solution.py:259
  72.4 0.0 collective-permute-done.17.one_ref
  72.4 0.7 shard_map.110
  (4 shorter events, 0.0 us)
Async XLA Ops:
  1.6 7.4 %collective-permute-start.2 = (bf16[160,256]{1,0:T(8,128)(2,1)S(1)}, bf16[160,256]{1,0:T(8,128)(2,1)S(1)}, u32[]{:S(2)}, u32[]{:S(2)}) collective-permute-start(bf16[160,256]{1,0:T(8,128)(2,1)S(1)} %get-tuple-element.48.refs_0_), channel_id=1, source_target_pairs={{0,192},{16,208},{32,224},{48,240},{64,0},{80,16},{96,32},{112,48}... | collective-permute-start | bytes 245768 | tf_op jit(solution)/shard_map/ppermute | solution.py:279
  5.3 5.3 %collective-permute-start.1 = (bf16[160,256]{1,0:T(8,128)(2,1)S(1)}, bf16[160,256]{1,0:T(8,128)(2,1)S(1)}, u32[]{:S(2)}, u32[]{:S(2)}) collective-permute-start(bf16[160,256]{1,0:T(8,128)(2,1)S(1)} %get-tuple-element.48.refs_0_), channel_id=1, source_target_pairs={{0,128},{16,144},{32,160},{48,176},{64,192},{80,208},{96,224},{112... | collective-permute-start | bytes 245768 | tf_op jit(solution)/shard_map/ppermute | solution.py:279
  5.6 6.7 %collective-permute-start = (bf16[160,256]{1,0:T(8,128)(2,1)S(1)}, bf16[160,256]{1,0:T(8,128)(2,1)S(1)}, u32[]{:S(2)}, u32[]{:S(2)}) collective-permute-start(bf16[160,256]{1,0:T(8,128)(2,1)S(1)} %get-tuple-element.48.refs_0_), channel_id=1, source_target_pairs={{0,64},{16,80},{32,96},{48,112},{64,128},{80,144},{96,160},{112,17... | collective-permute-start | bytes 245768 | tf_op jit(solution)/shard_map/ppermute | solution.py:279
  6.3 8.8 %collective-permute-start.3 = (bf16[256,256]{1,0:T(8,128)(2,1)}, bf16[256,256]{1,0:T(8,128)(2,1)S(1)}, u32[]{:S(2)}, u32[]{:S(2)}) collective-permute-start(bf16[256,256]{1,0:T(8,128)(2,1)} %values_ref.1), channel_id=1, source_target_pairs={{0,16},{16,32},{32,48},{48,0},{64,80},{80,96},{96,112},{112,64},{1... | collective-permute-start | bytes 393224 | tf_op jit(solution)/shard_map/ppermute | solution.py:274
  7.5 7.5 %collective-permute-start.5 = (bf16[256,256]{1,0:T(8,128)(2,1)}, bf16[256,256]{1,0:T(8,128)(2,1)S(1)}, u32[]{:S(2)}, u32[]{:S(2)}) collective-permute-start(bf16[256,256]{1,0:T(8,128)(2,1)} %values_ref.1), channel_id=1, source_target_pairs={{0,48},{16,0},{32,16},{48,32},{64,112},{80,64},{96,80},{112,96},{1... | collective-permute-start | bytes 393224 | tf_op jit(solution)/shard_map/ppermute | solution.py:274
  9.0 7.2 %collective-permute-start.4 = (bf16[256,256]{1,0:T(8,128)(2,1)}, bf16[256,256]{1,0:T(8,128)(2,1)S(1)}, u32[]{:S(2)}, u32[]{:S(2)}) collective-permute-start(bf16[256,256]{1,0:T(8,128)(2,1)} %values_ref.1), channel_id=1, source_target_pairs={{0,32},{16,48},{32,0},{48,16},{64,96},{80,112},{96,64},{112,80},{1... | collective-permute-start | bytes 393224 | tf_op jit(solution)/shard_map/ppermute | solution.py:274
  17.4 27.3 %copy-start = (bf16[2,1024,512]{2,1,0:T(8,128)(2,1)S(1)}, bf16[2,1024,512]{2,1,0:T(8,128)(2,1)}, u32[]{:S(2)}) copy-start(bf16[2,1024,512]{2,1,0:T(8,128)(2,1)} %keys_ref.1) | copy-start | bytes 6291460
  17.4 27.3 %copy-start.1 = (bf16[128,1024]{1,0:T(8,128)(2,1)S(1)}, bf16[128,1024]{1,0:T(8,128)(2,1)}, u32[]{:S(2)}) copy-start(bf16[128,1024]{1,0:T(8,128)(2,1)} %queries_ref.1) | copy-start | bytes 786436
  17.4 27.3 %copy-start.2 = (bf16[128,256]{1,0:T(8,128)(2,1)S(1)}, bf16[128,256]{1,0:T(8,128)(2,1)}, u32[]{:S(2)}) copy-start(bf16[128,256]{1,0:T(8,128)(2,1)} %layer_ref.1) | copy-start | bytes 196612
  17.4 27.3 %copy-start.3 = (f32[128,32]{0,1:T(8,128)S(1)}, f32[128,32]{0,1:T(8,128)}, u32[]{:S(2)}) copy-start(f32[128,32]{0,1:T(8,128)} %param.11) | copy-start | bytes 49156
  17.4 27.2 %copy-start.4 = (s32[2,128,32]{1,2,0:T(8,128)S(1)}, s32[2,128,32]{1,2,0:T(8,128)}, u32[]{:S(2)}) copy-start(s32[2,128,32]{1,2,0:T(8,128)} %param.12) | copy-start | bytes 98308
  17.4 5.1 %collective-permute-start.6 = (f32[32,128]{1,0:T(8,128)S(1)}, f32[32,128]{1,0:T(8,128)S(1)}, u32[]{:S(2)}, u32[]{:S(2)}) collective-permute-start(f32[32,128]{1,0:T(8,128)S(1)} %get-tuple-element.43), channel_id=1, source_target_pairs={{0,64},{16,80},{32,96},{48,112},{64,128},{80,144},{96,160},{112,17... | collective-permute-start | bytes 49160 | tf_op jit(solution)/shard_map/ppermute | solution.py:279
  19.1 4.1 %collective-permute-start.7 = (f32[32,128]{1,0:T(8,128)S(1)}, f32[32,128]{1,0:T(8,128)S(1)}, u32[]{:S(2)}, u32[]{:S(2)}) collective-permute-start(f32[32,128]{1,0:T(8,128)S(1)} %get-tuple-element.44), channel_id=1, source_target_pairs={{0,128},{16,144},{32,160},{48,176},{64,192},{80,208},{96,224},{112... | collective-permute-start | bytes 49160 | tf_op jit(solution)/shard_map/ppermute | solution.py:279
  20.7 2.9 %collective-permute-start.8 = (f32[32,128]{1,0:T(8,128)S(1)}, f32[32,128]{1,0:T(8,128)S(1)}, u32[]{:S(2)}, u32[]{:S(2)}) collective-permute-start(f32[32,128]{1,0:T(8,128)S(1)} %get-tuple-element.45), channel_id=1, source_target_pairs={{0,192},{16,208},{32,224},{48,240},{64,0},{80,16},{96,32},{112,48}... | collective-permute-start | bytes 49160 | tf_op jit(solution)/shard_map/ppermute | solution.py:279
  23.6 8.1 %collective-permute-start.11 = (f32[32,128]{1,0:T(8,128)S(1)}, f32[32,128]{1,0:T(8,128)S(1)}, u32[]{:S(2)}, u32[]{:S(2)}) collective-permute-start(f32[32,128]{1,0:T(8,128)S(1)} %add_add_fusion.1), channel_id=1, source_target_pairs={{0,3},{1,2},{2,1},{3,0},{4,7},{5,6},{6,5},{7,4},{8,11},{9,10},{10,... | collective-permute-start | bytes 49160 | tf_op jit(solution)/shard_map/ppermute | solution.py:259
  28.4 3.3 %collective-permute-start.10 = (f32[32,128]{1,0:T(8,128)S(1)}, f32[32,128]{1,0:T(8,128)S(1)}, u32[]{:S(2)}, u32[]{:S(2)}) collective-permute-start(f32[32,128]{1,0:T(8,128)S(1)} %add_add_fusion.1), channel_id=1, source_target_pairs={{0,2},{1,3},{2,0},{3,1},{4,6},{5,7},{6,4},{7,5},{8,10},{9,11},{10,... | collective-permute-start | bytes 49160 | tf_op jit(solution)/shard_map/ppermute | solution.py:259
  28.4 3.3 %collective-permute-start.9 = (f32[32,128]{1,0:T(8,128)S(1)}, f32[32,128]{1,0:T(8,128)S(1)}, u32[]{:S(2)}, u32[]{:S(2)}) collective-permute-start(f32[32,128]{1,0:T(8,128)S(1)} %add_add_fusion.1), channel_id=1, source_target_pairs={{0,1},{1,0},{2,3},{3,2},{4,5},{5,4},{6,7},{7,6},{8,9},{9,8},{10,11... | collective-permute-start | bytes 49160 | tf_op jit(solution)/shard_map/ppermute | solution.py:259
  28.9 18.7 %collective-permute-start.14 = (bf16[256,256]{1,0:T(8,128)(2,1)S(1)}, bf16[256,256]{1,0:T(8,128)(2,1)S(1)}, u32[]{:S(2)}, u32[]{:S(2)}) collective-permute-start(bf16[256,256]{1,0:T(8,128)(2,1)S(1)} %get-tuple-element.56), channel_id=1, source_target_pairs={{0,32},{16,48},{32,0},{48,16},{64,96},{80,112},{96,64},{112,80},{1... | collective-permute-start | bytes 393224 | tf_op jit(solution)/shard_map/ppermute | solution.py:274
  31.4 16.1 %collective-permute-start.15 = (bf16[256,256]{1,0:T(8,128)(2,1)S(1)}, bf16[256,256]{1,0:T(8,128)(2,1)S(1)}, u32[]{:S(2)}, u32[]{:S(2)}) collective-permute-start(bf16[256,256]{1,0:T(8,128)(2,1)S(1)} %get-tuple-element.57), channel_id=1, source_target_pairs={{0,16},{16,32},{32,48},{48,0},{64,80},{80,96},{96,112},{112,64},{1... | collective-permute-start | bytes 393224 | tf_op jit(solution)/shard_map/ppermute | solution.py:274
  31.7 15.8 %collective-permute-start.16 = (bf16[256,256]{1,0:T(8,128)(2,1)S(1)}, bf16[256,256]{1,0:T(8,128)(2,1)S(1)}, u32[]{:S(2)}, u32[]{:S(2)}) collective-permute-start(bf16[256,256]{1,0:T(8,128)(2,1)S(1)} %get-tuple-element.58), channel_id=1, source_target_pairs={{0,48},{16,0},{32,16},{48,32},{64,112},{80,64},{96,80},{112,96},{1... | collective-permute-start | bytes 393224 | tf_op jit(solution)/shard_map/ppermute | solution.py:274
  34.3 4.3 %collective-permute-start.12 = (f32[32,128]{1,0:T(8,128)S(1)}, f32[32,128]{1,0:T(8,128)S(1)}, u32[]{:S(2)}, u32[]{:S(2)}) collective-permute-start(f32[32,128]{1,0:T(8,128)S(1)} %add_add_fusion), channel_id=1, source_target_pairs={{0,4},{1,5},{2,6},{3,7},{4,0},{5,1},{6,2},{7,3},{8,12},{9,13},{10,... | collective-permute-start | bytes 49160 | tf_op jit(solution)/shard_map/ppermute | solution.py:259
  38.7 5.9 %collective-permute-start.13 = (f32[32,128]{1,0:T(8,128)S(1)}, f32[32,128]{1,0:T(8,128)S(1)}, u32[]{:S(2)}, u32[]{:S(2)}) collective-permute-start(f32[32,128]{1,0:T(8,128)S(1)} %add.30), channel_id=1, source_target_pairs={{0,12},{1,13},{2,14},{3,15},{4,8},{5,9},{6,10},{7,11},{8,4},{9,5},... | collective-permute-start | bytes 49160 | tf_op jit(solution)/shard_map/ppermute | solution.py:259
  64.2 7.2 %collective-permute-start.19 = (bf16[64,256]{1,0:T(8,128)(2,1)S(1)}, bf16[64,256]{1,0:T(8,128)(2,1)S(1)}, u32[]{:S(2)}, u32[]{:S(2)}) collective-permute-start(bf16[64,256]{1,0:T(8,128)(2,1)S(1)} %shard_map.108.own_ref), channel_id=1, source_target_pairs={{0,3},{1,2},{2,1},{3,0},{4,7},{5,6},{6,5},{7,4},{8,11},{9,10},{10,... | collective-permute-start | bytes 98312 | tf_op jit(solution)/shard_map/ppermute | solution.py:259
  69.1 3.3 %collective-permute-start.18 = (bf16[64,256]{1,0:T(8,128)(2,1)S(1)}, bf16[64,256]{1,0:T(8,128)(2,1)S(1)}, u32[]{:S(2)}, u32[]{:S(2)}) collective-permute-start(bf16[64,256]{1,0:T(8,128)(2,1)S(1)} %shard_map.108.own_ref), channel_id=1, source_target_pairs={{0,2},{1,3},{2,0},{3,1},{4,6},{5,7},{6,4},{7,5},{8,10},{9,11},{10,... | collective-permute-start | bytes 98312 | tf_op jit(solution)/shard_map/ppermute | solution.py:259
  69.9 2.6 %collective-permute-start.17 = (bf16[64,256]{1,0:T(8,128)(2,1)S(1)}, bf16[64,256]{1,0:T(8,128)(2,1)S(1)}, u32[]{:S(2)}, u32[]{:S(2)}) collective-permute-start(bf16[64,256]{1,0:T(8,128)(2,1)S(1)} %shard_map.108.own_ref), channel_id=1, source_target_pairs={{0,1},{1,0},{2,3},{3,2},{4,5},{5,4},{6,7},{7,6},{8,9},{9,8},{10,11... | collective-permute-start | bytes 98312 | tf_op jit(solution)/shard_map/ppermute | solution.py:259
